TPU v7x, 256 devices: a whole 4x4x8 slice. The times are simulated.
256 devices in a mesh: tm: 16 (over y, x_hi, core), fsdp: 16 (over x_lo, z).
Axes of the slice: x: 4 (x_hi: 2, x_lo: 2; x = x_hi * 2 + x_lo), y: 4, z: 8, core: 2. Of those that a mesh axis runs over, the one named last changes fastest.
Arguments:
- stacked_mels: bfloat16 [16, 12288, 512], P('fsdp', 'tm'), may hold values from -6 to 6
- utt_lengths: int32 [16, 64], P('fsdp'), may hold values from 1 to 1536, 12288 in all within a row
- sub_weight: bfloat16 [512, 1536], P('fsdp'), may hold values from -0.25 to 0.25
- norm_gain: float32 [1536], replicated, may hold values from 0.1 to 1.9
- first_weight: bfloat16 [1536, 3072], P('fsdp'), may hold values from -0.15625 to 0.15625
- dw_kernel: bfloat16 [32, 1536], replicated, may hold values from -1 to 1
- bn_scale: float32 [1536], replicated, may hold values from 0.5 to 2
- second_weight: bfloat16 [1536, 1536], P('fsdp'), may hold values from -0.15625 to 0.15625
Outputs:
- encoded: bfloat16 [16, 12288, 1536], P('fsdp', 'tm')
Inputs may be any that keep to these rules, and one draw needn't show every extreme that they name: `utt_lengths`: each row sums to 12288; the longest utterance of every row has exactly 1536 frames.
All inputs are finite; a program needn't handle non-finite values.
Results may differ from a plain program's by a relative error of at most 0.008.
Values may be sent and summed in bfloat16 or wider, within the bound.
No kernel may reach another device: no remote copies, remote signals or barrier semaphores. Data moves between devices by JAX's collectives and lax.ppermute only.
A program may use at most 128 MiB of HBM per device.

v0:
```python
import jax
import jax.numpy as jnp
from jax import lax
from jax.sharding import PartitionSpec as P

KW = 32


def with_halo(array, sides, width):
    for axis, dim in sides:
        count, length = (lax.axis_size(axis), array.shape[dim])
        up = [(i, (i + 1) % count) for i in range(count - 1)]
        down = [(j, i) for i, j in up]
        last = lax.slice_in_dim(array, length - width, length, axis=dim)
        initial = lax.slice_in_dim(array, 0, width, axis=dim)
        before = lax.ppermute(last, axis, up)
        after = lax.ppermute(initial, axis, down)
        array = jnp.concatenate([before, array, after], axis=dim)
    return array


def fold_rows(left, piece):
    return jnp.dot(left, piece, preferred_element_type=jnp.float32)


def on_device(
    stacked_mels,
    utt_lengths,
    sub_weight,
    norm_gain,
    first_weight,
    dw_kernel,
    bn_scale,
    second_weight,
):
    seqs, frames, stack_width = stacked_mels.shape
    width = second_weight.shape[1]
    half = KW // 2
    tm_index = lax.axis_index("tm")
    span = stacked_mels.shape[1]
    rows = stacked_mels.reshape(seqs * span, stack_width)
    sub = fold_rows(rows, lax.all_gather(sub_weight, "fsdp", axis=0, tiled=True)).astype(
        jnp.bfloat16
    )
    subf = sub.astype(jnp.float32)
    mean = jnp.mean(subf, axis=1, keepdims=True)
    var = jnp.mean((subf - mean) ** 2, axis=1, keepdims=True)
    normed = ((subf - mean) * lax.rsqrt(var + 1e-05) * norm_gain).astype(jnp.bfloat16)
    proj = fold_rows(normed, lax.all_gather(first_weight, "fsdp", axis=0, tiled=True))
    glu = (proj[:, :width] * jax.nn.sigmoid(proj[:, width:])).astype(jnp.bfloat16)
    sub, glu = (sub.reshape(seqs, span, width), glu.reshape(seqs, span, width))
    glu_wide = with_halo(glu, (("tm", 1),), half)
    positions = tm_index * frames - half + jnp.arange(frames + 2 * half, dtype=jnp.int32)
    ends = jnp.cumsum(utt_lengths, axis=1)
    wide_ids = jnp.sum((positions[None, :, None] >= ends[:, None, :]).astype(jnp.int32), axis=2)
    own_ids = wide_ids[:, half : half + frames]
    depth = jnp.zeros((seqs, frames, width), jnp.float32)
    for k in range(KW):
        same = wide_ids[:, k : k + frames] == own_ids
        depth = depth + jnp.where(
            same[..., None], glu_wide[:, k : k + frames] * dw_kernel[k].astype(jnp.float32), 0.0
        )
    scaled = depth * bn_scale
    act = (scaled * jax.nn.sigmoid(scaled)).astype(jnp.bfloat16)
    second_act = act.reshape(seqs * frames, width)
    branch = fold_rows(
        second_act, lax.all_gather(second_weight, "fsdp", axis=0, tiled=True)
    ).reshape(seqs, frames, width)
    return (sub.astype(jnp.float32) + branch).astype(jnp.bfloat16)


def solution(mesh):
    in_specs = (
        P("fsdp", "tm", None),
        P("fsdp", None),
        P("fsdp", None),
        P(),
        P("fsdp", None),
        P(),
        P(),
        P("fsdp", None),
    )
    out_specs = P("fsdp", "tm", None)
    return jax.shard_map(
        on_device, mesh=mesh, in_specs=in_specs, out_specs=out_specs, check_vma=False
    )
```

profile of v0, /device:TPU:8, one launch (start us, length us, event | category | flops | bytes accessed | tf_op | source)
XLA Modules:
  0.0 337.1 jit_solution(11383324172235353229)
XLA Ops:
  6.5 0.0 copy-start
  6.5 0.0 all-gather.4.cloned.1.call-start
  6.5 0.7 all-gather.4.cloned.1.call-update
  7.3 0.0 all-gather.6.cloned.1.call-start
  7.3 0.7 all-gather.6.cloned.1.call-update
  8.0 0.0 all-gather.8.cloned.1.call-start
  8.1 0.7 all-gather.8.cloned.1.call-update
  8.7 0.9 reduce_window_sum.11
  9.6 0.1 convert_reduce_fusion.1
  9.8 0.8 compare_reduce_fusion.30
  10.5 0.8 compare_reduce_fusion.28
  11.3 1.4 convert_reduce_fusion.32
  12.7 1.6 convert_reduce_fusion.33
  14.3 0.0 copy-start.3
  14.3 68.1 %all-gather.4.cloned.1.call-done = bf16[512,1536]{1,0:T(8,128)(2,1)} async-done(((bf16[32,1536]{1,0:T(8,128)(2,1)}), bf16[512,1536]{1,0:T(8,128)(2,1)}) %all-gather.4.cloned.1.call-update) | async-done | bytes 1572880 | tf_op jit(solution)/shard_map/all_gather | solution.py:42
  82.4 0.0 copy-done
  82.4 2.9 convert_reduce_fusion
  85.3 0.0 copy-start.2
  85.3 0.8 fusion.2
  86.0 106.9 %all-gather.6.cloned.1.call-done = bf16[1536,3072]{1,0:T(8,128)(2,1)} async-done(((bf16[96,3072]{1,0:T(8,128)(2,1)}), bf16[1536,3072]{1,0:T(8,128)(2,1)}) %all-gather.6.cloned.1.call-update) | async-done | bytes 9437200 | tf_op jit(solution)/shard_map/all_gather | solution.py:49
  193.0 0.0 copy-done.2
  193.0 0.0 copy-done.3
  193.0 10.2 %fusion.28 = f32[768,3072]{1,0:T(8,128)S(1)} fusion(bf16[1536,3072]{1,0:T(8,128)(2,1)} %all-gather.6.cloned.1.call-done, bf16[768,1536]{1,0:T(8,128)(2,1)S(1)} %get-tuple-element.75, f32[1536]{0:T(1024)S(1)} %copy-done.3, f32[768]{0:T(1024)S(1)} %add_rsqrt_fusion, f32[768]{0:T(1024)S(1)} %broadcast_multiply_fusion), kind=kOutput, calls=%fused_computation.64 | convolution fusion | flops 7253655552 | bytes 21245952 | tf_op jit(solution)/shard_map/dot_general | solution.py:23
  203.2 1.3 fusion.71
  204.5 2.3 copy-done.1
  206.8 1.9 collective-permute-start
  208.7 6.0 %collective-permute-start.1 = (bf16[1,16,1536]{2,1,0:T(8,128)(2,1)S(1)}, bf16[1,16,1536]{2,1,0:T(8,128)(2,1)}, u32[]{:S(2)}, u32[]{:S(2)}) collective-permute-start(bf16[1,16,1536]{2,1,0:T(8,128)(2,1)S(1)} %get-tuple-element.69), channel_id=1, source_target_pairs={{16,0},{32,16},{48,32},{64,48},{80,64},{96,80},{112,96},{128,112},... | collective-permute-start | bytes 147464 | tf_op jit(solution)/shard_map/ppermute | solution.py:17
  214.8 0.8 compare_reduce_fusion.29
  215.6 55.0 %all-gather.8.cloned.1.call-done = bf16[1536,1536]{1,0:T(8,128)(2,1)} async-done(((bf16[96,1536]{1,0:T(8,128)(2,1)}), bf16[1536,1536]{1,0:T(8,128)(2,1)}) %all-gather.8.cloned.1.call-update) | async-done | bytes 4718608 | tf_op jit(solution)/shard_map/all_gather | solution.py:67
  270.6 0.0 collective-permute-done
  270.6 0.0 collective-permute-done.1
  270.6 60.0 %fusion.27 = bf16[1,768,1536]{2,1,0:T(8,128)(2,1)} fusion(bf16[1536,1536]{1,0:T(8,128)(2,1)} %all-gather.8.cloned.1.call-done, bf16[768,1536]{1,0:T(8,128)(2,1)} %copy-done.2, bf16[1,16,1536]{2,1,0:T(8,128)(2,1)} %collective-permute-done.1, bf16[1,16,1536]{2,1,0:T(8,128)(2,1)} %collective-permute-done, bf16[1,768,1536]{2,1,0:T(8,128)(2,1)S(1)} %fusion.71, ...), kind=kOutput, calls=%fused_computation.63 | convolution fusion | flops 3898736640 | bytes 21558528 | tf_op jit(solution)/shard_map/dot_general | solution.py:23
  (6 shorter events, 0.0 us)
Async XLA Ops:
  6.5 75.9 %copy-start = (bf16[1,768,512]{2,1,0:T(8,128)(2,1)S(1)}, bf16[1,768,512]{2,1,0:T(8,128)(2,1)}, u32[]{:S(2)}) copy-start(bf16[1,768,512]{2,1,0:T(8,128)(2,1)} %param.8) | copy-start | bytes 2359300
  6.5 75.9 %all-gather.4.cloned.1.call-start = ((), (), s32[]{:S(2)}) async-start(), calls=%async_computation | async-start | bytes 1671168 | tf_op jit(solution)/shard_map/all_gather | solution.py:42
  7.3 185.7 %all-gather.6.cloned.1.call-start = ((), (), s32[]{:S(2)}) async-start(), calls=%async_computation.1 | async-start | bytes 10027008 | tf_op jit(solution)/shard_map/all_gather | solution.py:49
  8.0 262.6 %all-gather.8.cloned.1.call-start = ((), (), s32[]{:S(2)}) async-start(), calls=%async_computation.2 | async-start | bytes 5013504 | tf_op jit(solution)/shard_map/all_gather | solution.py:67
  14.3 178.7 %copy-start.3 = (f32[1536]{0:T(1024)S(1)}, f32[1536]{0:T(1024)}, u32[]{:S(2)}) copy-start(f32[1536]{0:T(1024)} %param.11) | copy-start | bytes 18436
  85.3 107.7 %copy-start.2 = (bf16[768,1536]{1,0:T(8,128)(2,1)}, bf16[768,1536]{1,0:T(8,128)(2,1)S(1)}, u32[]{:S(2)}) copy-start(bf16[768,1536]{1,0:T(8,128)(2,1)S(1)} %get-tuple-element.75) | copy-start | bytes 7077892
  203.2 3.6 %copy-start.1 = (f32[768,3072]{1,0:T(8,128)}, f32[768,3072]{1,0:T(8,128)S(1)}, u32[]{:S(2)}) copy-start(f32[768,3072]{1,0:T(8,128)S(1)} %fusion.28) | copy-start | bytes 28311556
  206.8 63.7 %collective-permute-start = (bf16[1,16,1536]{2,1,0:T(8,128)(2,1)S(1)}, bf16[1,16,1536]{2,1,0:T(8,128)(2,1)}, u32[]{:S(2)}, u32[]{:S(2)}) collective-permute-start(bf16[1,16,1536]{2,1,0:T(8,128)(2,1)S(1)} %get-tuple-element.68), channel_id=1, source_target_pairs={{0,16},{16,32},{32,48},{48,64},{64,80},{80,96},{96,112},{112,128},... | collective-permute-start | bytes 147464 | tf_op jit(solution)/shard_map/ppermute | solution.py:16
  208.7 61.8 %collective-permute-start.1 = (bf16[1,16,1536]{2,1,0:T(8,128)(2,1)S(1)}, bf16[1,16,1536]{2,1,0:T(8,128)(2,1)}, u32[]{:S(2)}, u32[]{:S(2)}) collective-permute-start(bf16[1,16,1536]{2,1,0:T(8,128)(2,1)S(1)} %get-tuple-element.69), channel_id=1, source_target_pairs={{16,0},{32,16},{48,32},{64,48},{80,64},{96,80},{112,96},{128,112},... | collective-permute-start | bytes 147464 | tf_op jit(solution)/shard_map/ppermute | solution.py:17
Sparse Core Ops, SparseCore 0:
  9.1 73.1 all-gather.3
  84.2 108.7 all-gather.5
  194.8 75.7 all-gather.7
where the time goes:
time: 337 us
  waiting for transfers between devices  232 us (69%)
  matrix products  73 us (22%)
  between operations  13.2 us (4%)
  other arithmetic  8.29 us (2%)
  starting transfers between devices  8.04 us (2%)
    all_gather x1, waiting for transfers between devices, on_device(): lax.all_gather(first_weight, 'fsdp', axis=0, tiled=True)  107 us
    dot_general x3, matrix products, fold_rows(): return jnp.dot(left, piece, preferred_element_type=jnp.float32)  73 us
    all_gather x1, waiting for transfers between devices, on_device(): lax.all_gather(sub_weight, 'fsdp', axis=0, tiled=True)  68.1 us
    all_gather x1, waiting for transfers between devices, on_device(): lax.all_gather(second_weight, 'fsdp', axis=0, tiled=True)  55 us
  transfers between devices with their start and end apart: 5, of which 3 were waited for; matrix products, arithmetic and copies ran while one was open for 6% of the time, Pallas kernels for 0%

commit v1 on v0

v1 whole, which is shorter than its diff:
```python
import functools

import jax
import jax.numpy as jnp
from jax import lax
from jax.experimental import pallas as pl
from jax.experimental.pallas import tpu as pltpu
from jax.sharding import Mesh
from jax.sharding import PartitionSpec as P

KW = 32
HALF = KW // 2
TM = ("y", "xh", "c")
FS = ("xl", "z")
X = ("xh", "xl")
TILE = 32
ANY = pl.BlockSpec(memory_space=pl.ANY)
VM = pl.BlockSpec(memory_space=pltpu.VMEM)
SM = pl.BlockSpec(memory_space=pltpu.SMEM)


def cyc(n, s):
    return [(i, (i + s) % n) for i in range(n)]


def front_kernel(places, meta, ids_s, *refs):
    n = len(places)
    own, halo, recv = refs[:3]
    blocks = refs[3 : 3 + n]
    gain, taps, scale, ids_v, sub_out, act_own, act_send = refs[3 + n : 10 + n]
    mels, ws, wf, sub, normed, xs, idb, tmp, act, sem_in, sem_out = refs[10 + n :]
    c, z, xl = meta[0], meta[1], meta[2]
    span = own.shape[0]
    rows = mels.shape[0]
    width = sub.shape[1]
    hw = act.shape[1]
    sr = ws.shape[0] // 16
    fr = wf.shape[0] // 16

    mine = pl.multiple_of(HALF + span * c, HALF)
    other = pl.multiple_of(HALF + span * (1 - c), HALF)
    outer = pl.multiple_of((rows - HALF) * c, HALF)
    inner = pl.multiple_of((rows - HALF) * (1 - c), HALF)
    copies = [
        pltpu.make_async_copy(own, mels.at[pl.ds(mine, span)], sem_in.at[0]),
        pltpu.make_async_copy(recv.at[pl.ds(0, span)], mels.at[pl.ds(other, span)], sem_in.at[1]),
        pltpu.make_async_copy(halo, mels.at[pl.ds(outer, HALF)], sem_in.at[2]),
        pltpu.make_async_copy(recv.at[pl.ds(span, HALF)], mels.at[pl.ds(inner, HALF)], sem_in.at[3]),
    ]
    late = []
    at = 4
    for (flip, shift, lo, hi), block in zip(places, blocks):
        xx = (1 - xl) if flip else xl
        j = xx * 8 + lax.rem(z + shift + 8, 8)
        if lo < sr:
            copies.append(
                pltpu.make_async_copy(
                    block.at[pl.ds(0, sr)],
                    ws.at[pl.ds(pl.multiple_of(j * sr, sr), sr)],
                    sem_in.at[at],
                )
            )
            at += 1
        a, b = max(lo, sr), hi
        late.append(
            pltpu.make_async_copy(
                block.at[pl.ds(a - lo, b - a)],
                wf.at[pl.ds(pl.multiple_of(j * fr + (a - sr), 32), b - a)],
                sem_in.at[at],
            )
        )
        at += 1
    for cp in copies + late:
        cp.start()
    idb[...] = jnp.broadcast_to(ids_v[...], idb.shape)
    for cp in copies:
        cp.wait()

    nb = 112

    def front(i, _):
        r = pl.ds(pl.multiple_of(i * nb, 16), nb)
        s = jnp.dot(mels[r, :], ws[...], preferred_element_type=jnp.float32).astype(jnp.bfloat16)
        sub[r, :] = s
        f = s.astype(jnp.float32)
        mean = jnp.sum(f, axis=1, keepdims=True) * (1.0 / width)
        d = f - mean
        var = jnp.sum(d * d, axis=1, keepdims=True) * (1.0 / width)
        normed[r, :] = (d * lax.rsqrt(var + 1e-05) * gain[...]).astype(jnp.bfloat16)
        return 0

    lax.fori_loop(0, rows // nb, front, 0)
    out_sub = pltpu.make_async_copy(sub.at[pl.ds(mine, span)], sub_out, sem_out.at[0])
    out_sub.start()
    for cp in late:
        cp.wait()

    mb = 224
    for cg in range(hw // 256):
        vcol, gcol = cg * 256, hw + cg * 256

        def gated(i, _):
            r = pl.ds(pl.multiple_of(i * mb, 16), mb)
            lhs = normed[r, :]
            v = jnp.dot(lhs, wf[:, vcol : vcol + 256], preferred_element_type=jnp.float32)
            g = jnp.dot(lhs, wf[:, gcol : gcol + 256], preferred_element_type=jnp.float32)
            glu = (v * jax.nn.sigmoid(g)).astype(jnp.bfloat16).astype(jnp.float32)
            xs[2 * cg, r, :] = glu[:, :128]
            xs[2 * cg + 1, r, :] = glu[:, 128:]
            return 0

        lax.fori_loop(0, rows // mb, gated, 0)

        for g in (2 * cg, 2 * cg + 1):

            def tile(i, _):
                t0 = pl.multiple_of(i * TILE, TILE)
                win = TILE + KW
                idw = idb[pl.ds(t0, win), :]
                ido = idb[pl.ds(pl.multiple_of(t0 + HALF, HALF), TILE), :]
                first = ids_s[t0 + HALF]
                last = ids_s[t0 + HALF + TILE - 1]

                def one(u, acc):
                    tmp[...] = jnp.where(idw == u, xs[g, pl.ds(t0, win), :], 0.0)
                    s = tmp[0:TILE, :] * taps[g, 0:1, :]
                    for k in range(1, KW):
                        s = s + tmp[k : k + TILE, :] * taps[g, k : k + 1, :]
                    return jnp.where(ido == u, s, acc)

                acc = lax.fori_loop(first, last + 1, one, jnp.zeros((TILE, 128), jnp.float32))
                u = acc * scale[:, g * 128 : (g + 1) * 128]
                act[pl.ds(t0, TILE), g * 128 : (g + 1) * 128] = (u * jax.nn.sigmoid(u)).astype(
                    jnp.bfloat16
                )
                return 0

            lax.fori_loop(0, 2 * span // TILE, tile, 0)

    outs = [
        pltpu.make_async_copy(
            act.at[pl.ds(pl.multiple_of(span * c, span), span)], act_own, sem_out.at[1]
        ),
        pltpu.make_async_copy(
            act.at[pl.ds(pl.multiple_of(span * (1 - c), span), span)], act_send, sem_out.at[2]
        ),
    ]
    for cp in outs:
        cp.start()
    out_sub.wait()
    for cp in outs:
        cp.wait()


def back_kernel(meta, sub, mine, theirs, w_mine, w_theirs, out, sub_v, a_v, w_v, o_v, sem_in, sem_out):
    c = meta[0]
    span, width = sub.shape
    hw = mine.shape[1]
    here = pl.multiple_of(hw * c, 128)
    there = pl.multiple_of(hw * (1 - c), 128)
    copies = [
        pltpu.make_async_copy(sub, sub_v, sem_in.at[0]),
        pltpu.make_async_copy(mine, a_v.at[:, pl.ds(here, hw)], sem_in.at[1]),
        pltpu.make_async_copy(theirs, a_v.at[:, pl.ds(there, hw)], sem_in.at[2]),
        pltpu.make_async_copy(w_mine, w_v.at[:, pl.ds(here, hw)], sem_in.at[3]),
        pltpu.make_async_copy(w_theirs, w_v.at[:, pl.ds(there, hw)], sem_in.at[4]),
    ]
    for cp in copies:
        cp.start()
    for cp in copies:
        cp.wait()
    nb = 192
    outs = []
    for i in range(span // nb):
        r = pl.ds(i * nb, nb)
        for n in range(0, width, 512):
            y = jnp.dot(a_v[r, :], w_v[:, n : n + 512], preferred_element_type=jnp.float32)
            o_v[r, n : n + 512] = (sub_v[r, n : n + 512].astype(jnp.float32) + y).astype(
                jnp.bfloat16
            )
        outs.append(pltpu.make_async_copy(o_v.at[r], out.at[r], sem_out.at[i]))
        outs[-1].start()
    for cp in outs:
        cp.wait()


def on_device(mels, utt_lengths, sub_weight, norm_gain, first_weight, dw_kernel, bn_scale, second_weight):
    _, span, stack = mels.shape
    width = second_weight.shape[1]
    hw = width // 2
    sr, fr = sub_weight.shape[0], first_weight.shape[0]
    c = lax.axis_index("c")
    z = lax.axis_index("z")
    xl = lax.axis_index("xl")
    chip = lax.axis_index("y") * 2 + lax.axis_index("xh")
    zp = lambda a: lax.ppermute(a, "z", cyc(8, 1))
    zm = lambda a: lax.ppermute(a, "z", cyc(8, -1))
    xp = lambda a: lax.ppermute(a, X, cyc(4, 1))
    xm = lambda a: lax.ppermute(a, X, cyc(4, -1))
    swap = lambda a: lax.ppermute(a, "c", cyc(2, 1))

    half = lambda a, at: lax.dynamic_slice_in_dim(a, at + c * hw, hw, axis=a.ndim - 1)
    block = jnp.concatenate(
        [sub_weight, jnp.concatenate([half(first_weight, 0), half(first_weight, width)], axis=1)]
    )
    hi = sr + fr
    mid = hi // 2
    places = [(False, 0, 0, hi), (True, 0, 0, hi)]
    blocks = [block, xp(block)]
    p = m = block
    for s in (1, 2, 3):
        p, m = zp(p), zm(m)
        blocks += [p, m, xp(p), xm(m)]
        places += [(False, -s, 0, hi), (False, s, 0, hi), (True, -s, 0, hi), (True, s, 0, hi)]
    p, m = zp(p[:mid]), zm(m[mid:])
    blocks += [p, m, xp(p), xm(m)]
    places += [(False, 4, 0, mid), (False, 4, mid, hi), (True, 4, 0, mid), (True, 4, mid, hi)]

    w_mine = lax.all_gather(half(second_weight, 0), FS, axis=0, tiled=True)
    w_theirs = swap(w_mine)

    own = mels.reshape(span, stack)
    edge = lax.dynamic_slice_in_dim(own, c * (span - HALF), HALF, axis=0)
    n_tm = 16
    out_pairs = [(2 * j + 1, 2 * j + 2) for j in range(n_tm // 2 - 1)]
    halo = lax.ppermute(edge, TM, out_pairs + [(b, a) for a, b in out_pairs])
    recv = swap(jnp.concatenate([own, halo]))

    rows = 2 * span + 2 * HALF
    ends = jnp.cumsum(utt_lengths.reshape(-1))
    positions = chip * 2 * span - HALF + jnp.arange(rows, dtype=jnp.int32)
    ids = jnp.sum((positions[:, None] >= ends[None, :]).astype(jnp.int32), axis=1)
    meta = jnp.stack([c, z, xl]).astype(jnp.int32)
    taps = half(dw_kernel, 0).astype(jnp.float32).reshape(KW, hw // 128, 128).transpose(1, 0, 2)

    bf, f32 = jnp.bfloat16, jnp.float32
    n_in = 4 + 2 * len(blocks)
    sub, act_own, act_send = pl.pallas_call(
        functools.partial(front_kernel, places),
        out_shape=[
            jax.ShapeDtypeStruct((span, width), bf),
            jax.ShapeDtypeStruct((span, hw), bf),
            jax.ShapeDtypeStruct((span, hw), bf),
        ],
        in_specs=[SM, SM] + [ANY] * (3 + len(blocks)) + [VM] * 4,
        out_specs=[ANY] * 3,
        scratch_shapes=[
            pltpu.VMEM((rows, stack), bf),
            pltpu.VMEM((16 * sr, width), bf),
            pltpu.VMEM((16 * fr, width), bf),
            pltpu.VMEM((rows, width), bf),
            pltpu.VMEM((rows, width), bf),
            pltpu.VMEM((hw // 128, rows, 128), f32),
            pltpu.VMEM((rows, 128), jnp.int32),
            pltpu.VMEM((TILE + KW, 128), f32),
            pltpu.VMEM((2 * span, hw), bf),
            pltpu.SemaphoreType.DMA((n_in,)),
            pltpu.SemaphoreType.DMA((3,)),
        ],
        compiler_params=pltpu.CompilerParams(vmem_limit_bytes=48 << 20),
        cost_estimate=pl.CostEstimate(flops=10_000_000_000, bytes_accessed=12 << 20, transcendentals=0),
        name="front",
    )(meta, ids, own, halo, recv, *blocks, norm_gain.reshape(1, width), taps,
      half(bn_scale.reshape(1, width), 0), ids.reshape(rows, 1))

    act_recv = swap(act_send)
    out = pl.pallas_call(
        back_kernel,
        out_shape=jax.ShapeDtypeStruct((span, width), bf),
        in_specs=[SM] + [ANY] * 5,
        out_specs=ANY,
        scratch_shapes=[
            pltpu.VMEM((span, width), bf),
            pltpu.VMEM((span, width), bf),
            pltpu.VMEM((width, width), bf),
            pltpu.VMEM((span, width), bf),
            pltpu.SemaphoreType.DMA((5,)),
            pltpu.SemaphoreType.DMA((4,)),
        ],
        compiler_params=pltpu.CompilerParams(vmem_limit_bytes=32 << 20),
        cost_estimate=pl.CostEstimate(flops=3_600_000_000, bytes_accessed=12 << 20, transcendentals=0),
        name="back",
    )(meta, sub, act_own, act_recv, w_mine, w_theirs)
    return out.reshape(1, span, width)


def solution(mesh):
    fine = Mesh(mesh.devices.reshape(4, 2, 2, 2, 8), ("y", "xh", "c", "xl", "z"))
    in_specs = (
        P(FS, TM, None),
        P(FS, None),
        P(FS, None),
        P(),
        P(FS, None),
        P(),
        P(),
        P(FS, None),
    )
    return jax.shard_map(
        on_device, mesh=fine, in_specs=in_specs, out_specs=P(FS, TM, None), check_vma=False
    )
```

time: 337 us -> 169 us (0.50)
  the two profiles are of different devices: /device:TPU:8 before, /device:TPU:1 now
where the time goes in v1:
time: 169 us; the launch traced here: 168 us
  Pallas kernels  56.5 us (33%)
  waiting for transfers between devices  45.2 us (27%)
  starting transfers between devices  41.6 us (25%)
  between operations  13.5 us (8%)
  local copies, waits for them, and re-layouts  8.44 us (5%)
  other arithmetic  3.08 us (2%)
    pallas_call x1, Pallas kernels, on_device(): pl.pallas_call(functools.partial(front_kernel, places), out_shape=[jax.Sh...  49 us
    ppermute x5, waiting for transfers between devices, on_device(): xp = lambda a: lax.ppermute(a, X, cyc(4, 1))  18.2 us
    ppermute x4, waiting for transfers between devices, on_device(): xm = lambda a: lax.ppermute(a, X, cyc(4, -1))  12.1 us
    ppermute x4, starting transfers between devices, on_device(): xm = lambda a: lax.ppermute(a, X, cyc(4, -1))  10.8 us
    ppermute x4, starting transfers between devices, on_device(): zm = lambda a: lax.ppermute(a, 'z', cyc(8, -1))  10.6 us
    ppermute x4, waiting for transfers between devices, on_device(): zp = lambda a: lax.ppermute(a, 'z', cyc(8, 1))  10.4 us
    ppermute x1, starting transfers between devices, on_device(): halo = lax.ppermute(edge, TM, out_pairs + [(b, a) for a, b in out_pairs])  7.69 us
    pallas_call x1, Pallas kernels, on_device(): pl.pallas_call(back_kernel, out_shape=jax.ShapeDtypeStruct((span, width),...  7.46 us
  transfers between devices with their start and end apart: 22, of which 9 were waited for; matrix products, arithmetic and copies ran while one was open for 4% of the time, Pallas kernels for 29%

profile of v1, /device:TPU:1, one launch (start us, length us, event | category | flops | bytes accessed | tf_op | source)
XLA Modules:
  0.0 168.3 jit_solution(12926248962746766806)
XLA Ops:
  6.5 1.0 copy-done
  8.2 1.0 constant_dynamic-slice_fusion.2
  9.3 0.9 maximum_maximum_fusion.refs_3_
  10.2 2.5 %collective-permute-start.3 = (bf16[128,1536]{1,0:T(8,128)(2,1)S(1)}, bf16[128,1536]{1,0:T(8,128)(2,1)S(1)}, u32[]{:S(2)}, u32[]{:S(2)}) collective-permute-start(bf16[128,1536]{1,0:T(8,128)(2,1)S(1)} %maximum_maximum_fusion.refs_3_), channel_id=1, source_target_pairs={{0,1},{1,2},{2,3},{3,4},{4,5},{5,6},{6,7},{7,0},{8,9},{9,10},{10,1... | collective-permute-start | bytes 1179656 | tf_op jit(solution)/shard_map/ppermute | solution.py:196
  12.7 4.0 %collective-permute-start.4 = (bf16[128,1536]{1,0:T(8,128)(2,1)S(1)}, bf16[128,1536]{1,0:T(8,128)(2,1)S(1)}, u32[]{:S(2)}, u32[]{:S(2)}) collective-permute-start(bf16[128,1536]{1,0:T(8,128)(2,1)S(1)} %maximum_maximum_fusion.refs_3_), channel_id=1, source_target_pairs={{0,7},{1,0},{2,1},{3,2},{4,3},{5,4},{6,5},{7,6},{8,15},{9,8},{10,9... | collective-permute-start | bytes 1179656 | tf_op jit(solution)/shard_map/ppermute | solution.py:197
  16.8 8.8 %collective-permute-done.3.refs_5_ = bf16[128,1536]{1,0:T(8,128)(2,1)S(1)} collective-permute-done((bf16[128,1536]{1,0:T(8,128)(2,1)S(1)}, bf16[128,1536]{1,0:T(8,128)(2,1)S(1)}, u32[]{:S(2)}, u32[]{:S(2)}) %collective-permute-start.3) | collective-permute-done | bytes 393248 | tf_op jit(solution)/shard_map/ppermute | solution.py:196
  25.5 2.7 %collective-permute-start.8 = (bf16[128,1536]{1,0:T(8,128)(2,1)S(1)}, bf16[128,1536]{1,0:T(8,128)(2,1)S(1)}, u32[]{:S(2)}, u32[]{:S(2)}) collective-permute-start(bf16[128,1536]{1,0:T(8,128)(2,1)S(1)} %collective-permute-done.4.refs_6_), channel_id=1, source_target_pairs={{0,7},{1,0},{2,1},{3,2},{4,3},{5,4},{6,5},{7,6},{8,15},{9,8},{10,9... | collective-permute-start | bytes 1179656 | tf_op jit(solution)/shard_map/ppermute | solution.py:197
  28.2 7.7 %collective-permute-start = (bf16[16,512]{1,0:T(8,128)(2,1)S(1)}, bf16[16,512]{1,0:T(8,128)(2,1)S(1)}, u32[]{:S(2)}, u32[]{:S(2)}) collective-permute-start(bf16[16,512]{1,0:T(8,128)(2,1)S(1)} %dynamic-slice_bitcast_fusion), channel_id=1, source_target_pairs={{16,32},{48,64},{80,96},{112,128},{144,160},{176,192},{208,224},{3... | collective-permute-start | bytes 49160 | tf_op jit(solution)/shard_map/ppermute | solution.py:226
  35.9 1.7 %collective-permute-done.refs_1_ = bf16[16,512]{1,0:T(8,128)(2,1)S(1)} collective-permute-done((bf16[16,512]{1,0:T(8,128)(2,1)S(1)}, bf16[16,512]{1,0:T(8,128)(2,1)S(1)}, u32[]{:S(2)}, u32[]{:S(2)}) %collective-permute-start) | collective-permute-done | bytes 16416 | tf_op jit(solution)/shard_map/ppermute | solution.py:226
  37.6 0.9 pad_maximum_fusion
  38.9 1.6 collective-permute-done.7.refs_9_
  40.5 3.2 %collective-permute-start.12 = (bf16[128,1536]{1,0:T(8,128)(2,1)S(1)}, bf16[128,1536]{1,0:T(8,128)(2,1)S(1)}, u32[]{:S(2)}, u32[]{:S(2)}) collective-permute-start(bf16[128,1536]{1,0:T(8,128)(2,1)S(1)} %collective-permute-done.8.refs_10_), channel_id=1, source_target_pairs={{0,7},{1,0},{2,1},{3,2},{4,3},{5,4},{6,5},{7,6},{8,15},{9,8},{10,9... | collective-permute-start | bytes 1179656 | tf_op jit(solution)/shard_map/ppermute | solution.py:197
  43.7 1.0 collective-permute-start.5
  44.7 7.7 %collective-permute-done.2.refs_4_ = bf16[128,1536]{1,0:T(8,128)(2,1)S(1)} collective-permute-done((bf16[128,1536]{1,0:T(8,128)(2,1)S(1)}, bf16[128,1536]{1,0:T(8,128)(2,1)S(1)}, u32[]{:S(2)}, u32[]{:S(2)}) %collective-permute-start.2) | collective-permute-done | bytes 393248 | tf_op jit(solution)/shard_map/ppermute | solution.py:198
  52.4 5.7 %collective-permute-start.6 = (bf16[128,1536]{1,0:T(8,128)(2,1)S(1)}, bf16[128,1536]{1,0:T(8,128)(2,1)}, u32[]{:S(2)}, u32[]{:S(2)}) collective-permute-start(bf16[128,1536]{1,0:T(8,128)(2,1)S(1)} %collective-permute-done.4.refs_6_), channel_id=1, source_target_pairs={{0,40},{8,0},{32,8},{40,32},{1,41},{9,1},{33,9},{41,33},{2,42},{10... | collective-permute-start | bytes 1179656 | tf_op jit(solution)/shard_map/ppermute | solution.py:199
  58.1 1.4 collective-permute-start.9
  60.9 6.1 %collective-permute-done.5.refs_7_ = bf16[128,1536]{1,0:T(8,128)(2,1)} collective-permute-done((bf16[128,1536]{1,0:T(8,128)(2,1)S(1)}, bf16[128,1536]{1,0:T(8,128)(2,1)}, u32[]{:S(2)}, u32[]{:S(2)}) %collective-permute-start.5) | collective-permute-done | bytes 393248 | tf_op jit(solution)/shard_map/ppermute | solution.py:198
  67.1 1.9 %collective-permute-done.6.refs_8_ = bf16[128,1536]{1,0:T(8,128)(2,1)} collective-permute-done((bf16[128,1536]{1,0:T(8,128)(2,1)S(1)}, bf16[128,1536]{1,0:T(8,128)(2,1)}, u32[]{:S(2)}, u32[]{:S(2)}) %collective-permute-start.6) | collective-permute-done | bytes 393248 | tf_op jit(solution)/shard_map/ppermute | solution.py:199
  69.7 2.8 %collective-permute-start.13 = (bf16[128,1536]{1,0:T(8,128)(2,1)S(1)}, bf16[128,1536]{1,0:T(8,128)(2,1)}, u32[]{:S(2)}, u32[]{:S(2)}) collective-permute-start(bf16[128,1536]{1,0:T(8,128)(2,1)S(1)} %collective-permute-done.11.refs_13_), channel_id=1, source_target_pairs={{0,8},{8,32},{32,40},{40,0},{1,9},{9,33},{33,41},{41,1},{2,10},{10... | collective-permute-start | bytes 1179656 | tf_op jit(solution)/shard_map/ppermute | solution.py:198
  72.6 10.2 %collective-permute-done.10.refs_12_ = bf16[128,1536]{1,0:T(8,128)(2,1)} collective-permute-done((bf16[128,1536]{1,0:T(8,128)(2,1)S(1)}, bf16[128,1536]{1,0:T(8,128)(2,1)}, u32[]{:S(2)}, u32[]{:S(2)}) %collective-permute-start.10) | collective-permute-done | bytes 393248 | tf_op jit(solution)/shard_map/ppermute | solution.py:199
  82.8 2.8 %collective-permute-start.14 = (bf16[128,1536]{1,0:T(8,128)(2,1)S(1)}, bf16[128,1536]{1,0:T(8,128)(2,1)}, u32[]{:S(2)}, u32[]{:S(2)}) collective-permute-start(bf16[128,1536]{1,0:T(8,128)(2,1)S(1)} %collective-permute-done.12.refs_14_), channel_id=1, source_target_pairs={{0,40},{8,0},{32,8},{40,32},{1,41},{9,1},{33,9},{41,33},{2,42},{10... | collective-permute-start | bytes 1179656 | tf_op jit(solution)/shard_map/ppermute | solution.py:199
  85.9 2.9 %collective-permute-start.20 = (bf16[1536,768]{1,0:T(8,128)(2,1)}, bf16[1536,768]{1,0:T(8,128)(2,1)}, u32[]{:S(2)}, u32[]{:S(2)}) collective-permute-start(bf16[1536,768]{1,0:T(8,128)(2,1)} %all-gather.2.cloned.1.call-done.w_mine), channel_id=1, source_target_pairs={{0,16},{16,0},{1,17},{17,1},{2,18},{18,2},{3,19},{19,3},{4,20},{20... | collective-permute-start | bytes 7077896 | tf_op jit(solution)/shard_map/ppermute | solution.py:200
  89.0 1.2 reshape.56.refs_24_
  90.7 2.3 %collective-permute-start.18 = (bf16[64,1536]{1,0:T(8,128)(2,1)}, bf16[64,1536]{1,0:T(8,128)(2,1)S(1)}, u32[]{:S(2)}, u32[]{:S(2)}) collective-permute-start(bf16[64,1536]{1,0:T(8,128)(2,1)} %collective-permute-done.16.refs_18_), channel_id=1, source_target_pairs={{0,40},{8,0},{32,8},{40,32},{1,41},{9,1},{33,9},{41,33},{2,42},{10... | collective-permute-start | bytes 589832 | tf_op jit(solution)/shard_map/ppermute | solution.py:199
  93.1 0.8 bitcast_bitcast_fusion.refs_22_
  93.9 4.4 %collective-permute-done.17.refs_19_ = bf16[64,1536]{1,0:T(8,128)(2,1)S(1)} collective-permute-done((bf16[64,1536]{1,0:T(8,128)(2,1)}, bf16[64,1536]{1,0:T(8,128)(2,1)S(1)}, u32[]{:S(2)}, u32[]{:S(2)}) %collective-permute-start.17) | collective-permute-done | bytes 196640 | tf_op jit(solution)/shard_map/ppermute | solution.py:198
  98.3 49.0 %front.1 = (bf16[768,1536]{1,0:T(8,128)(2,1)}, bf16[768,768]{1,0:T(8,128)(2,1)}, bf16[768,768]{1,0:T(8,128)(2,1)}) custom-call(s32[3]{0:T(128)S(1)} %pad_add_fusion.meta, s32[1568]{0:T(1024)S(1)} %convert_reduce_fusion.ids_s, bf16[768,512]{1,0:T(8,128)(2,1)} %bitcast.15, bf16[16,512]{1,0:T(8,128)(2,1)S(1)} %collective-permute-done.refs_1_, ...), custom_call_target="tpu_custom_call" | custom-call | flops 10000000000 | bytes 12582912 | tf_op jit(solution)/shard_map/front/pallas_call | solution.py:238
  147.3 1.0 collective-permute-start.19
  148.3 2.7 %collective-permute-done.19.theirs = bf16[768,768]{1,0:T(8,128)(2,1)S(1)} collective-permute-done((bf16[768,768]{1,0:T(8,128)(2,1)}, bf16[768,768]{1,0:T(8,128)(2,1)S(1)}, u32[]{:S(2)}, u32[]{:S(2)}) %collective-permute-start.19) | collective-permute-done | bytes 1179680 | tf_op jit(solution)/shard_map/ppermute | solution.py:200
  151.0 1.7 copy-done.2
  152.7 1.3 copy-done.3
  154.0 7.5 %back.1 = bf16[768,1536]{1,0:T(8,128)(2,1)} custom-call(s32[3]{0:T(128)S(1)} %pad_add_fusion.meta, bf16[768,1536]{1,0:T(8,128)(2,1)S(1)} %copy-done.2, bf16[768,768]{1,0:T(8,128)(2,1)S(1)} %copy-done.3, bf16[768,768]{1,0:T(8,128)(2,1)S(1)} %collective-permute-done.19.theirs, bf16[1536,768]{1,0:T(8,128)(2,1)S(1)} %copy-done.1, ...), custom_call_target="tpu_custom_call" | custom-call | flops 3600000000 | bytes 12582912 | tf_op jit(solution)/shard_map/back/pallas_call | solution.py:267
  (49 shorter events, 4.3 us)
Async XLA Ops:
  6.5 1.0 copy-start
  6.5 21.7 %copy-start.4 = (bf16[1,768,512]{2,1,0:T(8,128)(2,1)S(1)}, bf16[1,768,512]{2,1,0:T(8,128)(2,1)}, u32[]{:S(2)}) copy-start(bf16[1,768,512]{2,1,0:T(8,128)(2,1)} %param.8) | copy-start | bytes 2359300
  6.5 79.4 %all-gather.2.cloned.1.call-start = ((), (), s32[]{:S(2)}) async-start(), calls=%async_computation | async-start | bytes 2506752 | tf_op jit(solution)/shard_map/all_gather | solution.py:219
  9.2 76.3 %copy-start.7 = (s32[1,64]{1,0:T(1,128)S(1)}, s32[1,64]{1,0:T(1,128)}, u32[]{:S(2)}) copy-start(s32[1,64]{1,0:T(1,128)} %param.9) | copy-start | bytes 772
  9.2 79.7 %copy-start.6 = (f32[1536]{0:T(1024)S(1)}, f32[1536]{0:T(1024)}, u32[]{:S(2)}) copy-start(f32[1536]{0:T(1024)} %param.14) | copy-start | bytes 18436
  10.2 15.3 %collective-permute-start.3 = (bf16[128,1536]{1,0:T(8,128)(2,1)S(1)}, bf16[128,1536]{1,0:T(8,128)(2,1)S(1)}, u32[]{:S(2)}, u32[]{:S(2)}) collective-permute-start(bf16[128,1536]{1,0:T(8,128)(2,1)S(1)} %maximum_maximum_fusion.refs_3_), channel_id=1, source_target_pairs={{0,1},{1,2},{2,3},{3,4},{4,5},{5,6},{6,7},{7,0},{8,9},{9,10},{10,1... | collective-permute-start | bytes 1179656 | tf_op jit(solution)/shard_map/ppermute | solution.py:196
  12.7 12.8 %collective-permute-start.4 = (bf16[128,1536]{1,0:T(8,128)(2,1)S(1)}, bf16[128,1536]{1,0:T(8,128)(2,1)S(1)}, u32[]{:S(2)}, u32[]{:S(2)}) collective-permute-start(bf16[128,1536]{1,0:T(8,128)(2,1)S(1)} %maximum_maximum_fusion.refs_3_), channel_id=1, source_target_pairs={{0,7},{1,0},{2,1},{3,2},{4,3},{5,4},{6,5},{7,6},{8,15},{9,8},{10,9... | collective-permute-start | bytes 1179656 | tf_op jit(solution)/shard_map/ppermute | solution.py:197
  25.5 15.0 %collective-permute-start.7 = (bf16[128,1536]{1,0:T(8,128)(2,1)S(1)}, bf16[128,1536]{1,0:T(8,128)(2,1)S(1)}, u32[]{:S(2)}, u32[]{:S(2)}) collective-permute-start(bf16[128,1536]{1,0:T(8,128)(2,1)S(1)} %collective-permute-done.3.refs_5_), channel_id=1, source_target_pairs={{0,1},{1,2},{2,3},{3,4},{4,5},{5,6},{6,7},{7,0},{8,9},{9,10},{10,1... | collective-permute-start | bytes 1179656 | tf_op jit(solution)/shard_map/ppermute | solution.py:196
  25.5 15.0 %collective-permute-start.8 = (bf16[128,1536]{1,0:T(8,128)(2,1)S(1)}, bf16[128,1536]{1,0:T(8,128)(2,1)S(1)}, u32[]{:S(2)}, u32[]{:S(2)}) collective-permute-start(bf16[128,1536]{1,0:T(8,128)(2,1)S(1)} %collective-permute-done.4.refs_6_), channel_id=1, source_target_pairs={{0,7},{1,0},{2,1},{3,2},{4,3},{5,4},{6,5},{7,6},{8,15},{9,8},{10,9... | collective-permute-start | bytes 1179656 | tf_op jit(solution)/shard_map/ppermute | solution.py:197
  28.2 9.4 %collective-permute-start = (bf16[16,512]{1,0:T(8,128)(2,1)S(1)}, bf16[16,512]{1,0:T(8,128)(2,1)S(1)}, u32[]{:S(2)}, u32[]{:S(2)}) collective-permute-start(bf16[16,512]{1,0:T(8,128)(2,1)S(1)} %dynamic-slice_bitcast_fusion), channel_id=1, source_target_pairs={{16,32},{48,64},{80,96},{112,128},{144,160},{176,192},{208,224},{3... | collective-permute-start | bytes 49160 | tf_op jit(solution)/shard_map/ppermute | solution.py:226
  37.6 52.6 %copy-start.5 = (f32[1536]{0:T(1024)S(1)}, f32[1536]{0:T(1024)}, u32[]{:S(2)}) copy-start(f32[1536]{0:T(1024)} %param.11) | copy-start | bytes 18436
  38.6 31.2 %collective-permute-start.1 = (bf16[784,512]{1,0:T(8,128)(2,1)}, bf16[784,512]{1,0:T(8,128)(2,1)}, u32[]{:S(2)}, u32[]{:S(2)}) collective-permute-start(bf16[784,512]{1,0:T(8,128)(2,1)} %pad_maximum_fusion), channel_id=1, source_target_pairs={{0,16},{16,0},{1,17},{17,1},{2,18},{18,2},{3,19},{19,3},{4,20},{20... | collective-permute-start | bytes 2408456 | tf_op jit(solution)/shard_map/ppermute | solution.py:200
  38.6 13.9 %collective-permute-start.2 = (bf16[128,1536]{1,0:T(8,128)(2,1)S(1)}, bf16[128,1536]{1,0:T(8,128)(2,1)S(1)}, u32[]{:S(2)}, u32[]{:S(2)}) collective-permute-start(bf16[128,1536]{1,0:T(8,128)(2,1)S(1)} %maximum_maximum_fusion.refs_3_), channel_id=1, source_target_pairs={{0,8},{8,32},{32,40},{40,0},{1,9},{9,33},{33,41},{41,1},{2,10},{10... | collective-permute-start | bytes 1179656 | tf_op jit(solution)/shard_map/ppermute | solution.py:198
  40.5 17.6 %collective-permute-start.11 = (bf16[128,1536]{1,0:T(8,128)(2,1)S(1)}, bf16[128,1536]{1,0:T(8,128)(2,1)S(1)}, u32[]{:S(2)}, u32[]{:S(2)}) collective-permute-start(bf16[128,1536]{1,0:T(8,128)(2,1)S(1)} %collective-permute-done.7.refs_9_), channel_id=1, source_target_pairs={{0,1},{1,2},{2,3},{3,4},{4,5},{5,6},{6,7},{7,0},{8,9},{9,10},{10,1... | collective-permute-start | bytes 1179656 | tf_op jit(solution)/shard_map/ppermute | solution.py:196
  40.5 17.6 %collective-permute-start.12 = (bf16[128,1536]{1,0:T(8,128)(2,1)S(1)}, bf16[128,1536]{1,0:T(8,128)(2,1)S(1)}, u32[]{:S(2)}, u32[]{:S(2)}) collective-permute-start(bf16[128,1536]{1,0:T(8,128)(2,1)S(1)} %collective-permute-done.8.refs_10_), channel_id=1, source_target_pairs={{0,7},{1,0},{2,1},{3,2},{4,3},{5,4},{6,5},{7,6},{8,15},{9,8},{10,9... | collective-permute-start | bytes 1179656 | tf_op jit(solution)/shard_map/ppermute | solution.py:197
  43.7 23.3 %collective-permute-start.5 = (bf16[128,1536]{1,0:T(8,128)(2,1)S(1)}, bf16[128,1536]{1,0:T(8,128)(2,1)}, u32[]{:S(2)}, u32[]{:S(2)}) collective-permute-start(bf16[128,1536]{1,0:T(8,128)(2,1)S(1)} %collective-permute-done.3.refs_5_), channel_id=1, source_target_pairs={{0,8},{8,32},{32,40},{40,0},{1,9},{9,33},{33,41},{41,1},{2,10},{10... | collective-permute-start | bytes 1179656 | tf_op jit(solution)/shard_map/ppermute | solution.py:198
  52.4 16.6 %collective-permute-start.6 = (bf16[128,1536]{1,0:T(8,128)(2,1)S(1)}, bf16[128,1536]{1,0:T(8,128)(2,1)}, u32[]{:S(2)}, u32[]{:S(2)}) collective-permute-start(bf16[128,1536]{1,0:T(8,128)(2,1)S(1)} %collective-permute-done.4.refs_6_), channel_id=1, source_target_pairs={{0,40},{8,0},{32,8},{40,32},{1,41},{9,1},{33,9},{41,33},{2,42},{10... | collective-permute-start | bytes 1179656 | tf_op jit(solution)/shard_map/ppermute | solution.py:199
  58.1 24.7 %collective-permute-start.10 = (bf16[128,1536]{1,0:T(8,128)(2,1)S(1)}, bf16[128,1536]{1,0:T(8,128)(2,1)}, u32[]{:S(2)}, u32[]{:S(2)}) collective-permute-start(bf16[128,1536]{1,0:T(8,128)(2,1)S(1)} %collective-permute-done.8.refs_10_), channel_id=1, source_target_pairs={{0,40},{8,0},{32,8},{40,32},{1,41},{9,1},{33,9},{41,33},{2,42},{10... | collective-permute-start | bytes 1179656 | tf_op jit(solution)/shard_map/ppermute | solution.py:199
  58.1 27.8 %collective-permute-start.9 = (bf16[128,1536]{1,0:T(8,128)(2,1)S(1)}, bf16[128,1536]{1,0:T(8,128)(2,1)}, u32[]{:S(2)}, u32[]{:S(2)}) collective-permute-start(bf16[128,1536]{1,0:T(8,128)(2,1)S(1)} %collective-permute-done.7.refs_9_), channel_id=1, source_target_pairs={{0,8},{8,32},{32,40},{40,0},{1,9},{9,33},{33,41},{41,1},{2,10},{10... | collective-permute-start | bytes 1179656 | tf_op jit(solution)/shard_map/ppermute | solution.py:198
  67.1 23.2 %collective-permute-start.15 = (bf16[64,1536]{1,0:T(8,128)(2,1)}, bf16[64,1536]{1,0:T(8,128)(2,1)}, u32[]{:S(2)}, u32[]{:S(2)}) collective-permute-start(bf16[64,1536]{1,0:T(8,128)(2,1)} %slice.8), channel_id=1, source_target_pairs={{0,1},{1,2},{2,3},{3,4},{4,5},{5,6},{6,7},{7,0},{8,9},{9,10},{10,1... | collective-permute-start | bytes 589832 | tf_op jit(solution)/shard_map/ppermute | solution.py:196
  69.0 21.7 %collective-permute-start.16 = (bf16[64,1536]{1,0:T(8,128)(2,1)}, bf16[64,1536]{1,0:T(8,128)(2,1)}, u32[]{:S(2)}, u32[]{:S(2)}) collective-permute-start(bf16[64,1536]{1,0:T(8,128)(2,1)} %slice.9), channel_id=1, source_target_pairs={{0,7},{1,0},{2,1},{3,2},{4,3},{5,4},{6,5},{7,6},{8,15},{9,8},{10,9... | collective-permute-start | bytes 589832 | tf_op jit(solution)/shard_map/ppermute | solution.py:197
  69.7 28.6 %collective-permute-start.13 = (bf16[128,1536]{1,0:T(8,128)(2,1)S(1)}, bf16[128,1536]{1,0:T(8,128)(2,1)}, u32[]{:S(2)}, u32[]{:S(2)}) collective-permute-start(bf16[128,1536]{1,0:T(8,128)(2,1)S(1)} %collective-permute-done.11.refs_13_), channel_id=1, source_target_pairs={{0,8},{8,32},{32,40},{40,0},{1,9},{9,33},{33,41},{41,1},{2,10},{10... | collective-permute-start | bytes 1179656 | tf_op jit(solution)/shard_map/ppermute | solution.py:198
  82.8 15.6 %collective-permute-start.14 = (bf16[128,1536]{1,0:T(8,128)(2,1)S(1)}, bf16[128,1536]{1,0:T(8,128)(2,1)}, u32[]{:S(2)}, u32[]{:S(2)}) collective-permute-start(bf16[128,1536]{1,0:T(8,128)(2,1)S(1)} %collective-permute-done.12.refs_14_), channel_id=1, source_target_pairs={{0,40},{8,0},{32,8},{40,32},{1,41},{9,1},{33,9},{41,33},{2,42},{10... | collective-permute-start | bytes 1179656 | tf_op jit(solution)/shard_map/ppermute | solution.py:199
  85.9 65.1 %collective-permute-start.20 = (bf16[1536,768]{1,0:T(8,128)(2,1)}, bf16[1536,768]{1,0:T(8,128)(2,1)}, u32[]{:S(2)}, u32[]{:S(2)}) collective-permute-start(bf16[1536,768]{1,0:T(8,128)(2,1)} %all-gather.2.cloned.1.call-done.w_mine), channel_id=1, source_target_pairs={{0,16},{16,0},{1,17},{17,1},{2,18},{18,2},{3,19},{19,3},{4,20},{20... | collective-permute-start | bytes 7077896 | tf_op jit(solution)/shard_map/ppermute | solution.py:200
  90.3 8.0 %collective-permute-start.17 = (bf16[64,1536]{1,0:T(8,128)(2,1)}, bf16[64,1536]{1,0:T(8,128)(2,1)S(1)}, u32[]{:S(2)}, u32[]{:S(2)}) collective-permute-start(bf16[64,1536]{1,0:T(8,128)(2,1)} %collective-permute-done.15.refs_17_), channel_id=1, source_target_pairs={{0,8},{8,32},{32,40},{40,0},{1,9},{9,33},{33,41},{41,1},{2,10},{10... | collective-permute-start | bytes 589832 | tf_op jit(solution)/shard_map/ppermute | solution.py:198
  90.7 7.6 %collective-permute-start.18 = (bf16[64,1536]{1,0:T(8,128)(2,1)}, bf16[64,1536]{1,0:T(8,128)(2,1)S(1)}, u32[]{:S(2)}, u32[]{:S(2)}) collective-permute-start(bf16[64,1536]{1,0:T(8,128)(2,1)} %collective-permute-done.16.refs_18_), channel_id=1, source_target_pairs={{0,40},{8,0},{32,8},{40,32},{1,41},{9,1},{33,9},{41,33},{2,42},{10... | collective-permute-start | bytes 589832 | tf_op jit(solution)/shard_map/ppermute | solution.py:199
  93.9 57.1 %copy-start.1 = (bf16[1536,768]{1,0:T(8,128)(2,1)S(1)}, bf16[1536,768]{1,0:T(8,128)(2,1)}, u32[]{:S(2)}) copy-start(bf16[1536,768]{1,0:T(8,128)(2,1)} %all-gather.2.cloned.1.call-done.w_mine) | copy-start | bytes 7077892
  147.3 3.7 %collective-permute-start.19 = (bf16[768,768]{1,0:T(8,128)(2,1)}, bf16[768,768]{1,0:T(8,128)(2,1)S(1)}, u32[]{:S(2)}, u32[]{:S(2)}) collective-permute-start(bf16[768,768]{1,0:T(8,128)(2,1)} %get-tuple-element.10), channel_id=1, source_target_pairs={{0,16},{16,0},{1,17},{17,1},{2,18},{18,2},{3,19},{19,3},{4,20},{20... | collective-permute-start | bytes 3538952 | tf_op jit(solution)/shard_map/ppermute | solution.py:200
  151.0 1.7 copy-start.2
  152.7 1.3 copy-start.3
Sparse Core Ops, SparseCore 0:
  9.1 71.6 all-gather.1

commit v2 on v1

v2 whole, which is shorter than its diff:
```python
import functools

import jax
import jax.numpy as jnp
from jax import lax
from jax.experimental import pallas as pl
from jax.experimental.pallas import tpu as pltpu
from jax.sharding import Mesh
from jax.sharding import PartitionSpec as P

KW = 32
HALF = KW // 2
TM = ("y", "xh", "c")
FS = ("xl", "z")
CROSS = [
    ((xh * 2 + c) * 2 + xl, ((x2 // 2) * 2 + c) * 2 + x2 % 2)
    for xh in range(2)
    for c in range(2)
    for xl in range(2)
    for x2 in [(xh * 2 + xl + (1 if c == 0 else 3)) % 4]
]
DIAG = [
    (((xh * 2 + c) * 2 + xl) * 8 + z, (((x2 // 2) * 2 + c) * 2 + x2 % 2) * 8 + (z + d) % 8)
    for xh in range(2)
    for c in range(2)
    for xl in range(2)
    for z in range(8)
    for d in [1 if c == 0 else -1]
    for x2 in [(xh * 2 + xl + d) % 4]
]
TILE = 32
ANY = pl.BlockSpec(memory_space=pl.ANY)
VM = pl.BlockSpec(memory_space=pltpu.VMEM)
SM = pl.BlockSpec(memory_space=pltpu.SMEM)


def cyc(n, s):
    return [(i, (i + s) % n) for i in range(n)]


def front_kernel(places, meta, ids_s, *refs):
    n = places[-1][0] + 1
    own, halo, recv = refs[:3]
    blocks = refs[3 : 3 + n]
    gain, taps, scale, ids_v, sub_out, act_own, act_send = refs[3 + n : 10 + n]
    mels, ws, wf, sub, normed, xs, idb, tmp, act, sem_in, sem_out = refs[10 + n :]
    c, z, xl = meta[0], meta[1], meta[2]
    span = own.shape[0]
    rows = mels.shape[0]
    width = sub.shape[1]
    hw = act.shape[1]
    sr = ws.shape[0] // 16
    fr = wf.shape[0] // 16

    mine = pl.multiple_of(HALF + span * c, HALF)
    other = pl.multiple_of(HALF + span * (1 - c), HALF)
    outer = pl.multiple_of((rows - HALF) * c, HALF)
    inner = pl.multiple_of((rows - HALF) * (1 - c), HALF)
    copies = [
        pltpu.make_async_copy(own, mels.at[pl.ds(mine, span)], sem_in.at[0]),
        pltpu.make_async_copy(recv.at[pl.ds(0, span)], mels.at[pl.ds(other, span)], sem_in.at[1]),
        pltpu.make_async_copy(halo, mels.at[pl.ds(outer, HALF)], sem_in.at[2]),
        pltpu.make_async_copy(recv.at[pl.ds(span, HALF)], mels.at[pl.ds(inner, HALF)], sem_in.at[3]),
    ]
    late = []
    at = 4
    for which, base, flip, shift, lo, hi in places:
        block = blocks[which]
        xx = (1 - xl) if flip else xl
        j = xx * 8 + lax.rem(z + shift + 8, 8)
        if lo < sr:
            copies.append(
                pltpu.make_async_copy(
                    block.at[pl.ds(base, sr)],
                    ws.at[pl.ds(pl.multiple_of(j * sr, sr), sr)],
                    sem_in.at[at],
                )
            )
            at += 1
        a, b = max(lo, sr), hi
        late.append(
            pltpu.make_async_copy(
                block.at[pl.ds(base + a - lo, b - a)],
                wf.at[pl.ds(pl.multiple_of(j * fr + (a - sr), 32), b - a)],
                sem_in.at[at],
            )
        )
        at += 1
    for cp in copies + late:
        cp.start()
    idb[...] = jnp.broadcast_to(ids_v[...], idb.shape)
    for cp in copies:
        cp.wait()

    steps = 8
    chunk = 2 * span // steps
    tail = rows - HALF

    def embed(i):
        r = pl.ds(pl.multiple_of(HALF + i * chunk, HALF), chunk)
        sub[r, :] = jnp.dot(mels[r, :], ws[...], preferred_element_type=jnp.float32).astype(
            jnp.bfloat16
        )

    def norm16(at):
        r = pl.ds(pl.multiple_of(at, HALF), HALF)
        f = sub[r, :].astype(jnp.float32)
        mean = jnp.sum(f, axis=1, keepdims=True) * (1.0 / width)
        d = f - mean
        var = jnp.sum(d * d, axis=1, keepdims=True) * (1.0 / width)
        normed[r, :] = (d * lax.rsqrt(var + 1e-05) * gain[...]).astype(jnp.bfloat16)

    def norm(i):
        for q in range(chunk // HALF):
            norm16(HALF + i * chunk + q * HALF)

    ends = jnp.concatenate([mels[0:HALF, :], mels[tail:, :]])
    s = jnp.dot(ends, ws[...], preferred_element_type=jnp.float32).astype(jnp.bfloat16)
    sub[0:HALF, :] = s[:HALF]
    sub[tail:, :] = s[HALF:]
    embed(0)
    norm16(0)
    norm16(tail)

    def front(i, _):
        embed(i)
        norm(i - 1)
        return 0

    lax.fori_loop(1, steps, front, 0)
    norm(steps - 1)
    out_sub = pltpu.make_async_copy(sub.at[pl.ds(mine, span)], sub_out, sem_out.at[0])
    out_sub.start()
    for cp in late:
        cp.wait()

    def gated(lhs, cg):
        vcol, gcol = cg * 256, hw + cg * 256
        v = jnp.dot(lhs, wf[:, vcol : vcol + 256], preferred_element_type=jnp.float32)
        g = jnp.dot(lhs, wf[:, gcol : gcol + 256], preferred_element_type=jnp.float32)
        return (v * jax.nn.sigmoid(g)).astype(jnp.bfloat16).astype(jnp.float32)

    def edges(cg):
        glu = gated(jnp.concatenate([normed[0:HALF, :], normed[tail:, :]]), cg)
        for h in range(2):
            part = glu[:, h * 128 : (h + 1) * 128]
            xs[2 * cg + h, 0:HALF, :] = part[:HALF]
            xs[2 * cg + h, tail:, :] = part[HALF:]

    def project(i, cg):
        r = pl.ds(pl.multiple_of(HALF + i * chunk, HALF), chunk)
        glu = gated(normed[r, :], cg)
        for h in range(2):
            xs[2 * cg + h, r, :] = glu[:, h * 128 : (h + 1) * 128]

    win = TILE + KW

    def conv(g, t0, u, buf):
        buf[...] = jnp.where(idb[pl.ds(t0, win), :] == u, xs[g, pl.ds(t0, win), :], 0.0)
        s = None
        for b in range(8):
            y = buf[b : b + TILE + KW - 8, :]
            for a in range(KW // 8):
                k = 8 * a + b
                term = y[8 * a : 8 * a + TILE] * taps[g, k : k + 1, :]
                s = term if s is None else s + term
        v = s * scale[:, g * 128 : (g + 1) * 128]
        return (v * jax.nn.sigmoid(v)).astype(jnp.bfloat16)

    def tiles(i, cg):
        for q in range(chunk // TILE):
            t0 = pl.multiple_of(i * chunk + q * TILE, TILE)
            for g in (2 * cg, 2 * cg + 1):
                act[pl.ds(t0, TILE), g * 128 : (g + 1) * 128] = conv(
                    g, t0, ids_s[t0 + HALF], tmp.at[(2 * q + g) % 4]
                )

        def again(q, _):
            t0 = pl.multiple_of(i * chunk + q * TILE, TILE)

            def one(u, _):
                keep = idb[pl.ds(pl.multiple_of(t0 + HALF, HALF), TILE), :] == u
                for g in (2 * cg, 2 * cg + 1):
                    cols = slice(g * 128, (g + 1) * 128)
                    new = conv(g, t0, u, tmp.at[g % 4]).astype(jnp.float32)
                    old = act[pl.ds(t0, TILE), cols].astype(jnp.float32)
                    act[pl.ds(t0, TILE), cols] = jnp.where(keep, new, old).astype(jnp.bfloat16)
                return 0

            lax.fori_loop(ids_s[t0 + HALF] + 1, ids_s[t0 + HALF + TILE - 1] + 1, one, 0)
            return 0

        lax.fori_loop(0, chunk // TILE, again, 0)

    groups = hw // 256
    for cg in range(groups):
        edges(cg)

    def lead(i, _):
        project(i, 0)
        return 0

    lax.fori_loop(0, steps, lead, 0)
    for cg in range(groups):

        def both(i, _):
            if cg + 1 < groups:
                project(i, cg + 1)
            tiles(i, cg)
            return 0

        lax.fori_loop(0, steps, both, 0)

    outs = [
        pltpu.make_async_copy(
            act.at[pl.ds(pl.multiple_of(span * c, span), span)], act_own, sem_out.at[1]
        ),
        pltpu.make_async_copy(
            act.at[pl.ds(pl.multiple_of(span * (1 - c), span), span)], act_send, sem_out.at[2]
        ),
    ]
    for cp in outs:
        cp.start()
    out_sub.wait()
    for cp in outs:
        cp.wait()


def back_kernel(meta, sub, mine, theirs, w, out, sub_v, a_v, w_v, o_v, sem_in, sem_out):
    c = meta[0]
    span, width = sub.shape
    hw = mine.shape[1]
    here = pl.multiple_of(hw * c, 128)
    there = pl.multiple_of(hw * (1 - c), 128)
    copies = [
        pltpu.make_async_copy(
            w.at[j, h],
            w_v.at[pl.ds(j * w.shape[2], w.shape[2]), pl.ds(h * hw, hw)],
            sem_in.at[2 * j + h],
        )
        for j in range(w.shape[0])
        for h in range(2)
    ]
    first = len(copies)
    copies += [
        pltpu.make_async_copy(mine, a_v.at[:, pl.ds(here, hw)], sem_in.at[first]),
        pltpu.make_async_copy(theirs, a_v.at[:, pl.ds(there, hw)], sem_in.at[first + 1]),
        pltpu.make_async_copy(sub, sub_v, sem_in.at[first + 2]),
    ]
    for cp in copies:
        cp.start()
    for cp in copies:
        cp.wait()
    nb = 192
    outs = []
    for i in range(span // nb):
        r = pl.ds(i * nb, nb)
        for n in range(0, width, 512):
            y = jnp.dot(a_v[r, :], w_v[:, n : n + 512], preferred_element_type=jnp.float32)
            o_v[r, n : n + 512] = (sub_v[r, n : n + 512].astype(jnp.float32) + y).astype(
                jnp.bfloat16
            )
        outs.append(pltpu.make_async_copy(o_v.at[r], out.at[r], sem_out.at[i]))
        outs[-1].start()
    for cp in outs:
        cp.wait()


def on_device(mels, utt_lengths, sub_weight, norm_gain, first_weight, dw_kernel, bn_scale, second_weight):
    _, span, stack = mels.shape
    width = second_weight.shape[1]
    hw = width // 2
    sr, fr = sub_weight.shape[0], first_weight.shape[0]
    c = lax.axis_index("c")
    z = lax.axis_index("z")
    xl = lax.axis_index("xl")
    chip = lax.axis_index("y") * 2 + lax.axis_index("xh")
    barrier = lax.optimization_barrier
    zshift = lambda a, s: lax.ppermute(a, "z", cyc(8, s))
    cross = lambda a: lax.ppermute(a, ("xh", "c", "xl"), CROSS)
    swap = lambda a: lax.ppermute(a, "c", cyc(2, 1))

    half = lambda a, at: lax.dynamic_slice_in_dim(a, at + c * hw, hw, axis=a.ndim - 1)
    block = jnp.concatenate(
        [sub_weight, jnp.concatenate([half(first_weight, 0), half(first_weight, width)], axis=1)]
    )
    hi = sr + fr
    mid = hi // 2
    blocks, places = [], []

    def landed(array, parts):
        at = 0
        for flip, shift, lo, up in parts:
            places.append((len(blocks), at, flip, shift, lo, up))
            at += up - lo
        blocks.append(array)

    p = m = block
    crossed = [cross(block)]
    for s in (1, 2, 3):
        p, m = zshift(p, 1), zshift(m, -1)
        if s > 1:
            p, m, crossed[s - 2] = barrier((p, m, crossed[s - 2]))
        landed(p, [(False, -s, 0, hi)])
        landed(m, [(False, s, 0, hi)])
        crossed.append(cross(jnp.concatenate([p, m])))
    landed(block, [(False, 0, 0, hi)])
    for s, array in enumerate(crossed):
        landed(array, [(True, -s, 0, hi), (True, s, 0, hi)] if s else [(True, 0, 0, hi)])
    landed(lax.ppermute(jnp.where(c == 0, p, m), ("xh", "c", "xl", "z"), DIAG), [(True, 4, 0, hi)])
    landed(zshift(p[:mid], 1), [(False, 4, 0, mid)])
    landed(zshift(m[mid:], -1), [(False, 4, mid, hi)])

    w_back = lax.all_gather(half(second_weight, 0), FS + ("c",), axis=0, tiled=True)
    w_back = w_back.reshape(16, 2, fr, hw)

    own = mels.reshape(span, stack)
    edge = lax.dynamic_slice_in_dim(own, c * (span - HALF), HALF, axis=0)
    n_tm = 16
    out_pairs = [(2 * j + 1, 2 * j + 2) for j in range(n_tm // 2 - 1)]
    halo = lax.ppermute(edge, TM, out_pairs + [(b, a) for a, b in out_pairs])
    recv = swap(jnp.concatenate([own, halo]))

    rows = 2 * span + 2 * HALF
    ends = jnp.cumsum(utt_lengths.reshape(-1))
    positions = chip * 2 * span - HALF + jnp.arange(rows, dtype=jnp.int32)
    ids = jnp.sum((positions[:, None] >= ends[None, :]).astype(jnp.int32), axis=1)
    meta = jnp.stack([c, z, xl]).astype(jnp.int32)
    taps = half(dw_kernel, 0).astype(jnp.float32).reshape(KW, hw // 128, 128).transpose(1, 0, 2)

    bf, f32 = jnp.bfloat16, jnp.float32
    n_in = 4 + 2 * len(places)
    sub, act_own, act_send = pl.pallas_call(
        functools.partial(front_kernel, places),
        out_shape=[
            jax.ShapeDtypeStruct((span, width), bf),
            jax.ShapeDtypeStruct((span, hw), bf),
            jax.ShapeDtypeStruct((span, hw), bf),
        ],
        in_specs=[SM, SM] + [ANY] * (3 + len(blocks)) + [VM] * 4,
        out_specs=[ANY] * 3,
        scratch_shapes=[
            pltpu.VMEM((rows, stack), bf),
            pltpu.VMEM((16 * sr, width), bf),
            pltpu.VMEM((16 * fr, width), bf),
            pltpu.VMEM((rows, width), bf),
            pltpu.VMEM((rows, width), bf),
            pltpu.VMEM((hw // 128, rows, 128), f32),
            pltpu.VMEM((rows, 128), jnp.int32),
            pltpu.VMEM((4, TILE + KW, 128), f32),
            pltpu.VMEM((2 * span, hw), bf),
            pltpu.SemaphoreType.DMA((n_in,)),
            pltpu.SemaphoreType.DMA((3,)),
        ],
        compiler_params=pltpu.CompilerParams(vmem_limit_bytes=48 << 20),
        cost_estimate=pl.CostEstimate(flops=10_000_000_000, bytes_accessed=12 << 20, transcendentals=0),
        name="front",
    )(meta, ids, own, halo, recv, *blocks, norm_gain.reshape(1, width), taps,
      half(bn_scale.reshape(1, width), 0), ids.reshape(rows, 1))

    w_back, act_send = barrier((w_back, act_send))
    act_recv = swap(act_send)
    out = pl.pallas_call(
        back_kernel,
        out_shape=jax.ShapeDtypeStruct((span, width), bf),
        in_specs=[SM] + [ANY] * 4,
        out_specs=ANY,
        scratch_shapes=[
            pltpu.VMEM((span, width), bf),
            pltpu.VMEM((span, width), bf),
            pltpu.VMEM((width, width), bf),
            pltpu.VMEM((span, width), bf),
            pltpu.SemaphoreType.DMA((35,)),
            pltpu.SemaphoreType.DMA((4,)),
        ],
        compiler_params=pltpu.CompilerParams(vmem_limit_bytes=60 << 20),
        cost_estimate=pl.CostEstimate(flops=3_600_000_000, bytes_accessed=12 << 20, transcendentals=0),
        name="back",
    )(meta, sub, act_own, act_recv, w_back)
    return out.reshape(1, span, width)


def solution(mesh):
    fine = Mesh(mesh.devices.reshape(4, 2, 2, 2, 8), ("y", "xh", "c", "xl", "z"))
    in_specs = (
        P(FS, TM, None),
        P(FS, None),
        P(FS, None),
        P(),
        P(FS, None),
        P(),
        P(),
        P(FS, None),
    )
    return jax.shard_map(
        on_device, mesh=fine, in_specs=in_specs, out_specs=P(FS, TM, None), check_vma=False
    )
```

time: 169 us -> 146 us (0.86)
  starting transfers between devices: 41.6 us -> 29.4 us
  Pallas kernels: 56.5 us -> 45.7 us
  other arithmetic: 3.08 us -> 6.9 us
  local copies, waits for them, and re-layouts: 8.44 us -> 5.98 us
    pallas_call x1, Pallas kernels: 49 us -> 36.1 us  [on_device(): pl.pallas_call(functools.partial(front_kernel, places), out_shape=[jax.Sh...]
    ppermute x17 -> x13, waiting for transfers between devices: 40.7 us -> 32.4 us  [the longest x8 23.3 us: on_device(): zshift = lambda a, s: lax.ppermute(a, 'z', cyc(8, s))]
    ppermute x1, waiting for transfers between devices: 1.72 us -> 8.68 us  [on_device(): halo = lax.ppermute(edge, TM, out_pairs + [(b, a) for a, b in out_pairs])]
    ppermute x17 -> x13, starting transfers between devices: 30 us -> 24.3 us  [the longest x8 15.8 us: on_device(): zshift = lambda a, s: lax.ppermute(a, 'z', cyc(8, s))]
    concatenate x0 -> x3, other arithmetic: none -> 3.83 us  [on_device(): crossed.append(cross(jnp.concatenate([p, m])))]
    ppermute x3 -> x2, starting transfers between devices: 3.9 us -> 0.09 us  [on_device(): swap = lambda a: lax.ppermute(a, 'c', cyc(2, 1))]
    ppermute x1, starting transfers between devices: 7.69 us -> 5.03 us  [on_device(): halo = lax.ppermute(edge, TM, out_pairs + [(b, a) for a, b in out_pairs])]
    pallas_call x1, Pallas kernels: 7.46 us -> 9.57 us  [on_device(): pl.pallas_call(back_kernel, out_shape=jax.ShapeDtypeStruct((span, width),...]
  transfers between devices with their start and end apart: 22 -> 17, of which waited for: 9 -> 10; matrix products, arithmetic and copies ran while one was open for 4% -> 6% of each run, Pallas kernels for 29% -> 25%
where the time goes in v2:
time: 146 us
  Pallas kernels  45.7 us (31%)
  waiting for transfers between devices  44.2 us (30%)
  starting transfers between devices  29.4 us (20%)
  between operations  13.6 us (9%)
  other arithmetic  6.9 us (5%)
  local copies, waits for them, and re-layouts  5.98 us (4%)
    pallas_call x1, Pallas kernels, on_device(): pl.pallas_call(functools.partial(front_kernel, places), out_shape=[jax.Sh...  36.1 us
    ppermute x8, waiting for transfers between devices, on_device(): zshift = lambda a, s: lax.ppermute(a, 'z', cyc(8, s))  23.3 us
    ppermute x8, starting transfers between devices, on_device(): zshift = lambda a, s: lax.ppermute(a, 'z', cyc(8, s))  15.8 us
    pallas_call x1, Pallas kernels, on_device(): pl.pallas_call(back_kernel, out_shape=jax.ShapeDtypeStruct((span, width),...  9.57 us
    ppermute x4, waiting for transfers between devices, on_device(): cross = lambda a: lax.ppermute(a, ('xh', 'c', 'xl'), CROSS)  9.14 us
    ppermute x1, waiting for transfers between devices, on_device(): halo = lax.ppermute(edge, TM, out_pairs + [(b, a) for a, b in out_pairs])  8.68 us
    ppermute x4, starting transfers between devices, on_device(): cross = lambda a: lax.ppermute(a, ('xh', 'c', 'xl'), CROSS)  6.73 us
    ppermute x1, starting transfers between devices, on_device(): halo = lax.ppermute(edge, TM, out_pairs + [(b, a) for a, b in out_pairs])  5.03 us
  transfers between devices with their start and end apart: 17, of which 10 were waited for; matrix products, arithmetic and copies ran while one was open for 6% of the time, Pallas kernels for 25%

profile of v2, /device:TPU:1, one launch (start us, length us, event | category | flops | bytes accessed | tf_op | source)
XLA Modules:
  0.0 145.7 jit_solution(14792336908533414327)
XLA Ops:
  6.5 1.0 copy-done
  8.2 1.1 constant_dynamic-slice_fusion.2
  9.3 0.9 maximum_maximum_fusion.refs_9_
  10.2 2.5 %collective-permute-start.2 = (bf16[128,1536]{1,0:T(8,128)(2,1)S(1)}, bf16[128,1536]{1,0:T(8,128)(2,1)S(1)}, u32[]{:S(2)}, u32[]{:S(2)}) collective-permute-start(bf16[128,1536]{1,0:T(8,128)(2,1)S(1)} %maximum_maximum_fusion.refs_9_), channel_id=1, source_target_pairs={{0,1},{1,2},{2,3},{3,4},{4,5},{5,6},{6,7},{7,0},{8,9},{9,10},{10,1... | collective-permute-start | bytes 1179656 | tf_op jit(solution)/shard_map/ppermute | solution.py:279
  12.8 4.0 %collective-permute-start.3 = (bf16[128,1536]{1,0:T(8,128)(2,1)S(1)}, bf16[128,1536]{1,0:T(8,128)(2,1)S(1)}, u32[]{:S(2)}, u32[]{:S(2)}) collective-permute-start(bf16[128,1536]{1,0:T(8,128)(2,1)S(1)} %maximum_maximum_fusion.refs_9_), channel_id=1, source_target_pairs={{0,7},{1,0},{2,1},{3,2},{4,3},{5,4},{6,5},{7,6},{8,15},{9,8},{10,9... | collective-permute-start | bytes 1179656 | tf_op jit(solution)/shard_map/ppermute | solution.py:279
  16.8 2.5 %collective-permute-start.6 = (bf16[128,1536]{1,0:T(8,128)(2,1)S(1)}, bf16[128,1536]{1,0:T(8,128)(2,1)S(1)}, u32[]{:S(2)}, u32[]{:S(2)}) collective-permute-start(bf16[128,1536]{1,0:T(8,128)(2,1)S(1)} %maximum_maximum_fusion.refs_9_), channel_id=1, source_target_pairs={{0,8},{8,32},{16,56},{24,16},{32,40},{40,0},{48,24},{56,48},{1,9},... | collective-permute-start | bytes 1179656 | tf_op jit(solution)/shard_map/ppermute | solution.py:280
  19.3 6.3 %collective-permute-done.2.refs_3_ = bf16[128,1536]{1,0:T(8,128)(2,1)S(1)} collective-permute-done((bf16[128,1536]{1,0:T(8,128)(2,1)S(1)}, bf16[128,1536]{1,0:T(8,128)(2,1)S(1)}, u32[]{:S(2)}, u32[]{:S(2)}) %collective-permute-start.2) | collective-permute-done | bytes 393248 | tf_op jit(solution)/shard_map/ppermute | solution.py:279
  25.5 2.7 %collective-permute-start.5 = (bf16[128,1536]{1,0:T(8,128)(2,1)S(1)}, bf16[128,1536]{1,0:T(8,128)(2,1)}, u32[]{:S(2)}, u32[]{:S(2)}) collective-permute-start(bf16[128,1536]{1,0:T(8,128)(2,1)S(1)} %collective-permute-done.3.refs_4_), channel_id=1, source_target_pairs={{0,7},{1,0},{2,1},{3,2},{4,3},{5,4},{6,5},{7,6},{8,15},{9,8},{10,9... | collective-permute-start | bytes 1179656 | tf_op jit(solution)/shard_map/ppermute | solution.py:279
  28.2 0.9 pad_maximum_fusion.1
  29.1 2.5 %collective-permute-start.9 = (bf16[256,1536]{1,0:T(8,128)(2,1)}, bf16[256,1536]{1,0:T(8,128)(2,1)}, u32[]{:S(2)}, u32[]{:S(2)}) collective-permute-start(bf16[256,1536]{1,0:T(8,128)(2,1)} %pad_maximum_fusion.1), channel_id=1, source_target_pairs={{0,8},{8,32},{16,56},{24,16},{32,40},{40,0},{48,24},{56,48},{1,9},... | collective-permute-start | bytes 2359304 | tf_op jit(solution)/shard_map/ppermute | solution.py:280
  31.6 5.0 %collective-permute-start = (bf16[16,512]{1,0:T(8,128)(2,1)S(1)}, bf16[16,512]{1,0:T(8,128)(2,1)S(1)}, u32[]{:S(2)}, u32[]{:S(2)}) collective-permute-start(bf16[16,512]{1,0:T(8,128)(2,1)S(1)} %dynamic-slice_bitcast_fusion), channel_id=1, source_target_pairs={{16,32},{48,64},{80,96},{112,128},{144,160},{176,192},{208,224},{3... | collective-permute-start | bytes 49160 | tf_op jit(solution)/shard_map/ppermute | solution.py:321
  37.9 1.3 collective-permute-done.5.refs_6_
  39.2 2.7 %collective-permute-start.7 = (bf16[128,1536]{1,0:T(8,128)(2,1)S(1)}, bf16[128,1536]{1,0:T(8,128)(2,1)S(1)}, u32[]{:S(2)}, u32[]{:S(2)}) collective-permute-start(bf16[128,1536]{1,0:T(8,128)(2,1)S(1)} %collective-permute-done.4.refs_5_), channel_id=1, source_target_pairs={{0,1},{1,2},{2,3},{3,4},{4,5},{5,6},{6,7},{7,0},{8,9},{9,10},{10,1... | collective-permute-start | bytes 1179656 | tf_op jit(solution)/shard_map/ppermute | solution.py:279
  41.9 1.1 collective-permute-start.8
  43.0 8.7 %collective-permute-done.refs_1_ = bf16[16,512]{1,0:T(8,128)(2,1)S(1)} collective-permute-done((bf16[16,512]{1,0:T(8,128)(2,1)S(1)}, bf16[16,512]{1,0:T(8,128)(2,1)S(1)}, u32[]{:S(2)}, u32[]{:S(2)}) %collective-permute-start) | collective-permute-done | bytes 16416 | tf_op jit(solution)/shard_map/ppermute | solution.py:321
  51.6 0.9 pad_maximum_fusion
  52.6 2.0 %pad_maximum_fusion.2 = bf16[256,1536]{1,0:T(8,128)(2,1)} fusion(bf16[128,1536]{1,0:T(8,128)(2,1)} %collective-permute-done.5.refs_6_, bf16[128,1536]{1,0:T(8,128)(2,1)S(1)} %collective-permute-done.4.refs_5_), kind=kLoop, calls=%fused_computation.2 | loop fusion | flops 1572864 | bytes 1572864 | tf_op jit(solution)/shard_map/concatenate | solution.py:306
  54.6 1.0 collective-permute-done.7.refs_7_
  55.6 2.6 %collective-permute-done.8.refs_8_ = bf16[128,1536]{1,0:T(8,128)(2,1)S(1)} collective-permute-done((bf16[128,1536]{1,0:T(8,128)(2,1)}, bf16[128,1536]{1,0:T(8,128)(2,1)S(1)}, u32[]{:S(2)}, u32[]{:S(2)}) %collective-permute-start.8) | collective-permute-done | bytes 393248 | tf_op jit(solution)/shard_map/ppermute | solution.py:279
  58.2 0.9 pad_maximum_fusion.3
  59.1 1.8 %collective-permute-start.11 = (bf16[256,1536]{1,0:T(8,128)(2,1)}, bf16[256,1536]{1,0:T(8,128)(2,1)}, u32[]{:S(2)}, u32[]{:S(2)}) collective-permute-start(bf16[256,1536]{1,0:T(8,128)(2,1)} %pad_maximum_fusion.3), channel_id=1, source_target_pairs={{0,8},{8,32},{16,56},{24,16},{32,40},{40,0},{48,24},{56,48},{1,9},... | collective-permute-start | bytes 2359304 | tf_op jit(solution)/shard_map/ppermute | solution.py:280
  60.9 0.8 broadcast_select_fusion
  61.7 1.7 %collective-permute-start.12 = (bf16[128,1536]{1,0:T(8,128)(2,1)}, bf16[128,1536]{1,0:T(8,128)(2,1)}, u32[]{:S(2)}, u32[]{:S(2)}) collective-permute-start(bf16[128,1536]{1,0:T(8,128)(2,1)} %broadcast_select_fusion), channel_id=1, source_target_pairs={{0,9},{1,10},{2,11},{3,12},{4,13},{5,14},{6,15},{7,8},{8,33},{9,34... | collective-permute-start | bytes 1179656 | tf_op jit(solution)/shard_map/ppermute | solution.py:310
  64.0 1.2 reshape.60.refs_20_
  65.2 2.0 %collective-permute-start.13 = (bf16[64,1536]{1,0:T(8,128)(2,1)S(1)}, bf16[64,1536]{1,0:T(8,128)(2,1)S(1)}, u32[]{:S(2)}, u32[]{:S(2)}) collective-permute-start(bf16[64,1536]{1,0:T(8,128)(2,1)S(1)} %slice.6), channel_id=1, source_target_pairs={{0,1},{1,2},{2,3},{3,4},{4,5},{5,6},{6,7},{7,0},{8,9},{9,10},{10,1... | collective-permute-start | bytes 589832 | tf_op jit(solution)/shard_map/ppermute | solution.py:279
  68.1 5.4 %collective-permute-done.13.refs_15_ = bf16[64,1536]{1,0:T(8,128)(2,1)S(1)} collective-permute-done((bf16[64,1536]{1,0:T(8,128)(2,1)S(1)}, bf16[64,1536]{1,0:T(8,128)(2,1)S(1)}, u32[]{:S(2)}, u32[]{:S(2)}) %collective-permute-start.13) | collective-permute-done | bytes 196640 | tf_op jit(solution)/shard_map/ppermute | solution.py:279
  73.5 6.2 %collective-permute-done.14.refs_16_ = bf16[64,1536]{1,0:T(8,128)(2,1)S(1)} collective-permute-done((bf16[64,1536]{1,0:T(8,128)(2,1)S(1)}, bf16[64,1536]{1,0:T(8,128)(2,1)S(1)}, u32[]{:S(2)}, u32[]{:S(2)}) %collective-permute-start.14) | collective-permute-done | bytes 196640 | tf_op jit(solution)/shard_map/ppermute | solution.py:279
  79.7 9.1 %collective-permute-done.11.refs_13_ = bf16[256,1536]{1,0:T(8,128)(2,1)} collective-permute-done((bf16[256,1536]{1,0:T(8,128)(2,1)}, bf16[256,1536]{1,0:T(8,128)(2,1)}, u32[]{:S(2)}, u32[]{:S(2)}) %collective-permute-start.11) | collective-permute-done | bytes 786464 | tf_op jit(solution)/shard_map/ppermute | solution.py:280
  88.8 36.1 %front.1 = (bf16[768,1536]{1,0:T(8,128)(2,1)}, bf16[768,768]{1,0:T(8,128)(2,1)}, bf16[768,768]{1,0:T(8,128)(2,1)}) custom-call(s32[3]{0:T(128)S(1)} %pad_add_fusion.meta, s32[1568]{0:T(1024)S(1)} %convert_reduce_fusion.ids_s, bf16[768,512]{1,0:T(8,128)(2,1)S(1)} %bitcast.17, bf16[16,512]{1,0:T(8,128)(2,1)S(1)} %collective-permute-done.refs_1_, ...), custom_call_target="tpu_custom_call" | custom-call | flops 10000000000 | bytes 12582912 | tf_op jit(solution)/shard_map/front/pallas_call | solution.py:333
  125.1 3.0 %collective-permute-done.15.theirs = bf16[768,768]{1,0:T(8,128)(2,1)S(1)} collective-permute-done((bf16[768,768]{1,0:T(8,128)(2,1)}, bf16[768,768]{1,0:T(8,128)(2,1)S(1)}, u32[]{:S(2)}, u32[]{:S(2)}) %collective-permute-start.15) | collective-permute-done | bytes 1179680 | tf_op jit(solution)/shard_map/ppermute | solution.py:281
  128.1 1.1 copy-done.9
  129.2 9.6 %back.1 = bf16[768,1536]{1,0:T(8,128)(2,1)} custom-call(s32[3]{0:T(128)} %copy-done.2, bf16[768,1536]{1,0:T(8,128)(2,1)} %get-tuple-element.22.sub, bf16[768,768]{1,0:T(8,128)(2,1)} %get-tuple-element.23.mine, bf16[768,768]{1,0:T(8,128)(2,1)} %copy-done.9, bf16[16,2,96,768]{3,2,1,0:T(8,128)(2,1)} %bitcast.19), custom_call_target="tpu_custom_call" | custom-call | flops 3600000000 | bytes 12582912 | tf_op jit(solution)/shard_map/back/pallas_call | solution.py:363
  (47 shorter events, 3.4 us)
Async XLA Ops:
  6.5 1.0 copy-start
  6.5 118.4 %all-gather.2.cloned.1.call-start = ((), (), s32[]{:S(2)}) async-start(), calls=%async_computation | async-start | bytes 4866048 | tf_op jit(solution)/shard_map/all_gather | solution.py:314
  8.2 23.5 %copy-start.1 = (bf16[1,768,512]{2,1,0:T(8,128)(2,1)S(1)}, bf16[1,768,512]{2,1,0:T(8,128)(2,1)}, u32[]{:S(2)}) copy-start(bf16[1,768,512]{2,1,0:T(8,128)(2,1)} %param.8) | copy-start | bytes 2359300
  10.2 15.3 %collective-permute-start.2 = (bf16[128,1536]{1,0:T(8,128)(2,1)S(1)}, bf16[128,1536]{1,0:T(8,128)(2,1)S(1)}, u32[]{:S(2)}, u32[]{:S(2)}) collective-permute-start(bf16[128,1536]{1,0:T(8,128)(2,1)S(1)} %maximum_maximum_fusion.refs_9_), channel_id=1, source_target_pairs={{0,1},{1,2},{2,3},{3,4},{4,5},{5,6},{6,7},{7,0},{8,9},{9,10},{10,1... | collective-permute-start | bytes 1179656 | tf_op jit(solution)/shard_map/ppermute | solution.py:279
  12.8 12.8 %collective-permute-start.3 = (bf16[128,1536]{1,0:T(8,128)(2,1)S(1)}, bf16[128,1536]{1,0:T(8,128)(2,1)S(1)}, u32[]{:S(2)}, u32[]{:S(2)}) collective-permute-start(bf16[128,1536]{1,0:T(8,128)(2,1)S(1)} %maximum_maximum_fusion.refs_9_), channel_id=1, source_target_pairs={{0,7},{1,0},{2,1},{3,2},{4,3},{5,4},{6,5},{7,6},{8,15},{9,8},{10,9... | collective-permute-start | bytes 1179656 | tf_op jit(solution)/shard_map/ppermute | solution.py:279
  16.8 19.9 %collective-permute-start.6 = (bf16[128,1536]{1,0:T(8,128)(2,1)S(1)}, bf16[128,1536]{1,0:T(8,128)(2,1)S(1)}, u32[]{:S(2)}, u32[]{:S(2)}) collective-permute-start(bf16[128,1536]{1,0:T(8,128)(2,1)S(1)} %maximum_maximum_fusion.refs_9_), channel_id=1, source_target_pairs={{0,8},{8,32},{16,56},{24,16},{32,40},{40,0},{48,24},{56,48},{1,9},... | collective-permute-start | bytes 1179656 | tf_op jit(solution)/shard_map/ppermute | solution.py:280
  25.5 12.3 %collective-permute-start.4 = (bf16[128,1536]{1,0:T(8,128)(2,1)S(1)}, bf16[128,1536]{1,0:T(8,128)(2,1)S(1)}, u32[]{:S(2)}, u32[]{:S(2)}) collective-permute-start(bf16[128,1536]{1,0:T(8,128)(2,1)S(1)} %collective-permute-done.2.refs_3_), channel_id=1, source_target_pairs={{0,1},{1,2},{2,3},{3,4},{4,5},{5,6},{6,7},{7,0},{8,9},{9,10},{10,1... | collective-permute-start | bytes 1179656 | tf_op jit(solution)/shard_map/ppermute | solution.py:279
  25.5 13.6 %collective-permute-start.5 = (bf16[128,1536]{1,0:T(8,128)(2,1)S(1)}, bf16[128,1536]{1,0:T(8,128)(2,1)}, u32[]{:S(2)}, u32[]{:S(2)}) collective-permute-start(bf16[128,1536]{1,0:T(8,128)(2,1)S(1)} %collective-permute-done.3.refs_4_), channel_id=1, source_target_pairs={{0,7},{1,0},{2,1},{3,2},{4,3},{5,4},{6,5},{7,6},{8,15},{9,8},{10,9... | collective-permute-start | bytes 1179656 | tf_op jit(solution)/shard_map/ppermute | solution.py:279
  29.1 29.0 %collective-permute-start.9 = (bf16[256,1536]{1,0:T(8,128)(2,1)}, bf16[256,1536]{1,0:T(8,128)(2,1)}, u32[]{:S(2)}, u32[]{:S(2)}) collective-permute-start(bf16[256,1536]{1,0:T(8,128)(2,1)} %pad_maximum_fusion.1), channel_id=1, source_target_pairs={{0,8},{8,32},{16,56},{24,16},{32,40},{40,0},{48,24},{56,48},{1,9},... | collective-permute-start | bytes 2359304 | tf_op jit(solution)/shard_map/ppermute | solution.py:280
  31.6 20.0 %collective-permute-start = (bf16[16,512]{1,0:T(8,128)(2,1)S(1)}, bf16[16,512]{1,0:T(8,128)(2,1)S(1)}, u32[]{:S(2)}, u32[]{:S(2)}) collective-permute-start(bf16[16,512]{1,0:T(8,128)(2,1)S(1)} %dynamic-slice_bitcast_fusion), channel_id=1, source_target_pairs={{16,32},{48,64},{80,96},{112,128},{144,160},{176,192},{208,224},{3... | collective-permute-start | bytes 49160 | tf_op jit(solution)/shard_map/ppermute | solution.py:321
  36.7 0.7 copy-start.3
  39.2 16.4 %collective-permute-start.7 = (bf16[128,1536]{1,0:T(8,128)(2,1)S(1)}, bf16[128,1536]{1,0:T(8,128)(2,1)S(1)}, u32[]{:S(2)}, u32[]{:S(2)}) collective-permute-start(bf16[128,1536]{1,0:T(8,128)(2,1)S(1)} %collective-permute-done.4.refs_5_), channel_id=1, source_target_pairs={{0,1},{1,2},{2,3},{3,4},{4,5},{5,6},{6,7},{7,0},{8,9},{9,10},{10,1... | collective-permute-start | bytes 1179656 | tf_op jit(solution)/shard_map/ppermute | solution.py:279
  41.9 16.3 %collective-permute-start.8 = (bf16[128,1536]{1,0:T(8,128)(2,1)}, bf16[128,1536]{1,0:T(8,128)(2,1)S(1)}, u32[]{:S(2)}, u32[]{:S(2)}) collective-permute-start(bf16[128,1536]{1,0:T(8,128)(2,1)} %collective-permute-done.5.refs_6_), channel_id=1, source_target_pairs={{0,7},{1,0},{2,1},{3,2},{4,3},{5,4},{6,5},{7,6},{8,15},{9,8},{10,9... | collective-permute-start | bytes 1179656 | tf_op jit(solution)/shard_map/ppermute | solution.py:279
  52.6 14.6 %collective-permute-start.1 = (bf16[784,512]{1,0:T(8,128)(2,1)}, bf16[784,512]{1,0:T(8,128)(2,1)}, u32[]{:S(2)}, u32[]{:S(2)}) collective-permute-start(bf16[784,512]{1,0:T(8,128)(2,1)} %pad_maximum_fusion), channel_id=1, source_target_pairs={{0,16},{16,0},{1,17},{17,1},{2,18},{18,2},{3,19},{19,3},{4,20},{20... | collective-permute-start | bytes 2408456 | tf_op jit(solution)/shard_map/ppermute | solution.py:281
  54.5 8.9 %copy-start.7 = (f32[1536]{0:T(1024)S(1)}, f32[1536]{0:T(1024)}, u32[]{:S(2)}) copy-start(f32[1536]{0:T(1024)} %param.14) | copy-start | bytes 18436
  54.5 9.0 %copy-start.8 = (s32[1,64]{1,0:T(1,128)S(1)}, s32[1,64]{1,0:T(1,128)}, u32[]{:S(2)}) copy-start(s32[1,64]{1,0:T(1,128)} %param.9) | copy-start | bytes 772
  54.5 10.6 %copy-start.6 = (f32[1536]{0:T(1024)S(1)}, f32[1536]{0:T(1024)}, u32[]{:S(2)}) copy-start(f32[1536]{0:T(1024)} %param.11) | copy-start | bytes 18436
  54.6 25.2 %collective-permute-start.10 = (bf16[256,1536]{1,0:T(8,128)(2,1)}, bf16[256,1536]{1,0:T(8,128)(2,1)}, u32[]{:S(2)}, u32[]{:S(2)}) collective-permute-start(bf16[256,1536]{1,0:T(8,128)(2,1)} %pad_maximum_fusion.2), channel_id=1, source_target_pairs={{0,8},{8,32},{16,56},{24,16},{32,40},{40,0},{48,24},{56,48},{1,9},... | collective-permute-start | bytes 2359304 | tf_op jit(solution)/shard_map/ppermute | solution.py:280
  59.1 29.7 %collective-permute-start.11 = (bf16[256,1536]{1,0:T(8,128)(2,1)}, bf16[256,1536]{1,0:T(8,128)(2,1)}, u32[]{:S(2)}, u32[]{:S(2)}) collective-permute-start(bf16[256,1536]{1,0:T(8,128)(2,1)} %pad_maximum_fusion.3), channel_id=1, source_target_pairs={{0,8},{8,32},{16,56},{24,16},{32,40},{40,0},{48,24},{56,48},{1,9},... | collective-permute-start | bytes 2359304 | tf_op jit(solution)/shard_map/ppermute | solution.py:280
  61.7 18.0 %collective-permute-start.12 = (bf16[128,1536]{1,0:T(8,128)(2,1)}, bf16[128,1536]{1,0:T(8,128)(2,1)}, u32[]{:S(2)}, u32[]{:S(2)}) collective-permute-start(bf16[128,1536]{1,0:T(8,128)(2,1)} %broadcast_select_fusion), channel_id=1, source_target_pairs={{0,9},{1,10},{2,11},{3,12},{4,13},{5,14},{6,15},{7,8},{8,33},{9,34... | collective-permute-start | bytes 1179656 | tf_op jit(solution)/shard_map/ppermute | solution.py:310
  63.8 4.2 %copy-start.5 = (bf16[32,1536]{1,0:T(8,128)(2,1)S(1)}, bf16[32,1536]{1,0:T(8,128)(2,1)}, u32[]{:S(2)}) copy-start(bf16[32,1536]{1,0:T(8,128)(2,1)} %param.13) | copy-start | bytes 294916
  63.8 25.0 %copy-start.4 = (bf16[128,1536]{1,0:T(8,128)(2,1)S(1)}, bf16[128,1536]{1,0:T(8,128)(2,1)}, u32[]{:S(2)}) copy-start(bf16[128,1536]{1,0:T(8,128)(2,1)} %copy-done.3) | copy-start | bytes 1179652
  65.2 8.3 %collective-permute-start.13 = (bf16[64,1536]{1,0:T(8,128)(2,1)S(1)}, bf16[64,1536]{1,0:T(8,128)(2,1)S(1)}, u32[]{:S(2)}, u32[]{:S(2)}) collective-permute-start(bf16[64,1536]{1,0:T(8,128)(2,1)S(1)} %slice.6), channel_id=1, source_target_pairs={{0,1},{1,2},{2,3},{3,4},{4,5},{5,6},{6,7},{7,0},{8,9},{9,10},{10,1... | collective-permute-start | bytes 589832 | tf_op jit(solution)/shard_map/ppermute | solution.py:279
  67.2 12.5 %collective-permute-start.14 = (bf16[64,1536]{1,0:T(8,128)(2,1)S(1)}, bf16[64,1536]{1,0:T(8,128)(2,1)S(1)}, u32[]{:S(2)}, u32[]{:S(2)}) collective-permute-start(bf16[64,1536]{1,0:T(8,128)(2,1)S(1)} %slice.7), channel_id=1, source_target_pairs={{0,7},{1,0},{2,1},{3,2},{4,3},{5,4},{6,5},{7,6},{8,15},{9,8},{10,9... | collective-permute-start | bytes 589832 | tf_op jit(solution)/shard_map/ppermute | solution.py:279
  68.1 56.9 %copy-start.2 = (s32[3]{0:T(128)}, s32[3]{0:T(128)S(1)}, u32[]{:S(2)}) copy-start(s32[3]{0:T(128)S(1)} %pad_add_fusion.meta) | copy-start | bytes 40
  125.0 3.1 %collective-permute-start.15 = (bf16[768,768]{1,0:T(8,128)(2,1)}, bf16[768,768]{1,0:T(8,128)(2,1)S(1)}, u32[]{:S(2)}, u32[]{:S(2)}) collective-permute-start(bf16[768,768]{1,0:T(8,128)(2,1)} %get-tuple-element.25), channel_id=1, source_target_pairs={{0,16},{16,0},{1,17},{17,1},{2,18},{18,2},{3,19},{19,3},{4,20},{20... | collective-permute-start | bytes 3538952 | tf_op jit(solution)/shard_map/ppermute | solution.py:281
  128.1 1.1 copy-start.9
Sparse Core Ops, SparseCore 0:
  9.2 76.4 all-gather.1

commit v3 on v2

--- a/solution.py
+++ b/solution.py
@@ -38,7 +38,17 @@
     return [(i, (i + s) % n) for i in range(n)]
 
 
-def front_kernel(places, meta, ids_s, *refs):
+def pack_kernel(sub, first, out):
+    c = lax.axis_index("c")
+    sr, width = sub.shape
+    hw = width // 2
+    out[0:sr, :] = sub[...]
+    for h in range(2):
+        cols = pl.ds(pl.multiple_of(h * width + c * hw, 128), hw)
+        out[sr:, h * hw : (h + 1) * hw] = first[:, cols]
+
+
+def front_kernel(places, meta, ids_s, starts, *refs):
     n = places[-1][0] + 1
     own, halo, recv = refs[:3]
     blocks = refs[3 : 3 + n]
@@ -162,9 +172,9 @@
             y = buf[b : b + TILE + KW - 8, :]
             for a in range(KW // 8):
                 k = 8 * a + b
-                term = y[8 * a : 8 * a + TILE] * taps[g, k : k + 1, :]
+                term = y[8 * a : 8 * a + TILE].reshape(TILE // 8, 8, 128) * taps[g, k][None]
                 s = term if s is None else s + term
-        v = s * scale[:, g * 128 : (g + 1) * 128]
+        v = s.reshape(TILE, 128) * scale[:, g * 128 : (g + 1) * 128]
         return (v * jax.nn.sigmoid(v)).astype(jnp.bfloat16)
 
     def tiles(i, cg):
@@ -175,22 +185,18 @@
                     g, t0, ids_s[t0 + HALF], tmp.at[(2 * q + g) % 4]
                 )
 
-        def again(q, _):
-            t0 = pl.multiple_of(i * chunk + q * TILE, TILE)
-
-            def one(u, _):
-                keep = idb[pl.ds(pl.multiple_of(t0 + HALF, HALF), TILE), :] == u
-                for g in (2 * cg, 2 * cg + 1):
-                    cols = slice(g * 128, (g + 1) * 128)
-                    new = conv(g, t0, u, tmp.at[g % 4]).astype(jnp.float32)
-                    old = act[pl.ds(t0, TILE), cols].astype(jnp.float32)
-                    act[pl.ds(t0, TILE), cols] = jnp.where(keep, new, old).astype(jnp.bfloat16)
-                return 0
-
-            lax.fori_loop(ids_s[t0 + HALF] + 1, ids_s[t0 + HALF + TILE - 1] + 1, one, 0)
+        def again(u, _):
+            t0 = pl.multiple_of(jnp.bitwise_and(starts[u], -TILE), TILE)
+            keep = idb[pl.ds(pl.multiple_of(t0 + HALF, HALF), TILE), :] == u
+            for g in (2 * cg, 2 * cg + 1):
+                cols = slice(g * 128, (g + 1) * 128)
+                new = conv(g, t0, u, tmp.at[g % 4]).astype(jnp.float32)
+                old = act[pl.ds(t0, TILE), cols].astype(jnp.float32)
+                act[pl.ds(t0, TILE), cols] = jnp.where(keep, new, old).astype(jnp.bfloat16)
             return 0
 
-        lax.fori_loop(0, chunk // TILE, again, 0)
+        row = i * chunk + HALF
+        lax.fori_loop(ids_s[row] + 1, ids_s[row + chunk - 1] + 1, again, 0)
 
     groups = hw // 256
     for cg in range(groups):
@@ -247,21 +253,26 @@
         pltpu.make_async_copy(theirs, a_v.at[:, pl.ds(there, hw)], sem_in.at[first + 1]),
         pltpu.make_async_copy(sub, sub_v, sem_in.at[first + 2]),
     ]
-    for cp in copies:
+    order = [cp for cp in copies[first:]] + [cp for h in range(2) for cp in copies[h:first:2]]
+    for cp in order:
         cp.start()
-    for cp in copies:
+    for cp in copies[first:]:
         cp.wait()
-    nb = 192
+    nb = 256
     outs = []
-    for i in range(span // nb):
-        r = pl.ds(i * nb, nb)
-        for n in range(0, width, 512):
-            y = jnp.dot(a_v[r, :], w_v[:, n : n + 512], preferred_element_type=jnp.float32)
-            o_v[r, n : n + 512] = (sub_v[r, n : n + 512].astype(jnp.float32) + y).astype(
-                jnp.bfloat16
-            )
-        outs.append(pltpu.make_async_copy(o_v.at[r], out.at[r], sem_out.at[i]))
-        outs[-1].start()
+    for h in range(2):
+        for cp in copies[h:first:2]:
+            cp.wait()
+        for i in range(span // nb):
+            r = pl.ds(i * nb, nb)
+            for n in range(h * hw, (h + 1) * hw, 256):
+                y = jnp.dot(a_v[r, :], w_v[:, n : n + 256], preferred_element_type=jnp.float32)
+                o_v[r, n : n + 256] = (sub_v[r, n : n + 256].astype(jnp.float32) + y).astype(
+                    jnp.bfloat16
+                )
+            cols = pl.ds(h * hw, hw)
+            outs.append(pltpu.make_async_copy(o_v.at[r, cols], out.at[r, cols], sem_out.at[len(outs)]))
+            outs[-1].start()
     for cp in outs:
         cp.wait()
 
@@ -281,12 +292,33 @@
     swap = lambda a: lax.ppermute(a, "c", cyc(2, 1))
 
     half = lambda a, at: lax.dynamic_slice_in_dim(a, at + c * hw, hw, axis=a.ndim - 1)
-    block = jnp.concatenate(
-        [sub_weight, jnp.concatenate([half(first_weight, 0), half(first_weight, width)], axis=1)]
-    )
     hi = sr + fr
-    mid = hi // 2
+    block = pl.pallas_call(
+        pack_kernel,
+        out_shape=jax.ShapeDtypeStruct((hi, width), jnp.bfloat16),
+        in_specs=[VM] * 2,
+        out_specs=VM,
+        name="front_pack",
+    )(sub_weight, first_weight)
+    rows = 2 * span + 2 * HALF
+    ends = jnp.cumsum(utt_lengths.reshape(-1))
+    positions = chip * 2 * span - HALF + jnp.arange(rows, dtype=jnp.int32)
+    ids = jnp.sum((positions[:, None] >= ends[None, :]).astype(jnp.int32), axis=1)
+    meta = jnp.stack([c, z, xl]).astype(jnp.int32)
+    starts = jnp.concatenate([jnp.zeros(1, jnp.int32), ends]) - chip * 2 * span
+    taps = half(dw_kernel, 0).astype(jnp.float32).reshape(KW, hw // 128, 128).transpose(1, 0, 2)
+    taps = jnp.broadcast_to(taps[:, :, None, :], (hw // 128, KW, 8, 128))
+    gain = norm_gain.reshape(1, width)
+    scale = half(bn_scale.reshape(1, width), 0)
+    small = (meta, ids, ids.reshape(rows, 1), starts, taps, gain, scale)
+
     blocks, places = [], []
+
+    own = mels.reshape(span, stack)
+    edge = lax.dynamic_slice_in_dim(own, c * (span - HALF), HALF, axis=0)
+    n_tm = 16
+    out_pairs = [(2 * j + 1, 2 * j + 2) for j in range(n_tm // 2 - 1)]
+    halo = lax.ppermute(edge, TM, out_pairs + [(b, a) for a, b in out_pairs])
 
     def landed(array, parts):
         at = 0
@@ -295,12 +327,17 @@
             at += up - lo
         blocks.append(array)
 
+    w_half = half(second_weight, 0)
     p = m = block
     crossed = [cross(block)]
     for s in (1, 2, 3):
         p, m = zshift(p, 1), zshift(m, -1)
-        if s > 1:
-            p, m, crossed[s - 2] = barrier((p, m, crossed[s - 2]))
+        if s == 1:
+            p, m, small = barrier((p, m, small))
+        elif s == 2:
+            p, m, crossed[0] = barrier((p, m, crossed[0]))
+        elif s == 3:
+            p, m, crossed[1] = barrier((p, m, crossed[1]))
         landed(p, [(False, -s, 0, hi)])
         landed(m, [(False, s, 0, hi)])
         crossed.append(cross(jnp.concatenate([p, m])))
@@ -308,26 +345,14 @@
     for s, array in enumerate(crossed):
         landed(array, [(True, -s, 0, hi), (True, s, 0, hi)] if s else [(True, 0, 0, hi)])
     landed(lax.ppermute(jnp.where(c == 0, p, m), ("xh", "c", "xl", "z"), DIAG), [(True, 4, 0, hi)])
-    landed(zshift(p[:mid], 1), [(False, 4, 0, mid)])
-    landed(zshift(m[mid:], -1), [(False, 4, mid, hi)])
-
-    w_back = lax.all_gather(half(second_weight, 0), FS + ("c",), axis=0, tiled=True)
+    landed(zshift(p[: hi // 2], 1), [(False, 4, 0, hi // 2)])
+    landed(zshift(m[hi // 2 :], -1), [(False, 4, hi // 2, hi)])
+
+    recv = swap(jnp.concatenate([own, halo]))
+    w_back = lax.all_gather(w_half, FS + ("c",), axis=0, tiled=True)
     w_back = w_back.reshape(16, 2, fr, hw)
 
-    own = mels.reshape(span, stack)
-    edge = lax.dynamic_slice_in_dim(own, c * (span - HALF), HALF, axis=0)
-    n_tm = 16
-    out_pairs = [(2 * j + 1, 2 * j + 2) for j in range(n_tm // 2 - 1)]
-    halo = lax.ppermute(edge, TM, out_pairs + [(b, a) for a, b in out_pairs])
-    recv = swap(jnp.concatenate([own, halo]))
-
-    rows = 2 * span + 2 * HALF
-    ends = jnp.cumsum(utt_lengths.reshape(-1))
-    positions = chip * 2 * span - HALF + jnp.arange(rows, dtype=jnp.int32)
-    ids = jnp.sum((positions[:, None] >= ends[None, :]).astype(jnp.int32), axis=1)
-    meta = jnp.stack([c, z, xl]).astype(jnp.int32)
-    taps = half(dw_kernel, 0).astype(jnp.float32).reshape(KW, hw // 128, 128).transpose(1, 0, 2)
-
+    meta, ids, ids_col, starts, taps, gain, scale = small
     bf, f32 = jnp.bfloat16, jnp.float32
     n_in = 4 + 2 * len(places)
     sub, act_own, act_send = pl.pallas_call(
@@ -337,7 +362,7 @@
             jax.ShapeDtypeStruct((span, hw), bf),
             jax.ShapeDtypeStruct((span, hw), bf),
         ],
-        in_specs=[SM, SM] + [ANY] * (3 + len(blocks)) + [VM] * 4,
+        in_specs=[SM] * 3 + [ANY] * (3 + len(blocks)) + [VM] * 4,
         out_specs=[ANY] * 3,
         scratch_shapes=[
             pltpu.VMEM((rows, stack), bf),
@@ -355,8 +380,7 @@
         compiler_params=pltpu.CompilerParams(vmem_limit_bytes=48 << 20),
         cost_estimate=pl.CostEstimate(flops=10_000_000_000, bytes_accessed=12 << 20, transcendentals=0),
         name="front",
-    )(meta, ids, own, halo, recv, *blocks, norm_gain.reshape(1, width), taps,
-      half(bn_scale.reshape(1, width), 0), ids.reshape(rows, 1))
+    )(meta, ids, starts, own, halo, recv, *blocks, gain, taps, scale, ids_col)
 
     w_back, act_send = barrier((w_back, act_send))
     act_recv = swap(act_send)
@@ -371,7 +395,7 @@
             pltpu.VMEM((width, width), bf),
             pltpu.VMEM((span, width), bf),
             pltpu.SemaphoreType.DMA((35,)),
-            pltpu.SemaphoreType.DMA((4,)),
+            pltpu.SemaphoreType.DMA((6,)),
         ],
         compiler_params=pltpu.CompilerParams(vmem_limit_bytes=60 << 20),
         cost_estimate=pl.CostEstimate(flops=3_600_000_000, bytes_accessed=12 << 20, transcendentals=0),

time: 146 us -> 144 us (0.986)
  local copies, waits for them, and re-layouts: 5.98 us -> 10.2 us
  other arithmetic: 6.9 us -> 4.19 us
  Pallas kernels: 45.7 us -> 43.9 us
    pallas_call x1, Pallas kernels: 36.1 us -> 32.8 us  [on_device(): pl.pallas_call(functools.partial(front_kernel, places), out_shape=[jax.Sh...]
    unnamed x20 -> x28, local copies, waits for them, and re-layouts: 2.83 us -> 5.78 us
    pallas_call x0 -> x1, Pallas kernels: none -> 1.91 us  [on_device(): pl.pallas_call(pack_kernel, out_shape=jax.ShapeDtypeStruct((hi, width), j...]
  transfers between devices with their start and end apart: 17 -> 17, of which waited for: 10 -> 10; matrix products, arithmetic and copies ran while one was open for 6% -> 6% of each run, Pallas kernels for 25% -> 24%
where the time goes in v3:
time: 144 us; the launch traced here: 143 us
  Pallas kernels  43.9 us (30%)
  waiting for transfers between devices  43.3 us (30%)
  starting transfers between devices  28.1 us (20%)
  between operations  13.6 us (9%)
  local copies, waits for them, and re-layouts  10.2 us (7%)
  other arithmetic  4.19 us (3%)
    pallas_call x1, Pallas kernels, on_device(): pl.pallas_call(functools.partial(front_kernel, places), out_shape=[jax.Sh...  32.8 us
    ppermute x8, waiting for transfers between devices, on_device(): zshift = lambda a, s: lax.ppermute(a, 'z', cyc(8, s))  24 us
    ppermute x8, starting transfers between devices, on_device(): zshift = lambda a, s: lax.ppermute(a, 'z', cyc(8, s))  14.4 us
    pallas_call x1, Pallas kernels, on_device(): pl.pallas_call(back_kernel, out_shape=jax.ShapeDtypeStruct((span, width),...  9.16 us
    ppermute x4, waiting for transfers between devices, on_device(): cross = lambda a: lax.ppermute(a, ('xh', 'c', 'xl'), CROSS)  8.35 us
    ppermute x1, waiting for transfers between devices, on_device(): halo = lax.ppermute(edge, TM, out_pairs + [(b, a) for a, b in out_pairs])  7.8 us
    ppermute x4, starting transfers between devices, on_device(): cross = lambda a: lax.ppermute(a, ('xh', 'c', 'xl'), CROSS)  7.29 us
    unnamed x28, local copies, waits for them, and re-layouts  5.78 us
  transfers between devices with their start and end apart: 17, of which 10 were waited for; matrix products, arithmetic and copies ran while one was open for 6% of the time, Pallas kernels for 24%

profile of v3, /device:TPU:1, one launch (start us, length us, event | category | flops | bytes accessed | tf_op | source)
XLA Modules:
  0.0 143.2 jit_solution(5515815711419140696)
XLA Ops:
  8.2 1.9 %front_pack.1.refs_9_ = bf16[128,1536]{1,0:T(8,128)(2,1)} custom-call(bf16[32,1536]{1,0:T(8,128)(2,1)} %sub.15, bf16[96,3072]{1,0:T(8,128)(2,1)} %first.1), custom_call_target="tpu_custom_call" | custom-call | tf_op jit(solution)/shard_map/front_pack/pallas_call | solution.py:296
  10.1 2.5 %collective-permute-start = (bf16[128,1536]{1,0:T(8,128)(2,1)}, bf16[128,1536]{1,0:T(8,128)(2,1)S(1)}, u32[]{:S(2)}, u32[]{:S(2)}) collective-permute-start(bf16[128,1536]{1,0:T(8,128)(2,1)} %front_pack.1.refs_9_), channel_id=1, source_target_pairs={{0,1},{1,2},{2,3},{3,4},{4,5},{5,6},{6,7},{7,0},{8,9},{9,10},{10,1... | collective-permute-start | bytes 1179656 | tf_op jit(solution)/shard_map/ppermute | solution.py:290
  12.6 3.9 %collective-permute-start.1 = (bf16[128,1536]{1,0:T(8,128)(2,1)}, bf16[128,1536]{1,0:T(8,128)(2,1)S(1)}, u32[]{:S(2)}, u32[]{:S(2)}) collective-permute-start(bf16[128,1536]{1,0:T(8,128)(2,1)} %front_pack.1.refs_9_), channel_id=1, source_target_pairs={{0,7},{1,0},{2,1},{3,2},{4,3},{5,4},{6,5},{7,6},{8,15},{9,8},{10,9... | collective-permute-start | bytes 1179656 | tf_op jit(solution)/shard_map/ppermute | solution.py:290
  16.5 2.5 %collective-permute-start.6 = (bf16[128,1536]{1,0:T(8,128)(2,1)}, bf16[128,1536]{1,0:T(8,128)(2,1)S(1)}, u32[]{:S(2)}, u32[]{:S(2)}) collective-permute-start(bf16[128,1536]{1,0:T(8,128)(2,1)} %front_pack.1.refs_9_), channel_id=1, source_target_pairs={{0,8},{8,32},{16,56},{24,16},{32,40},{40,0},{48,24},{56,48},{1,9},... | collective-permute-start | bytes 1179656 | tf_op jit(solution)/shard_map/ppermute | solution.py:291
  19.8 5.7 %collective-permute-done.refs_3_ = bf16[128,1536]{1,0:T(8,128)(2,1)S(1)} collective-permute-done((bf16[128,1536]{1,0:T(8,128)(2,1)}, bf16[128,1536]{1,0:T(8,128)(2,1)S(1)}, u32[]{:S(2)}, u32[]{:S(2)}) %collective-permute-start) | collective-permute-done | bytes 393248 | tf_op jit(solution)/shard_map/ppermute | solution.py:290
  25.5 0.9 broadcast_in_dim.2.refs_18_
  26.5 2.7 %collective-permute-start.5 = (bf16[128,1536]{1,0:T(8,128)(2,1)S(1)}, bf16[128,1536]{1,0:T(8,128)(2,1)S(1)}, u32[]{:S(2)}, u32[]{:S(2)}) collective-permute-start(bf16[128,1536]{1,0:T(8,128)(2,1)S(1)} %collective-permute-done.1.refs_4_), channel_id=1, source_target_pairs={{0,7},{1,0},{2,1},{3,2},{4,3},{5,4},{6,5},{7,6},{8,15},{9,8},{10,9... | collective-permute-start | bytes 1179656 | tf_op jit(solution)/shard_map/ppermute | solution.py:290
  29.2 0.9 pad_maximum_fusion.1
  30.1 2.5 %collective-permute-start.9 = (bf16[256,1536]{1,0:T(8,128)(2,1)}, bf16[256,1536]{1,0:T(8,128)(2,1)}, u32[]{:S(2)}, u32[]{:S(2)}) collective-permute-start(bf16[256,1536]{1,0:T(8,128)(2,1)} %pad_maximum_fusion.1), channel_id=1, source_target_pairs={{0,8},{8,32},{16,56},{24,16},{32,40},{40,0},{48,24},{56,48},{1,9},... | collective-permute-start | bytes 2359304 | tf_op jit(solution)/shard_map/ppermute | solution.py:291
  32.6 5.0 %collective-permute-start.2 = (bf16[16,512]{1,0:T(8,128)(2,1)S(1)}, bf16[16,512]{1,0:T(8,128)(2,1)S(1)}, u32[]{:S(2)}, u32[]{:S(2)}) collective-permute-start(bf16[16,512]{1,0:T(8,128)(2,1)S(1)} %dynamic-slice_bitcast_fusion), channel_id=1, source_target_pairs={{16,32},{48,64},{80,96},{112,128},{144,160},{176,192},{208,224},{3... | collective-permute-start | bytes 49160 | tf_op jit(solution)/shard_map/ppermute | solution.py:321
  38.5 3.1 %collective-permute-done.5.refs_6_ = bf16[128,1536]{1,0:T(8,128)(2,1)S(1)} collective-permute-done((bf16[128,1536]{1,0:T(8,128)(2,1)S(1)}, bf16[128,1536]{1,0:T(8,128)(2,1)S(1)}, u32[]{:S(2)}, u32[]{:S(2)}) %collective-permute-start.5) | collective-permute-done | bytes 393248 | tf_op jit(solution)/shard_map/ppermute | solution.py:290
  41.6 2.6 %collective-permute-start.7 = (bf16[128,1536]{1,0:T(8,128)(2,1)S(1)}, bf16[128,1536]{1,0:T(8,128)(2,1)S(1)}, u32[]{:S(2)}, u32[]{:S(2)}) collective-permute-start(bf16[128,1536]{1,0:T(8,128)(2,1)S(1)} %collective-permute-done.4.refs_5_), channel_id=1, source_target_pairs={{0,1},{1,2},{2,3},{3,4},{4,5},{5,6},{6,7},{7,0},{8,9},{9,10},{10,1... | collective-permute-start | bytes 1179656 | tf_op jit(solution)/shard_map/ppermute | solution.py:290
  44.3 7.8 %collective-permute-done.2.refs_1_ = bf16[16,512]{1,0:T(8,128)(2,1)S(1)} collective-permute-done((bf16[16,512]{1,0:T(8,128)(2,1)S(1)}, bf16[16,512]{1,0:T(8,128)(2,1)S(1)}, u32[]{:S(2)}, u32[]{:S(2)}) %collective-permute-start.2) | collective-permute-done | bytes 16416 | tf_op jit(solution)/shard_map/ppermute | solution.py:321
  52.3 1.0 pad_maximum_fusion.2
  53.2 4.1 %collective-permute-done.7.refs_7_ = bf16[128,1536]{1,0:T(8,128)(2,1)S(1)} collective-permute-done((bf16[128,1536]{1,0:T(8,128)(2,1)S(1)}, bf16[128,1536]{1,0:T(8,128)(2,1)S(1)}, u32[]{:S(2)}, u32[]{:S(2)}) %collective-permute-start.7) | collective-permute-done | bytes 393248 | tf_op jit(solution)/shard_map/ppermute | solution.py:290
  57.3 2.2 %collective-permute-done.8.refs_8_ = bf16[128,1536]{1,0:T(8,128)(2,1)S(1)} collective-permute-done((bf16[128,1536]{1,0:T(8,128)(2,1)S(1)}, bf16[128,1536]{1,0:T(8,128)(2,1)S(1)}, u32[]{:S(2)}, u32[]{:S(2)}) %collective-permute-start.8) | collective-permute-done | bytes 393248 | tf_op jit(solution)/shard_map/ppermute | solution.py:290
  59.5 0.9 pad_maximum_fusion.3
  60.4 2.3 %collective-permute-start.11 = (bf16[256,1536]{1,0:T(8,128)(2,1)}, bf16[256,1536]{1,0:T(8,128)(2,1)}, u32[]{:S(2)}, u32[]{:S(2)}) collective-permute-start(bf16[256,1536]{1,0:T(8,128)(2,1)} %pad_maximum_fusion.3), channel_id=1, source_target_pairs={{0,8},{8,32},{16,56},{24,16},{32,40},{40,0},{48,24},{56,48},{1,9},... | collective-permute-start | bytes 2359304 | tf_op jit(solution)/shard_map/ppermute | solution.py:291
  63.6 1.1 collective-permute-start.12
  66.1 1.2 collective-permute-start.13
  67.3 1.0 copy-done.13
  68.3 1.4 %collective-permute-start.14 = (bf16[64,1536]{1,0:T(8,128)(2,1)}, bf16[64,1536]{1,0:T(8,128)(2,1)}, u32[]{:S(2)}, u32[]{:S(2)}) collective-permute-start(bf16[64,1536]{1,0:T(8,128)(2,1)} %slice.7), channel_id=1, source_target_pairs={{0,7},{1,0},{2,1},{3,2},{4,3},{5,4},{6,5},{7,6},{8,15},{9,8},{10,9... | collective-permute-start | bytes 589832 | tf_op jit(solution)/shard_map/ppermute | solution.py:290
  69.7 1.2 copy.16.refs_20_
  70.9 1.5 %collective-permute-done.13.refs_15_ = bf16[64,1536]{1,0:T(8,128)(2,1)} collective-permute-done((bf16[64,1536]{1,0:T(8,128)(2,1)}, bf16[64,1536]{1,0:T(8,128)(2,1)}, u32[]{:S(2)}, u32[]{:S(2)}) %collective-permute-start.13) | collective-permute-done | bytes 196640 | tf_op jit(solution)/shard_map/ppermute | solution.py:290
  72.4 7.3 %collective-permute-done.14.refs_16_ = bf16[64,1536]{1,0:T(8,128)(2,1)} collective-permute-done((bf16[64,1536]{1,0:T(8,128)(2,1)}, bf16[64,1536]{1,0:T(8,128)(2,1)}, u32[]{:S(2)}, u32[]{:S(2)}) %collective-permute-start.14) | collective-permute-done | bytes 196640 | tf_op jit(solution)/shard_map/ppermute | solution.py:290
  79.7 8.3 %collective-permute-done.11.refs_13_ = bf16[256,1536]{1,0:T(8,128)(2,1)} collective-permute-done((bf16[256,1536]{1,0:T(8,128)(2,1)}, bf16[256,1536]{1,0:T(8,128)(2,1)}, u32[]{:S(2)}, u32[]{:S(2)}) %collective-permute-start.11) | collective-permute-done | bytes 786464 | tf_op jit(solution)/shard_map/ppermute | solution.py:291
  88.1 1.0 copy-done.4
  89.1 1.0 copy-done.7
  90.1 32.8 %front.1 = (bf16[768,1536]{1,0:T(8,128)(2,1)}, bf16[768,768]{1,0:T(8,128)(2,1)}, bf16[768,768]{1,0:T(8,128)(2,1)}) custom-call(s32[3]{0:T(128)S(1)} %pad_add_fusion.meta, s32[1568]{0:T(1024)S(1)} %convert_reduce_fusion.ids_s, s32[65]{0:T(128)S(1)} %add_subtract_fusion.starts, bf16[768,512]{1,0:T(8,128)(2,1)S(1)} %bitcast.11, ...), custom_call_target="tpu_custom_call" | custom-call | flops 10000000000 | bytes 12582912 | tf_op jit(solution)/shard_map/front/pallas_call | solution.py:358
  123.0 3.0 %collective-permute-done.15.theirs = bf16[768,768]{1,0:T(8,128)(2,1)S(1)} collective-permute-done((bf16[768,768]{1,0:T(8,128)(2,1)}, bf16[768,768]{1,0:T(8,128)(2,1)S(1)}, u32[]{:S(2)}, u32[]{:S(2)}) %collective-permute-start.15) | collective-permute-done | bytes 1179680 | tf_op jit(solution)/shard_map/ppermute | solution.py:292
  126.1 1.1 copy-done.12
  127.2 9.2 %back.1 = bf16[768,1536]{1,0:T(8,128)(2,1)} custom-call(s32[3]{0:T(128)} %copy-done.5, bf16[768,1536]{1,0:T(8,128)(2,1)} %get-tuple-element.40.sub, bf16[768,768]{1,0:T(8,128)(2,1)} %get-tuple-element.41.mine, bf16[768,768]{1,0:T(8,128)(2,1)} %copy-done.12, bf16[16,2,96,768]{3,2,1,0:T(8,128)(2,1)} %bitcast.14), custom_call_target="tpu_custom_call" | custom-call | flops 3600000000 | bytes 12582912 | tf_op jit(solution)/shard_map/back/pallas_call | solution.py:387
  (59 shorter events, 5.8 us)
Async XLA Ops:
  6.5 1.0 copy-start
  6.5 12.4 %copy-start.8 = (bf16[32,1536]{1,0:T(8,128)(2,1)S(1)}, bf16[32,1536]{1,0:T(8,128)(2,1)}, u32[]{:S(2)}) copy-start(bf16[32,1536]{1,0:T(8,128)(2,1)} %param.13) | copy-start | bytes 294916
  6.5 12.5 %copy-start.10 = (f32[1536]{0:T(1024)S(1)}, f32[1536]{0:T(1024)}, u32[]{:S(2)}) copy-start(f32[1536]{0:T(1024)} %param.14) | copy-start | bytes 18436
  6.5 12.6 %copy-start.11 = (s32[1,64]{1,0:T(1,128)S(1)}, s32[1,64]{1,0:T(1,128)}, u32[]{:S(2)}) copy-start(s32[1,64]{1,0:T(1,128)} %param.9) | copy-start | bytes 772
  6.5 13.1 %copy-start.9 = (f32[1536]{0:T(1024)S(1)}, f32[1536]{0:T(1024)}, u32[]{:S(2)}) copy-start(f32[1536]{0:T(1024)} %param.11) | copy-start | bytes 18436
  6.5 116.4 %all-gather.2.cloned.1.call-start = ((), (), s32[]{:S(2)}) async-start(), calls=%async_computation | async-start | bytes 4866048 | tf_op jit(solution)/shard_map/all_gather | solution.py:352
  10.1 15.5 %collective-permute-start = (bf16[128,1536]{1,0:T(8,128)(2,1)}, bf16[128,1536]{1,0:T(8,128)(2,1)S(1)}, u32[]{:S(2)}, u32[]{:S(2)}) collective-permute-start(bf16[128,1536]{1,0:T(8,128)(2,1)} %front_pack.1.refs_9_), channel_id=1, source_target_pairs={{0,1},{1,2},{2,3},{3,4},{4,5},{5,6},{6,7},{7,0},{8,9},{9,10},{10,1... | collective-permute-start | bytes 1179656 | tf_op jit(solution)/shard_map/ppermute | solution.py:290
  12.6 13.0 %collective-permute-start.1 = (bf16[128,1536]{1,0:T(8,128)(2,1)}, bf16[128,1536]{1,0:T(8,128)(2,1)S(1)}, u32[]{:S(2)}, u32[]{:S(2)}) collective-permute-start(bf16[128,1536]{1,0:T(8,128)(2,1)} %front_pack.1.refs_9_), channel_id=1, source_target_pairs={{0,7},{1,0},{2,1},{3,2},{4,3},{5,4},{6,5},{7,6},{8,15},{9,8},{10,9... | collective-permute-start | bytes 1179656 | tf_op jit(solution)/shard_map/ppermute | solution.py:290
  16.5 21.1 %collective-permute-start.6 = (bf16[128,1536]{1,0:T(8,128)(2,1)}, bf16[128,1536]{1,0:T(8,128)(2,1)S(1)}, u32[]{:S(2)}, u32[]{:S(2)}) collective-permute-start(bf16[128,1536]{1,0:T(8,128)(2,1)} %front_pack.1.refs_9_), channel_id=1, source_target_pairs={{0,8},{8,32},{16,56},{24,16},{32,40},{40,0},{48,24},{56,48},{1,9},... | collective-permute-start | bytes 1179656 | tf_op jit(solution)/shard_map/ppermute | solution.py:291
  19.0 13.6 %copy-start.1 = (bf16[1,768,512]{2,1,0:T(8,128)(2,1)S(1)}, bf16[1,768,512]{2,1,0:T(8,128)(2,1)}, u32[]{:S(2)}) copy-start(bf16[1,768,512]{2,1,0:T(8,128)(2,1)} %param.8) | copy-start | bytes 2359300
  19.8 68.3 %copy-start.5 = (s32[3]{0:T(128)}, s32[3]{0:T(128)S(1)}, u32[]{:S(2)}) copy-start(s32[3]{0:T(128)S(1)} %pad_add_fusion.meta) | copy-start | bytes 40
  26.5 12.0 %collective-permute-start.4 = (bf16[128,1536]{1,0:T(8,128)(2,1)S(1)}, bf16[128,1536]{1,0:T(8,128)(2,1)S(1)}, u32[]{:S(2)}, u32[]{:S(2)}) collective-permute-start(bf16[128,1536]{1,0:T(8,128)(2,1)S(1)} %collective-permute-done.refs_3_), channel_id=1, source_target_pairs={{0,1},{1,2},{2,3},{3,4},{4,5},{5,6},{6,7},{7,0},{8,9},{9,10},{10,1... | collective-permute-start | bytes 1179656 | tf_op jit(solution)/shard_map/ppermute | solution.py:290
  26.5 15.1 %collective-permute-start.5 = (bf16[128,1536]{1,0:T(8,128)(2,1)S(1)}, bf16[128,1536]{1,0:T(8,128)(2,1)S(1)}, u32[]{:S(2)}, u32[]{:S(2)}) collective-permute-start(bf16[128,1536]{1,0:T(8,128)(2,1)S(1)} %collective-permute-done.1.refs_4_), channel_id=1, source_target_pairs={{0,7},{1,0},{2,1},{3,2},{4,3},{5,4},{6,5},{7,6},{8,15},{9,8},{10,9... | collective-permute-start | bytes 1179656 | tf_op jit(solution)/shard_map/ppermute | solution.py:290
  30.1 23.1 %collective-permute-start.9 = (bf16[256,1536]{1,0:T(8,128)(2,1)}, bf16[256,1536]{1,0:T(8,128)(2,1)}, u32[]{:S(2)}, u32[]{:S(2)}) collective-permute-start(bf16[256,1536]{1,0:T(8,128)(2,1)} %pad_maximum_fusion.1), channel_id=1, source_target_pairs={{0,8},{8,32},{16,56},{24,16},{32,40},{40,0},{48,24},{56,48},{1,9},... | collective-permute-start | bytes 2359304 | tf_op jit(solution)/shard_map/ppermute | solution.py:291
  32.6 19.5 %collective-permute-start.2 = (bf16[16,512]{1,0:T(8,128)(2,1)S(1)}, bf16[16,512]{1,0:T(8,128)(2,1)S(1)}, u32[]{:S(2)}, u32[]{:S(2)}) collective-permute-start(bf16[16,512]{1,0:T(8,128)(2,1)S(1)} %dynamic-slice_bitcast_fusion), channel_id=1, source_target_pairs={{16,32},{48,64},{80,96},{112,128},{144,160},{176,192},{208,224},{3... | collective-permute-start | bytes 49160 | tf_op jit(solution)/shard_map/ppermute | solution.py:321
  37.6 0.8 copy-start.6
  41.6 11.6 %copy-start.3 = (bf16[128,1536]{1,0:T(8,128)(2,1)}, bf16[128,1536]{1,0:T(8,128)(2,1)S(1)}, u32[]{:S(2)}) copy-start(bf16[128,1536]{1,0:T(8,128)(2,1)S(1)} %collective-permute-done.5.refs_6_) | copy-start | bytes 1179652
  41.6 15.7 %collective-permute-start.7 = (bf16[128,1536]{1,0:T(8,128)(2,1)S(1)}, bf16[128,1536]{1,0:T(8,128)(2,1)S(1)}, u32[]{:S(2)}, u32[]{:S(2)}) collective-permute-start(bf16[128,1536]{1,0:T(8,128)(2,1)S(1)} %collective-permute-done.4.refs_5_), channel_id=1, source_target_pairs={{0,1},{1,2},{2,3},{3,4},{4,5},{5,6},{6,7},{7,0},{8,9},{9,10},{10,1... | collective-permute-start | bytes 1179656 | tf_op jit(solution)/shard_map/ppermute | solution.py:290
  44.3 15.2 %collective-permute-start.8 = (bf16[128,1536]{1,0:T(8,128)(2,1)S(1)}, bf16[128,1536]{1,0:T(8,128)(2,1)S(1)}, u32[]{:S(2)}, u32[]{:S(2)}) collective-permute-start(bf16[128,1536]{1,0:T(8,128)(2,1)S(1)} %collective-permute-done.5.refs_6_), channel_id=1, source_target_pairs={{0,7},{1,0},{2,1},{3,2},{4,3},{5,4},{6,5},{7,6},{8,15},{9,8},{10,9... | collective-permute-start | bytes 1179656 | tf_op jit(solution)/shard_map/ppermute | solution.py:290
  52.2 15.2 %collective-permute-start.3 = (bf16[784,512]{1,0:T(8,128)(2,1)S(1)}, bf16[784,512]{1,0:T(8,128)(2,1)S(1)}, u32[]{:S(2)}, u32[]{:S(2)}) collective-permute-start(bf16[784,512]{1,0:T(8,128)(2,1)S(1)} %pad_maximum_fusion), channel_id=1, source_target_pairs={{0,16},{16,0},{1,17},{17,1},{2,18},{18,2},{3,19},{19,3},{4,20},{20... | collective-permute-start | bytes 2408456 | tf_op jit(solution)/shard_map/ppermute | solution.py:292
  53.2 26.5 %collective-permute-start.10 = (bf16[256,1536]{1,0:T(8,128)(2,1)}, bf16[256,1536]{1,0:T(8,128)(2,1)}, u32[]{:S(2)}, u32[]{:S(2)}) collective-permute-start(bf16[256,1536]{1,0:T(8,128)(2,1)} %pad_maximum_fusion.2), channel_id=1, source_target_pairs={{0,8},{8,32},{16,56},{24,16},{32,40},{40,0},{48,24},{56,48},{1,9},... | collective-permute-start | bytes 2359304 | tf_op jit(solution)/shard_map/ppermute | solution.py:291
  60.4 27.7 %copy-start.2 = (bf16[128,1536]{1,0:T(8,128)(2,1)S(1)}, bf16[128,1536]{1,0:T(8,128)(2,1)}, u32[]{:S(2)}) copy-start(bf16[128,1536]{1,0:T(8,128)(2,1)} %front_pack.1.refs_9_) | copy-start | bytes 1179652
  60.4 27.6 %collective-permute-start.11 = (bf16[256,1536]{1,0:T(8,128)(2,1)}, bf16[256,1536]{1,0:T(8,128)(2,1)}, u32[]{:S(2)}, u32[]{:S(2)}) collective-permute-start(bf16[256,1536]{1,0:T(8,128)(2,1)} %pad_maximum_fusion.3), channel_id=1, source_target_pairs={{0,8},{8,32},{16,56},{24,16},{32,40},{40,0},{48,24},{56,48},{1,9},... | collective-permute-start | bytes 2359304 | tf_op jit(solution)/shard_map/ppermute | solution.py:291
  63.6 16.2 %collective-permute-start.12 = (bf16[128,1536]{1,0:T(8,128)(2,1)}, bf16[128,1536]{1,0:T(8,128)(2,1)}, u32[]{:S(2)}, u32[]{:S(2)}) collective-permute-start(bf16[128,1536]{1,0:T(8,128)(2,1)} %broadcast_select_fusion), channel_id=1, source_target_pairs={{0,9},{1,10},{2,11},{3,12},{4,13},{5,14},{6,15},{7,8},{8,33},{9,34... | collective-permute-start | bytes 1179656 | tf_op jit(solution)/shard_map/ppermute | solution.py:347
  66.1 6.3 %collective-permute-start.13 = (bf16[64,1536]{1,0:T(8,128)(2,1)}, bf16[64,1536]{1,0:T(8,128)(2,1)}, u32[]{:S(2)}, u32[]{:S(2)}) collective-permute-start(bf16[64,1536]{1,0:T(8,128)(2,1)} %slice.6), channel_id=1, source_target_pairs={{0,1},{1,2},{2,3},{3,4},{4,5},{5,6},{6,7},{7,0},{8,9},{9,10},{10,1... | collective-permute-start | bytes 589832 | tf_op jit(solution)/shard_map/ppermute | solution.py:290
  67.3 1.0 copy-start.13
  68.3 11.4 %collective-permute-start.14 = (bf16[64,1536]{1,0:T(8,128)(2,1)}, bf16[64,1536]{1,0:T(8,128)(2,1)}, u32[]{:S(2)}, u32[]{:S(2)}) collective-permute-start(bf16[64,1536]{1,0:T(8,128)(2,1)} %slice.7), channel_id=1, source_target_pairs={{0,7},{1,0},{2,1},{3,2},{4,3},{5,4},{6,5},{7,6},{8,15},{9,8},{10,9... | collective-permute-start | bytes 589832 | tf_op jit(solution)/shard_map/ppermute | solution.py:290
  88.1 1.0 copy-start.4
  89.1 1.0 copy-start.7
  122.9 3.1 %collective-permute-start.15 = (bf16[768,768]{1,0:T(8,128)(2,1)}, bf16[768,768]{1,0:T(8,128)(2,1)S(1)}, u32[]{:S(2)}, u32[]{:S(2)}) collective-permute-start(bf16[768,768]{1,0:T(8,128)(2,1)} %get-tuple-element.43), channel_id=1, source_target_pairs={{0,16},{16,0},{1,17},{17,1},{2,18},{18,2},{3,19},{19,3},{4,20},{20... | collective-permute-start | bytes 3538952 | tf_op jit(solution)/shard_map/ppermute | solution.py:292
  126.1 1.1 copy-start.12
Sparse Core Ops, SparseCore 0:
  9.2 77.0 all-gather.1

commit v4 on v3

--- a/solution.py
+++ b/solution.py
@@ -377,7 +377,7 @@
             pltpu.SemaphoreType.DMA((n_in,)),
             pltpu.SemaphoreType.DMA((3,)),
         ],
-        compiler_params=pltpu.CompilerParams(vmem_limit_bytes=48 << 20),
+        compiler_params=pltpu.CompilerParams(vmem_limit_bytes=60 << 20),
         cost_estimate=pl.CostEstimate(flops=10_000_000_000, bytes_accessed=12 << 20, transcendentals=0),
         name="front",
     )(meta, ids, starts, own, halo, recv, *blocks, gain, taps, scale, ids_col)
@@ -387,7 +387,7 @@
     out = pl.pallas_call(
         back_kernel,
         out_shape=jax.ShapeDtypeStruct((span, width), bf),
-        in_specs=[SM] + [ANY] * 4,
+        in_specs=[SM] + [ANY] * 2 + [VM] + [ANY],
         out_specs=ANY,
         scratch_shapes=[
             pltpu.VMEM((span, width), bf),

time: 144 us -> 141 us (0.979); the launches traced: 143 us -> 139 us
  local copies, waits for them, and re-layouts: 10.2 us -> 7.32 us
  Pallas kernels: 43.9 us -> 41.9 us
    unnamed x28 -> x34, local copies, waits for them, and re-layouts: 5.78 us -> 3.03 us
    ppermute x8, waiting for transfers between devices: 24 us -> 26.8 us  [on_device(): zshift = lambda a, s: lax.ppermute(a, 'z', cyc(8, s))]
    pallas_call x1, Pallas kernels: 32.8 us -> 30.5 us  [on_device(): pl.pallas_call(functools.partial(front_kernel, places), out_shape=[jax.Sh...]
    concatenate x3, other arithmetic: 2.82 us -> 1.27 us  [on_device(): crossed.append(cross(jnp.concatenate([p, m])))]
  transfers between devices with their start and end apart: 17 -> 17, of which waited for: 10 -> 10; matrix products, arithmetic and copies ran while one was open for 6% -> 5% of each run, Pallas kernels for 24% -> 23%
where the time goes in v4:
time: 141 us; the launch traced here: 139 us
  waiting for transfers between devices  43.7 us (31%)
  Pallas kernels  41.9 us (30%)
  starting transfers between devices  29 us (21%)
  between operations  13.7 us (10%)
  local copies, waits for them, and re-layouts  7.32 us (5%)
  other arithmetic  2.97 us (2%)
    pallas_call x1, Pallas kernels, on_device(): pl.pallas_call(functools.partial(front_kernel, places), out_shape=[jax.Sh...  30.5 us
    ppermute x8, waiting for transfers between devices, on_device(): zshift = lambda a, s: lax.ppermute(a, 'z', cyc(8, s))  26.8 us
    ppermute x8, starting transfers between devices, on_device(): zshift = lambda a, s: lax.ppermute(a, 'z', cyc(8, s))  14.5 us
    pallas_call x1, Pallas kernels, on_device(): pl.pallas_call(back_kernel, out_shape=jax.ShapeDtypeStruct((span, width),...  9.46 us
    ppermute x4, starting transfers between devices, on_device(): cross = lambda a: lax.ppermute(a, ('xh', 'c', 'xl'), CROSS)  7.64 us
    ppermute x4, waiting for transfers between devices, on_device(): cross = lambda a: lax.ppermute(a, ('xh', 'c', 'xl'), CROSS)  7.36 us
    ppermute x1, waiting for transfers between devices, on_device(): halo = lax.ppermute(edge, TM, out_pairs + [(b, a) for a, b in out_pairs])  6.51 us
    ppermute x1, starting transfers between devices, on_device(): halo = lax.ppermute(edge, TM, out_pairs + [(b, a) for a, b in out_pairs])  5.03 us
  transfers between devices with their start and end apart: 17, of which 10 were waited for; matrix products, arithmetic and copies ran while one was open for 5% of the time, Pallas kernels for 23%

profile of v4, /device:TPU:1, one launch (start us, length us, event | category | flops | bytes accessed | tf_op | source)
XLA Modules:
  0.0 138.6 jit_solution(14439918769955472464)
XLA Ops:
  6.6 0.9 copy-done
  7.5 0.7 constant_dynamic-slice_fusion
  8.2 1.9 %front_pack.1.refs_9_ = bf16[128,1536]{1,0:T(8,128)(2,1)} custom-call(bf16[32,1536]{1,0:T(8,128)(2,1)} %sub.15, bf16[96,3072]{1,0:T(8,128)(2,1)} %first.1), custom_call_target="tpu_custom_call" | custom-call | tf_op jit(solution)/shard_map/front_pack/pallas_call | solution.py:296
  10.1 2.5 %collective-permute-start = (bf16[128,1536]{1,0:T(8,128)(2,1)}, bf16[128,1536]{1,0:T(8,128)(2,1)S(1)}, u32[]{:S(2)}, u32[]{:S(2)}) collective-permute-start(bf16[128,1536]{1,0:T(8,128)(2,1)} %front_pack.1.refs_9_), channel_id=1, source_target_pairs={{0,1},{1,2},{2,3},{3,4},{4,5},{5,6},{6,7},{7,0},{8,9},{9,10},{10,1... | collective-permute-start | bytes 1179656 | tf_op jit(solution)/shard_map/ppermute | solution.py:290
  12.6 3.9 %collective-permute-start.1 = (bf16[128,1536]{1,0:T(8,128)(2,1)}, bf16[128,1536]{1,0:T(8,128)(2,1)S(1)}, u32[]{:S(2)}, u32[]{:S(2)}) collective-permute-start(bf16[128,1536]{1,0:T(8,128)(2,1)} %front_pack.1.refs_9_), channel_id=1, source_target_pairs={{0,7},{1,0},{2,1},{3,2},{4,3},{5,4},{6,5},{7,6},{8,15},{9,8},{10,9... | collective-permute-start | bytes 1179656 | tf_op jit(solution)/shard_map/ppermute | solution.py:290
  16.5 2.5 %collective-permute-start.6 = (bf16[128,1536]{1,0:T(8,128)(2,1)}, bf16[128,1536]{1,0:T(8,128)(2,1)S(1)}, u32[]{:S(2)}, u32[]{:S(2)}) collective-permute-start(bf16[128,1536]{1,0:T(8,128)(2,1)} %front_pack.1.refs_9_), channel_id=1, source_target_pairs={{0,8},{8,32},{16,56},{24,16},{32,40},{40,0},{48,24},{56,48},{1,9},... | collective-permute-start | bytes 1179656 | tf_op jit(solution)/shard_map/ppermute | solution.py:291
  20.8 0.6 add_subtract_fusion.starts
  21.4 0.6 pad_add_fusion.meta
  22.1 3.5 %collective-permute-done.refs_3_ = bf16[128,1536]{1,0:T(8,128)(2,1)S(1)} collective-permute-done((bf16[128,1536]{1,0:T(8,128)(2,1)}, bf16[128,1536]{1,0:T(8,128)(2,1)S(1)}, u32[]{:S(2)}, u32[]{:S(2)}) %collective-permute-start) | collective-permute-done | bytes 393248 | tf_op jit(solution)/shard_map/ppermute | solution.py:290
  25.6 1.0 broadcast_in_dim.2.refs_18_
  26.6 2.7 %collective-permute-start.5 = (bf16[128,1536]{1,0:T(8,128)(2,1)S(1)}, bf16[128,1536]{1,0:T(8,128)(2,1)}, u32[]{:S(2)}, u32[]{:S(2)}) collective-permute-start(bf16[128,1536]{1,0:T(8,128)(2,1)S(1)} %collective-permute-done.1.refs_4_), channel_id=1, source_target_pairs={{0,7},{1,0},{2,1},{3,2},{4,3},{5,4},{6,5},{7,6},{8,15},{9,8},{10,9... | collective-permute-start | bytes 1179656 | tf_op jit(solution)/shard_map/ppermute | solution.py:290
  29.3 2.6 %collective-permute-start.9 = (bf16[256,1536]{1,0:T(8,128)(2,1)S(1)}, bf16[256,1536]{1,0:T(8,128)(2,1)}, u32[]{:S(2)}, u32[]{:S(2)}) collective-permute-start(bf16[256,1536]{1,0:T(8,128)(2,1)S(1)} %pad_maximum_fusion.1), channel_id=1, source_target_pairs={{0,8},{8,32},{16,56},{24,16},{32,40},{40,0},{48,24},{56,48},{1,9},... | collective-permute-start | bytes 2359304 | tf_op jit(solution)/shard_map/ppermute | solution.py:291
  31.9 5.0 %collective-permute-start.2 = (bf16[16,512]{1,0:T(8,128)(2,1)S(1)}, bf16[16,512]{1,0:T(8,128)(2,1)S(1)}, u32[]{:S(2)}, u32[]{:S(2)}) collective-permute-start(bf16[16,512]{1,0:T(8,128)(2,1)S(1)} %dynamic-slice_bitcast_fusion), channel_id=1, source_target_pairs={{16,32},{48,64},{80,96},{112,128},{144,160},{176,192},{208,224},{3... | collective-permute-start | bytes 49160 | tf_op jit(solution)/shard_map/ppermute | solution.py:321
  36.9 1.9 %collective-permute-done.4.refs_5_ = bf16[128,1536]{1,0:T(8,128)(2,1)} collective-permute-done((bf16[128,1536]{1,0:T(8,128)(2,1)S(1)}, bf16[128,1536]{1,0:T(8,128)(2,1)}, u32[]{:S(2)}, u32[]{:S(2)}) %collective-permute-start.4) | collective-permute-done | bytes 393248 | tf_op jit(solution)/shard_map/ppermute | solution.py:290
  38.8 3.0 %collective-permute-done.5.refs_6_ = bf16[128,1536]{1,0:T(8,128)(2,1)} collective-permute-done((bf16[128,1536]{1,0:T(8,128)(2,1)S(1)}, bf16[128,1536]{1,0:T(8,128)(2,1)}, u32[]{:S(2)}, u32[]{:S(2)}) %collective-permute-start.5) | collective-permute-done | bytes 393248 | tf_op jit(solution)/shard_map/ppermute | solution.py:290
  41.8 2.6 %collective-permute-start.7 = (bf16[128,1536]{1,0:T(8,128)(2,1)}, bf16[128,1536]{1,0:T(8,128)(2,1)S(1)}, u32[]{:S(2)}, u32[]{:S(2)}) collective-permute-start(bf16[128,1536]{1,0:T(8,128)(2,1)} %collective-permute-done.4.refs_5_), channel_id=1, source_target_pairs={{0,1},{1,2},{2,3},{3,4},{4,5},{5,6},{6,7},{7,0},{8,9},{9,10},{10,1... | collective-permute-start | bytes 1179656 | tf_op jit(solution)/shard_map/ppermute | solution.py:290
  44.5 6.5 %collective-permute-done.2.refs_1_ = bf16[16,512]{1,0:T(8,128)(2,1)S(1)} collective-permute-done((bf16[16,512]{1,0:T(8,128)(2,1)S(1)}, bf16[16,512]{1,0:T(8,128)(2,1)S(1)}, u32[]{:S(2)}, u32[]{:S(2)}) %collective-permute-start.2) | collective-permute-done | bytes 16416 | tf_op jit(solution)/shard_map/ppermute | solution.py:321
  51.2 1.2 pad_maximum_fusion.2
  52.5 5.8 %collective-permute-done.7.refs_7_ = bf16[128,1536]{1,0:T(8,128)(2,1)S(1)} collective-permute-done((bf16[128,1536]{1,0:T(8,128)(2,1)}, bf16[128,1536]{1,0:T(8,128)(2,1)S(1)}, u32[]{:S(2)}, u32[]{:S(2)}) %collective-permute-start.7) | collective-permute-done | bytes 393248 | tf_op jit(solution)/shard_map/ppermute | solution.py:290
  58.2 2.1 %collective-permute-done.8.refs_8_ = bf16[128,1536]{1,0:T(8,128)(2,1)S(1)} collective-permute-done((bf16[128,1536]{1,0:T(8,128)(2,1)}, bf16[128,1536]{1,0:T(8,128)(2,1)S(1)}, u32[]{:S(2)}, u32[]{:S(2)}) %collective-permute-start.8) | collective-permute-done | bytes 393248 | tf_op jit(solution)/shard_map/ppermute | solution.py:290
  60.4 2.5 %collective-permute-start.11 = (bf16[256,1536]{1,0:T(8,128)(2,1)S(1)}, bf16[256,1536]{1,0:T(8,128)(2,1)}, u32[]{:S(2)}, u32[]{:S(2)}) collective-permute-start(bf16[256,1536]{1,0:T(8,128)(2,1)S(1)} %pad_maximum_fusion.3), channel_id=1, source_target_pairs={{0,8},{8,32},{16,56},{24,16},{32,40},{40,0},{48,24},{56,48},{1,9},... | collective-permute-start | bytes 2359304 | tf_op jit(solution)/shard_map/ppermute | solution.py:291
  63.0 1.6 %collective-permute-start.12 = (bf16[128,1536]{1,0:T(8,128)(2,1)S(1)}, bf16[128,1536]{1,0:T(8,128)(2,1)}, u32[]{:S(2)}, u32[]{:S(2)}) collective-permute-start(bf16[128,1536]{1,0:T(8,128)(2,1)S(1)} %broadcast_select_fusion), channel_id=1, source_target_pairs={{0,9},{1,10},{2,11},{3,12},{4,13},{5,14},{6,15},{7,8},{8,33},{9,34... | collective-permute-start | bytes 1179656 | tf_op jit(solution)/shard_map/ppermute | solution.py:347
  65.2 1.0 copy-done.13
  66.2 2.2 %collective-permute-start.14 = (bf16[64,1536]{1,0:T(8,128)(2,1)S(1)}, bf16[64,1536]{1,0:T(8,128)(2,1)S(1)}, u32[]{:S(2)}, u32[]{:S(2)}) collective-permute-start(bf16[64,1536]{1,0:T(8,128)(2,1)S(1)} %slice.7), channel_id=1, source_target_pairs={{0,7},{1,0},{2,1},{3,2},{4,3},{5,4},{6,5},{7,6},{8,15},{9,8},{10,9... | collective-permute-start | bytes 589832 | tf_op jit(solution)/shard_map/ppermute | solution.py:290
  68.4 1.2 copy.16.refs_20_
  69.6 1.3 collective-permute-done.13.refs_15_
  70.8 9.3 %collective-permute-done.14.refs_16_ = bf16[64,1536]{1,0:T(8,128)(2,1)S(1)} collective-permute-done((bf16[64,1536]{1,0:T(8,128)(2,1)S(1)}, bf16[64,1536]{1,0:T(8,128)(2,1)S(1)}, u32[]{:S(2)}, u32[]{:S(2)}) %collective-permute-start.14) | collective-permute-done | bytes 196640 | tf_op jit(solution)/shard_map/ppermute | solution.py:290
  80.1 7.4 %collective-permute-done.11.refs_13_ = bf16[256,1536]{1,0:T(8,128)(2,1)} collective-permute-done((bf16[256,1536]{1,0:T(8,128)(2,1)S(1)}, bf16[256,1536]{1,0:T(8,128)(2,1)}, u32[]{:S(2)}, u32[]{:S(2)}) %collective-permute-start.11) | collective-permute-done | bytes 786464 | tf_op jit(solution)/shard_map/ppermute | solution.py:291
  87.5 30.5 %front.1 = (bf16[768,1536]{1,0:T(8,128)(2,1)}, bf16[768,768]{1,0:T(8,128)(2,1)}, bf16[768,768]{1,0:T(8,128)(2,1)}) custom-call(s32[3]{0:T(128)} %pad_add_fusion.meta, s32[1568]{0:T(1024)} %copy-done.6, s32[65]{0:T(128)} %add_subtract_fusion.starts, bf16[768,512]{1,0:T(8,128)(2,1)} %bitcast.10, bf16[16,512]{1,0:T(8,128)(2,1)} %copy-done.8, ...), custom_call_target="tpu_custom_call" | custom-call | flops 10000000000 | bytes 12582912 | tf_op jit(solution)/shard_map/front/pallas_call | solution.py:358
  118.1 3.0 %collective-permute-done.15.theirs = bf16[768,768]{1,0:T(8,128)(2,1)S(1)} collective-permute-done((bf16[768,768]{1,0:T(8,128)(2,1)}, bf16[768,768]{1,0:T(8,128)(2,1)S(1)}, u32[]{:S(2)}, u32[]{:S(2)}) %collective-permute-start.15) | collective-permute-done | bytes 1179680 | tf_op jit(solution)/shard_map/ppermute | solution.py:292
  121.2 1.1 copy-done.12
  122.3 9.5 %back.1 = bf16[768,1536]{1,0:T(8,128)(2,1)} custom-call(s32[3]{0:T(128)} %pad_add_fusion.meta, bf16[768,1536]{1,0:T(8,128)(2,1)} %get-tuple-element.40.sub, bf16[768,768]{1,0:T(8,128)(2,1)} %get-tuple-element.41.mine, bf16[768,768]{1,0:T(8,128)(2,1)} %copy-done.12, bf16[16,2,96,768]{3,2,1,0:T(8,128)(2,1)} %bitcast.14), custom_call_target="tpu_custom_call" | custom-call | flops 3600000000 | bytes 12582912 | tf_op jit(solution)/shard_map/back/pallas_call | solution.py:387
  (65 shorter events, 3.1 us)
Async XLA Ops:
  6.5 12.4 %copy-start.7 = (bf16[32,1536]{1,0:T(8,128)(2,1)S(1)}, bf16[32,1536]{1,0:T(8,128)(2,1)}, u32[]{:S(2)}) copy-start(bf16[32,1536]{1,0:T(8,128)(2,1)} %param.13) | copy-start | bytes 294916
  6.5 12.5 %copy-start.10 = (f32[1536]{0:T(1024)S(1)}, f32[1536]{0:T(1024)}, u32[]{:S(2)}) copy-start(f32[1536]{0:T(1024)} %param.14) | copy-start | bytes 18436
  6.5 13.2 %copy-start.11 = (s32[1,64]{1,0:T(1,128)S(1)}, s32[1,64]{1,0:T(1,128)}, u32[]{:S(2)}) copy-start(s32[1,64]{1,0:T(1,128)} %param.9) | copy-start | bytes 772
  6.5 13.7 %copy-start.9 = (f32[1536]{0:T(1024)S(1)}, f32[1536]{0:T(1024)}, u32[]{:S(2)}) copy-start(f32[1536]{0:T(1024)} %param.11) | copy-start | bytes 18436
  6.5 111.5 %all-gather.2.cloned.1.call-start = ((), (), s32[]{:S(2)}) async-start(), calls=%async_computation | async-start | bytes 4866048 | tf_op jit(solution)/shard_map/all_gather | solution.py:352
  10.1 15.5 %collective-permute-start = (bf16[128,1536]{1,0:T(8,128)(2,1)}, bf16[128,1536]{1,0:T(8,128)(2,1)S(1)}, u32[]{:S(2)}, u32[]{:S(2)}) collective-permute-start(bf16[128,1536]{1,0:T(8,128)(2,1)} %front_pack.1.refs_9_), channel_id=1, source_target_pairs={{0,1},{1,2},{2,3},{3,4},{4,5},{5,6},{6,7},{7,0},{8,9},{9,10},{10,1... | collective-permute-start | bytes 1179656 | tf_op jit(solution)/shard_map/ppermute | solution.py:290
  12.6 13.0 %collective-permute-start.1 = (bf16[128,1536]{1,0:T(8,128)(2,1)}, bf16[128,1536]{1,0:T(8,128)(2,1)S(1)}, u32[]{:S(2)}, u32[]{:S(2)}) collective-permute-start(bf16[128,1536]{1,0:T(8,128)(2,1)} %front_pack.1.refs_9_), channel_id=1, source_target_pairs={{0,7},{1,0},{2,1},{3,2},{4,3},{5,4},{6,5},{7,6},{8,15},{9,8},{10,9... | collective-permute-start | bytes 1179656 | tf_op jit(solution)/shard_map/ppermute | solution.py:290
  16.5 20.4 %collective-permute-start.6 = (bf16[128,1536]{1,0:T(8,128)(2,1)}, bf16[128,1536]{1,0:T(8,128)(2,1)S(1)}, u32[]{:S(2)}, u32[]{:S(2)}) collective-permute-start(bf16[128,1536]{1,0:T(8,128)(2,1)} %front_pack.1.refs_9_), channel_id=1, source_target_pairs={{0,8},{8,32},{16,56},{24,16},{32,40},{40,0},{48,24},{56,48},{1,9},... | collective-permute-start | bytes 1179656 | tf_op jit(solution)/shard_map/ppermute | solution.py:291
  19.0 12.8 %copy-start.3 = (bf16[1,768,512]{2,1,0:T(8,128)(2,1)S(1)}, bf16[1,768,512]{2,1,0:T(8,128)(2,1)}, u32[]{:S(2)}) copy-start(bf16[1,768,512]{2,1,0:T(8,128)(2,1)} %param.8) | copy-start | bytes 2359300
  20.2 30.9 %copy-start.6 = (s32[1568]{0:T(1024)}, s32[1568]{0:T(1024)S(1)}, u32[]{:S(2)}) copy-start(s32[1568]{0:T(1024)S(1)} %convert_reduce_fusion.ids_s) | copy-start | bytes 18820
  25.6 25.5 %copy-start.4 = (bf16[128,1536]{1,0:T(8,128)(2,1)}, bf16[128,1536]{1,0:T(8,128)(2,1)S(1)}, u32[]{:S(2)}) copy-start(bf16[128,1536]{1,0:T(8,128)(2,1)S(1)} %collective-permute-done.refs_3_) | copy-start | bytes 1179652
  25.6 25.5 %copy-start.5 = (bf16[128,1536]{1,0:T(8,128)(2,1)}, bf16[128,1536]{1,0:T(8,128)(2,1)S(1)}, u32[]{:S(2)}) copy-start(bf16[128,1536]{1,0:T(8,128)(2,1)S(1)} %collective-permute-done.1.refs_4_) | copy-start | bytes 1179652
  26.6 12.2 %collective-permute-start.4 = (bf16[128,1536]{1,0:T(8,128)(2,1)S(1)}, bf16[128,1536]{1,0:T(8,128)(2,1)}, u32[]{:S(2)}, u32[]{:S(2)}) collective-permute-start(bf16[128,1536]{1,0:T(8,128)(2,1)S(1)} %collective-permute-done.refs_3_), channel_id=1, source_target_pairs={{0,1},{1,2},{2,3},{3,4},{4,5},{5,6},{6,7},{7,0},{8,9},{9,10},{10,1... | collective-permute-start | bytes 1179656 | tf_op jit(solution)/shard_map/ppermute | solution.py:290
  26.6 15.2 %collective-permute-start.5 = (bf16[128,1536]{1,0:T(8,128)(2,1)S(1)}, bf16[128,1536]{1,0:T(8,128)(2,1)}, u32[]{:S(2)}, u32[]{:S(2)}) collective-permute-start(bf16[128,1536]{1,0:T(8,128)(2,1)S(1)} %collective-permute-done.1.refs_4_), channel_id=1, source_target_pairs={{0,7},{1,0},{2,1},{3,2},{4,3},{5,4},{6,5},{7,6},{8,15},{9,8},{10,9... | collective-permute-start | bytes 1179656 | tf_op jit(solution)/shard_map/ppermute | solution.py:290
  29.3 23.2 %collective-permute-start.9 = (bf16[256,1536]{1,0:T(8,128)(2,1)S(1)}, bf16[256,1536]{1,0:T(8,128)(2,1)}, u32[]{:S(2)}, u32[]{:S(2)}) collective-permute-start(bf16[256,1536]{1,0:T(8,128)(2,1)S(1)} %pad_maximum_fusion.1), channel_id=1, source_target_pairs={{0,8},{8,32},{16,56},{24,16},{32,40},{40,0},{48,24},{56,48},{1,9},... | collective-permute-start | bytes 2359304 | tf_op jit(solution)/shard_map/ppermute | solution.py:291
  31.9 19.1 %collective-permute-start.2 = (bf16[16,512]{1,0:T(8,128)(2,1)S(1)}, bf16[16,512]{1,0:T(8,128)(2,1)S(1)}, u32[]{:S(2)}, u32[]{:S(2)}) collective-permute-start(bf16[16,512]{1,0:T(8,128)(2,1)S(1)} %dynamic-slice_bitcast_fusion), channel_id=1, source_target_pairs={{16,32},{48,64},{80,96},{112,128},{144,160},{176,192},{208,224},{3... | collective-permute-start | bytes 49160 | tf_op jit(solution)/shard_map/ppermute | solution.py:321
  36.9 1.9 %copy-start.14 = (bf16[128,1536]{1,0:T(8,128)(2,1)}, bf16[128,1536]{1,0:T(8,128)(2,1)S(1)}, u32[]{:S(2)}) copy-start(bf16[128,1536]{1,0:T(8,128)(2,1)S(1)} %collective-permute-done.6.refs_10_) | copy-start | bytes 1179652
  41.8 16.4 %collective-permute-start.7 = (bf16[128,1536]{1,0:T(8,128)(2,1)}, bf16[128,1536]{1,0:T(8,128)(2,1)S(1)}, u32[]{:S(2)}, u32[]{:S(2)}) collective-permute-start(bf16[128,1536]{1,0:T(8,128)(2,1)} %collective-permute-done.4.refs_5_), channel_id=1, source_target_pairs={{0,1},{1,2},{2,3},{3,4},{4,5},{5,6},{6,7},{7,0},{8,9},{9,10},{10,1... | collective-permute-start | bytes 1179656 | tf_op jit(solution)/shard_map/ppermute | solution.py:290
  44.4 15.9 %collective-permute-start.8 = (bf16[128,1536]{1,0:T(8,128)(2,1)}, bf16[128,1536]{1,0:T(8,128)(2,1)S(1)}, u32[]{:S(2)}, u32[]{:S(2)}) collective-permute-start(bf16[128,1536]{1,0:T(8,128)(2,1)} %collective-permute-done.5.refs_6_), channel_id=1, source_target_pairs={{0,7},{1,0},{2,1},{3,2},{4,3},{5,4},{6,5},{7,6},{8,15},{9,8},{10,9... | collective-permute-start | bytes 1179656 | tf_op jit(solution)/shard_map/ppermute | solution.py:290
  51.0 1.4 copy-start.8
  51.1 14.1 %collective-permute-start.3 = (bf16[784,512]{1,0:T(8,128)(2,1)S(1)}, bf16[784,512]{1,0:T(8,128)(2,1)S(1)}, u32[]{:S(2)}, u32[]{:S(2)}) collective-permute-start(bf16[784,512]{1,0:T(8,128)(2,1)S(1)} %pad_maximum_fusion), channel_id=1, source_target_pairs={{0,16},{16,0},{1,17},{17,1},{2,18},{18,2},{3,19},{19,3},{4,20},{20... | collective-permute-start | bytes 2408456 | tf_op jit(solution)/shard_map/ppermute | solution.py:292
  52.4 27.8 %collective-permute-start.10 = (bf16[256,1536]{1,0:T(8,128)(2,1)S(1)}, bf16[256,1536]{1,0:T(8,128)(2,1)}, u32[]{:S(2)}, u32[]{:S(2)}) collective-permute-start(bf16[256,1536]{1,0:T(8,128)(2,1)S(1)} %pad_maximum_fusion.2), channel_id=1, source_target_pairs={{0,8},{8,32},{16,56},{24,16},{32,40},{40,0},{48,24},{56,48},{1,9},... | collective-permute-start | bytes 2359304 | tf_op jit(solution)/shard_map/ppermute | solution.py:291
  58.2 6.4 %copy-start.1 = (bf16[128,1536]{1,0:T(8,128)(2,1)}, bf16[128,1536]{1,0:T(8,128)(2,1)S(1)}, u32[]{:S(2)}) copy-start(bf16[128,1536]{1,0:T(8,128)(2,1)S(1)} %collective-permute-done.7.refs_7_) | copy-start | bytes 1179652
  60.3 4.3 %copy-start.2 = (bf16[128,1536]{1,0:T(8,128)(2,1)}, bf16[128,1536]{1,0:T(8,128)(2,1)S(1)}, u32[]{:S(2)}) copy-start(bf16[128,1536]{1,0:T(8,128)(2,1)S(1)} %collective-permute-done.8.refs_8_) | copy-start | bytes 1179652
  60.4 27.1 %collective-permute-start.11 = (bf16[256,1536]{1,0:T(8,128)(2,1)S(1)}, bf16[256,1536]{1,0:T(8,128)(2,1)}, u32[]{:S(2)}, u32[]{:S(2)}) collective-permute-start(bf16[256,1536]{1,0:T(8,128)(2,1)S(1)} %pad_maximum_fusion.3), channel_id=1, source_target_pairs={{0,8},{8,32},{16,56},{24,16},{32,40},{40,0},{48,24},{56,48},{1,9},... | collective-permute-start | bytes 2359304 | tf_op jit(solution)/shard_map/ppermute | solution.py:291
  63.0 17.2 %collective-permute-start.12 = (bf16[128,1536]{1,0:T(8,128)(2,1)S(1)}, bf16[128,1536]{1,0:T(8,128)(2,1)}, u32[]{:S(2)}, u32[]{:S(2)}) collective-permute-start(bf16[128,1536]{1,0:T(8,128)(2,1)S(1)} %broadcast_select_fusion), channel_id=1, source_target_pairs={{0,9},{1,10},{2,11},{3,12},{4,13},{5,14},{6,15},{7,8},{8,33},{9,34... | collective-permute-start | bytes 1179656 | tf_op jit(solution)/shard_map/ppermute | solution.py:347
  64.6 6.2 %collective-permute-start.13 = (bf16[64,1536]{1,0:T(8,128)(2,1)S(1)}, bf16[64,1536]{1,0:T(8,128)(2,1)S(1)}, u32[]{:S(2)}, u32[]{:S(2)}) collective-permute-start(bf16[64,1536]{1,0:T(8,128)(2,1)S(1)} %slice.6), channel_id=1, source_target_pairs={{0,1},{1,2},{2,3},{3,4},{4,5},{5,6},{6,7},{7,0},{8,9},{9,10},{10,1... | collective-permute-start | bytes 589832 | tf_op jit(solution)/shard_map/ppermute | solution.py:290
  66.2 13.9 %collective-permute-start.14 = (bf16[64,1536]{1,0:T(8,128)(2,1)S(1)}, bf16[64,1536]{1,0:T(8,128)(2,1)S(1)}, u32[]{:S(2)}, u32[]{:S(2)}) collective-permute-start(bf16[64,1536]{1,0:T(8,128)(2,1)S(1)} %slice.7), channel_id=1, source_target_pairs={{0,7},{1,0},{2,1},{3,2},{4,3},{5,4},{6,5},{7,6},{8,15},{9,8},{10,9... | collective-permute-start | bytes 589832 | tf_op jit(solution)/shard_map/ppermute | solution.py:290
  70.8 16.6 %copy-start.15 = (bf16[64,1536]{1,0:T(8,128)(2,1)}, bf16[64,1536]{1,0:T(8,128)(2,1)S(1)}, u32[]{:S(2)}) copy-start(bf16[64,1536]{1,0:T(8,128)(2,1)S(1)} %collective-permute-done.13.refs_15_) | copy-start | bytes 589828
  80.1 7.4 %copy-start.16 = (bf16[64,1536]{1,0:T(8,128)(2,1)}, bf16[64,1536]{1,0:T(8,128)(2,1)S(1)}, u32[]{:S(2)}) copy-start(bf16[64,1536]{1,0:T(8,128)(2,1)S(1)} %collective-permute-done.14.refs_16_) | copy-start | bytes 589828
  118.0 3.1 %collective-permute-start.15 = (bf16[768,768]{1,0:T(8,128)(2,1)}, bf16[768,768]{1,0:T(8,128)(2,1)S(1)}, u32[]{:S(2)}, u32[]{:S(2)}) collective-permute-start(bf16[768,768]{1,0:T(8,128)(2,1)} %get-tuple-element.43), channel_id=1, source_target_pairs={{0,16},{16,0},{1,17},{17,1},{2,18},{18,2},{3,19},{19,3},{4,20},{20... | collective-permute-start | bytes 3538952 | tf_op jit(solution)/shard_map/ppermute | solution.py:292
  121.2 1.1 copy-start.12
  (2 other events, 1.9 us)
Sparse Core Ops, SparseCore 0:
  9.2 78.9 all-gather.1

commit v5 on v4

--- a/solution.py
+++ b/solution.py
@@ -238,38 +238,29 @@
     hw = mine.shape[1]
     here = pl.multiple_of(hw * c, 128)
     there = pl.multiple_of(hw * (1 - c), 128)
-    copies = [
-        pltpu.make_async_copy(
-            w.at[j, h],
-            w_v.at[pl.ds(j * w.shape[2], w.shape[2]), pl.ds(h * hw, hw)],
-            sem_in.at[2 * j + h],
-        )
-        for j in range(w.shape[0])
-        for h in range(2)
+    acts = [
+        pltpu.make_async_copy(mine, a_v.at[:, pl.ds(here, hw)], sem_in.at[0]),
+        pltpu.make_async_copy(theirs, a_v.at[:, pl.ds(there, hw)], sem_in.at[1]),
     ]
-    first = len(copies)
-    copies += [
-        pltpu.make_async_copy(mine, a_v.at[:, pl.ds(here, hw)], sem_in.at[first]),
-        pltpu.make_async_copy(theirs, a_v.at[:, pl.ds(there, hw)], sem_in.at[first + 1]),
-        pltpu.make_async_copy(sub, sub_v, sem_in.at[first + 2]),
-    ]
-    order = [cp for cp in copies[first:]] + [cp for h in range(2) for cp in copies[h:first:2]]
-    for cp in order:
+    parts = [pltpu.make_async_copy(w.at[:, h], w_v.at[h], sem_in.at[2 + h]) for h in range(2)]
+    base = pltpu.make_async_copy(sub, sub_v, sem_in.at[4])
+    for cp in [parts[0]] + acts + [base, parts[1]]:
         cp.start()
-    for cp in copies[first:]:
+    for cp in acts:
         cp.wait()
     nb = 256
     outs = []
     for h in range(2):
-        for cp in copies[h:first:2]:
-            cp.wait()
+        parts[h].wait()
+        if h == 0:
+            base.wait()
         for i in range(span // nb):
             r = pl.ds(i * nb, nb)
-            for n in range(h * hw, (h + 1) * hw, 256):
-                y = jnp.dot(a_v[r, :], w_v[:, n : n + 256], preferred_element_type=jnp.float32)
-                o_v[r, n : n + 256] = (sub_v[r, n : n + 256].astype(jnp.float32) + y).astype(
-                    jnp.bfloat16
-                )
+            for n in range(0, hw, 256):
+                rhs = w_v[h, :, :, n : n + 256].reshape(width, 256)
+                y = jnp.dot(a_v[r, :], rhs, preferred_element_type=jnp.float32)
+                to = slice(h * hw + n, h * hw + n + 256)
+                o_v[r, to] = (sub_v[r, to].astype(jnp.float32) + y).astype(jnp.bfloat16)
             cols = pl.ds(h * hw, hw)
             outs.append(pltpu.make_async_copy(o_v.at[r, cols], out.at[r, cols], sem_out.at[len(outs)]))
             outs[-1].start()
@@ -392,9 +383,9 @@
         scratch_shapes=[
             pltpu.VMEM((span, width), bf),
             pltpu.VMEM((span, width), bf),
-            pltpu.VMEM((width, width), bf),
+            pltpu.VMEM((2, 16, fr, hw), bf),
             pltpu.VMEM((span, width), bf),
-            pltpu.SemaphoreType.DMA((35,)),
+            pltpu.SemaphoreType.DMA((5,)),
             pltpu.SemaphoreType.DMA((6,)),
         ],
         compiler_params=pltpu.CompilerParams(vmem_limit_bytes=60 << 20),

time: 141 us -> 141 us (level)
  transfers between devices with their start and end apart: 17 -> 17, of which waited for: 10 -> 10; matrix products, arithmetic and copies ran while one was open for 5% -> 5% of each run, Pallas kernels for 23% -> 24%
where the time goes in v5:
time: 141 us; the launch traced here: 139 us
  waiting for transfers between devices  43.7 us (31%)
  Pallas kernels  42 us (30%)
  starting transfers between devices  29 us (21%)
  between operations  13.7 us (10%)
  local copies, waits for them, and re-layouts  7.32 us (5%)
  other arithmetic  2.97 us (2%)
    pallas_call x1, Pallas kernels, on_device(): pl.pallas_call(functools.partial(front_kernel, places), out_shape=[jax.Sh...  30.8 us
    ppermute x8, waiting for transfers between devices, on_device(): zshift = lambda a, s: lax.ppermute(a, 'z', cyc(8, s))  26.8 us
    ppermute x8, starting transfers between devices, on_device(): zshift = lambda a, s: lax.ppermute(a, 'z', cyc(8, s))  14.5 us
    pallas_call x1, Pallas kernels, on_device(): pl.pallas_call(back_kernel, out_shape=jax.ShapeDtypeStruct((span, width),...  9.27 us
    ppermute x4, starting transfers between devices, on_device(): cross = lambda a: lax.ppermute(a, ('xh', 'c', 'xl'), CROSS)  7.64 us
    ppermute x4, waiting for transfers between devices, on_device(): cross = lambda a: lax.ppermute(a, ('xh', 'c', 'xl'), CROSS)  7.36 us
    ppermute x1, waiting for transfers between devices, on_device(): halo = lax.ppermute(edge, TM, out_pairs + [(b, a) for a, b in out_pairs])  6.51 us
    ppermute x1, starting transfers between devices, on_device(): halo = lax.ppermute(edge, TM, out_pairs + [(b, a) for a, b in out_pairs])  5.03 us
  transfers between devices with their start and end apart: 17, of which 10 were waited for; matrix products, arithmetic and copies ran while one was open for 5% of the time, Pallas kernels for 24%

profile of v5, /device:TPU:1, one launch (start us, length us, event | category | flops | bytes accessed | tf_op | source)
XLA Modules:
  0.0 138.7 jit_solution(4500440557745073224)
XLA Ops:
  6.6 0.9 copy-done
  7.5 0.7 constant_dynamic-slice_fusion
  8.2 1.9 %front_pack.1.refs_9_ = bf16[128,1536]{1,0:T(8,128)(2,1)} custom-call(bf16[32,1536]{1,0:T(8,128)(2,1)} %sub.15, bf16[96,3072]{1,0:T(8,128)(2,1)} %first.1), custom_call_target="tpu_custom_call" | custom-call | tf_op jit(solution)/shard_map/front_pack/pallas_call | solution.py:287
  10.1 2.5 %collective-permute-start = (bf16[128,1536]{1,0:T(8,128)(2,1)}, bf16[128,1536]{1,0:T(8,128)(2,1)S(1)}, u32[]{:S(2)}, u32[]{:S(2)}) collective-permute-start(bf16[128,1536]{1,0:T(8,128)(2,1)} %front_pack.1.refs_9_), channel_id=1, source_target_pairs={{0,1},{1,2},{2,3},{3,4},{4,5},{5,6},{6,7},{7,0},{8,9},{9,10},{10,1... | collective-permute-start | bytes 1179656 | tf_op jit(solution)/shard_map/ppermute | solution.py:281
  12.6 3.9 %collective-permute-start.1 = (bf16[128,1536]{1,0:T(8,128)(2,1)}, bf16[128,1536]{1,0:T(8,128)(2,1)S(1)}, u32[]{:S(2)}, u32[]{:S(2)}) collective-permute-start(bf16[128,1536]{1,0:T(8,128)(2,1)} %front_pack.1.refs_9_), channel_id=1, source_target_pairs={{0,7},{1,0},{2,1},{3,2},{4,3},{5,4},{6,5},{7,6},{8,15},{9,8},{10,9... | collective-permute-start | bytes 1179656 | tf_op jit(solution)/shard_map/ppermute | solution.py:281
  16.5 2.5 %collective-permute-start.6 = (bf16[128,1536]{1,0:T(8,128)(2,1)}, bf16[128,1536]{1,0:T(8,128)(2,1)S(1)}, u32[]{:S(2)}, u32[]{:S(2)}) collective-permute-start(bf16[128,1536]{1,0:T(8,128)(2,1)} %front_pack.1.refs_9_), channel_id=1, source_target_pairs={{0,8},{8,32},{16,56},{24,16},{32,40},{40,0},{48,24},{56,48},{1,9},... | collective-permute-start | bytes 1179656 | tf_op jit(solution)/shard_map/ppermute | solution.py:282
  20.8 0.6 add_subtract_fusion.starts
  21.4 0.6 pad_add_fusion.meta
  22.1 3.5 %collective-permute-done.refs_3_ = bf16[128,1536]{1,0:T(8,128)(2,1)S(1)} collective-permute-done((bf16[128,1536]{1,0:T(8,128)(2,1)}, bf16[128,1536]{1,0:T(8,128)(2,1)S(1)}, u32[]{:S(2)}, u32[]{:S(2)}) %collective-permute-start) | collective-permute-done | bytes 393248 | tf_op jit(solution)/shard_map/ppermute | solution.py:281
  25.6 1.0 broadcast_in_dim.2.refs_18_
  26.6 2.7 %collective-permute-start.5 = (bf16[128,1536]{1,0:T(8,128)(2,1)S(1)}, bf16[128,1536]{1,0:T(8,128)(2,1)}, u32[]{:S(2)}, u32[]{:S(2)}) collective-permute-start(bf16[128,1536]{1,0:T(8,128)(2,1)S(1)} %collective-permute-done.1.refs_4_), channel_id=1, source_target_pairs={{0,7},{1,0},{2,1},{3,2},{4,3},{5,4},{6,5},{7,6},{8,15},{9,8},{10,9... | collective-permute-start | bytes 1179656 | tf_op jit(solution)/shard_map/ppermute | solution.py:281
  29.3 2.6 %collective-permute-start.9 = (bf16[256,1536]{1,0:T(8,128)(2,1)S(1)}, bf16[256,1536]{1,0:T(8,128)(2,1)}, u32[]{:S(2)}, u32[]{:S(2)}) collective-permute-start(bf16[256,1536]{1,0:T(8,128)(2,1)S(1)} %pad_maximum_fusion.1), channel_id=1, source_target_pairs={{0,8},{8,32},{16,56},{24,16},{32,40},{40,0},{48,24},{56,48},{1,9},... | collective-permute-start | bytes 2359304 | tf_op jit(solution)/shard_map/ppermute | solution.py:282
  31.9 5.0 %collective-permute-start.2 = (bf16[16,512]{1,0:T(8,128)(2,1)S(1)}, bf16[16,512]{1,0:T(8,128)(2,1)S(1)}, u32[]{:S(2)}, u32[]{:S(2)}) collective-permute-start(bf16[16,512]{1,0:T(8,128)(2,1)S(1)} %dynamic-slice_bitcast_fusion), channel_id=1, source_target_pairs={{16,32},{48,64},{80,96},{112,128},{144,160},{176,192},{208,224},{3... | collective-permute-start | bytes 49160 | tf_op jit(solution)/shard_map/ppermute | solution.py:312
  36.9 1.9 %collective-permute-done.4.refs_5_ = bf16[128,1536]{1,0:T(8,128)(2,1)} collective-permute-done((bf16[128,1536]{1,0:T(8,128)(2,1)S(1)}, bf16[128,1536]{1,0:T(8,128)(2,1)}, u32[]{:S(2)}, u32[]{:S(2)}) %collective-permute-start.4) | collective-permute-done | bytes 393248 | tf_op jit(solution)/shard_map/ppermute | solution.py:281
  38.8 3.0 %collective-permute-done.5.refs_6_ = bf16[128,1536]{1,0:T(8,128)(2,1)} collective-permute-done((bf16[128,1536]{1,0:T(8,128)(2,1)S(1)}, bf16[128,1536]{1,0:T(8,128)(2,1)}, u32[]{:S(2)}, u32[]{:S(2)}) %collective-permute-start.5) | collective-permute-done | bytes 393248 | tf_op jit(solution)/shard_map/ppermute | solution.py:281
  41.8 2.6 %collective-permute-start.7 = (bf16[128,1536]{1,0:T(8,128)(2,1)}, bf16[128,1536]{1,0:T(8,128)(2,1)S(1)}, u32[]{:S(2)}, u32[]{:S(2)}) collective-permute-start(bf16[128,1536]{1,0:T(8,128)(2,1)} %collective-permute-done.4.refs_5_), channel_id=1, source_target_pairs={{0,1},{1,2},{2,3},{3,4},{4,5},{5,6},{6,7},{7,0},{8,9},{9,10},{10,1... | collective-permute-start | bytes 1179656 | tf_op jit(solution)/shard_map/ppermute | solution.py:281
  44.5 6.5 %collective-permute-done.2.refs_1_ = bf16[16,512]{1,0:T(8,128)(2,1)S(1)} collective-permute-done((bf16[16,512]{1,0:T(8,128)(2,1)S(1)}, bf16[16,512]{1,0:T(8,128)(2,1)S(1)}, u32[]{:S(2)}, u32[]{:S(2)}) %collective-permute-start.2) | collective-permute-done | bytes 16416 | tf_op jit(solution)/shard_map/ppermute | solution.py:312
  51.2 1.2 pad_maximum_fusion.2
  52.5 5.8 %collective-permute-done.7.refs_7_ = bf16[128,1536]{1,0:T(8,128)(2,1)S(1)} collective-permute-done((bf16[128,1536]{1,0:T(8,128)(2,1)}, bf16[128,1536]{1,0:T(8,128)(2,1)S(1)}, u32[]{:S(2)}, u32[]{:S(2)}) %collective-permute-start.7) | collective-permute-done | bytes 393248 | tf_op jit(solution)/shard_map/ppermute | solution.py:281
  58.2 2.1 %collective-permute-done.8.refs_8_ = bf16[128,1536]{1,0:T(8,128)(2,1)S(1)} collective-permute-done((bf16[128,1536]{1,0:T(8,128)(2,1)}, bf16[128,1536]{1,0:T(8,128)(2,1)S(1)}, u32[]{:S(2)}, u32[]{:S(2)}) %collective-permute-start.8) | collective-permute-done | bytes 393248 | tf_op jit(solution)/shard_map/ppermute | solution.py:281
  60.4 2.5 %collective-permute-start.11 = (bf16[256,1536]{1,0:T(8,128)(2,1)S(1)}, bf16[256,1536]{1,0:T(8,128)(2,1)}, u32[]{:S(2)}, u32[]{:S(2)}) collective-permute-start(bf16[256,1536]{1,0:T(8,128)(2,1)S(1)} %pad_maximum_fusion.3), channel_id=1, source_target_pairs={{0,8},{8,32},{16,56},{24,16},{32,40},{40,0},{48,24},{56,48},{1,9},... | collective-permute-start | bytes 2359304 | tf_op jit(solution)/shard_map/ppermute | solution.py:282
  63.0 1.6 %collective-permute-start.12 = (bf16[128,1536]{1,0:T(8,128)(2,1)S(1)}, bf16[128,1536]{1,0:T(8,128)(2,1)}, u32[]{:S(2)}, u32[]{:S(2)}) collective-permute-start(bf16[128,1536]{1,0:T(8,128)(2,1)S(1)} %broadcast_select_fusion), channel_id=1, source_target_pairs={{0,9},{1,10},{2,11},{3,12},{4,13},{5,14},{6,15},{7,8},{8,33},{9,34... | collective-permute-start | bytes 1179656 | tf_op jit(solution)/shard_map/ppermute | solution.py:338
  65.2 1.0 copy-done.13
  66.2 2.2 %collective-permute-start.14 = (bf16[64,1536]{1,0:T(8,128)(2,1)S(1)}, bf16[64,1536]{1,0:T(8,128)(2,1)S(1)}, u32[]{:S(2)}, u32[]{:S(2)}) collective-permute-start(bf16[64,1536]{1,0:T(8,128)(2,1)S(1)} %slice.7), channel_id=1, source_target_pairs={{0,7},{1,0},{2,1},{3,2},{4,3},{5,4},{6,5},{7,6},{8,15},{9,8},{10,9... | collective-permute-start | bytes 589832 | tf_op jit(solution)/shard_map/ppermute | solution.py:281
  68.4 1.2 copy.16.refs_20_
  69.6 1.3 collective-permute-done.13.refs_15_
  70.8 9.3 %collective-permute-done.14.refs_16_ = bf16[64,1536]{1,0:T(8,128)(2,1)S(1)} collective-permute-done((bf16[64,1536]{1,0:T(8,128)(2,1)S(1)}, bf16[64,1536]{1,0:T(8,128)(2,1)S(1)}, u32[]{:S(2)}, u32[]{:S(2)}) %collective-permute-start.14) | collective-permute-done | bytes 196640 | tf_op jit(solution)/shard_map/ppermute | solution.py:281
  80.1 7.4 %collective-permute-done.11.refs_13_ = bf16[256,1536]{1,0:T(8,128)(2,1)} collective-permute-done((bf16[256,1536]{1,0:T(8,128)(2,1)S(1)}, bf16[256,1536]{1,0:T(8,128)(2,1)}, u32[]{:S(2)}, u32[]{:S(2)}) %collective-permute-start.11) | collective-permute-done | bytes 786464 | tf_op jit(solution)/shard_map/ppermute | solution.py:282
  87.5 30.8 %front.1 = (bf16[768,1536]{1,0:T(8,128)(2,1)}, bf16[768,768]{1,0:T(8,128)(2,1)}, bf16[768,768]{1,0:T(8,128)(2,1)}) custom-call(s32[3]{0:T(128)} %pad_add_fusion.meta, s32[1568]{0:T(1024)} %copy-done.6, s32[65]{0:T(128)} %add_subtract_fusion.starts, bf16[768,512]{1,0:T(8,128)(2,1)} %bitcast.10, bf16[16,512]{1,0:T(8,128)(2,1)} %copy-done.8, ...), custom_call_target="tpu_custom_call" | custom-call | flops 10000000000 | bytes 12582912 | tf_op jit(solution)/shard_map/front/pallas_call | solution.py:349
  118.4 3.0 %collective-permute-done.15.theirs = bf16[768,768]{1,0:T(8,128)(2,1)S(1)} collective-permute-done((bf16[768,768]{1,0:T(8,128)(2,1)}, bf16[768,768]{1,0:T(8,128)(2,1)S(1)}, u32[]{:S(2)}, u32[]{:S(2)}) %collective-permute-start.15) | collective-permute-done | bytes 1179680 | tf_op jit(solution)/shard_map/ppermute | solution.py:283
  121.5 1.1 copy-done.12
  122.6 9.3 %back.1 = bf16[768,1536]{1,0:T(8,128)(2,1)} custom-call(s32[3]{0:T(128)} %pad_add_fusion.meta, bf16[768,1536]{1,0:T(8,128)(2,1)} %get-tuple-element.40.sub, bf16[768,768]{1,0:T(8,128)(2,1)} %get-tuple-element.41.mine, bf16[768,768]{1,0:T(8,128)(2,1)} %copy-done.12, bf16[16,2,96,768]{3,2,1,0:T(8,128)(2,1)} %bitcast.14), custom_call_target="tpu_custom_call" | custom-call | flops 3600000000 | bytes 12582912 | tf_op jit(solution)/shard_map/back/pallas_call | solution.py:378
  (65 shorter events, 3.1 us)
Async XLA Ops:
  6.5 12.4 %copy-start.7 = (bf16[32,1536]{1,0:T(8,128)(2,1)S(1)}, bf16[32,1536]{1,0:T(8,128)(2,1)}, u32[]{:S(2)}) copy-start(bf16[32,1536]{1,0:T(8,128)(2,1)} %param.13) | copy-start | bytes 294916
  6.5 12.5 %copy-start.10 = (f32[1536]{0:T(1024)S(1)}, f32[1536]{0:T(1024)}, u32[]{:S(2)}) copy-start(f32[1536]{0:T(1024)} %param.14) | copy-start | bytes 18436
  6.5 13.2 %copy-start.11 = (s32[1,64]{1,0:T(1,128)S(1)}, s32[1,64]{1,0:T(1,128)}, u32[]{:S(2)}) copy-start(s32[1,64]{1,0:T(1,128)} %param.9) | copy-start | bytes 772
  6.5 13.7 %copy-start.9 = (f32[1536]{0:T(1024)S(1)}, f32[1536]{0:T(1024)}, u32[]{:S(2)}) copy-start(f32[1536]{0:T(1024)} %param.11) | copy-start | bytes 18436
  6.5 111.8 %all-gather.2.cloned.1.call-start = ((), (), s32[]{:S(2)}) async-start(), calls=%async_computation | async-start | bytes 4866048 | tf_op jit(solution)/shard_map/all_gather | solution.py:343
  10.1 15.5 %collective-permute-start = (bf16[128,1536]{1,0:T(8,128)(2,1)}, bf16[128,1536]{1,0:T(8,128)(2,1)S(1)}, u32[]{:S(2)}, u32[]{:S(2)}) collective-permute-start(bf16[128,1536]{1,0:T(8,128)(2,1)} %front_pack.1.refs_9_), channel_id=1, source_target_pairs={{0,1},{1,2},{2,3},{3,4},{4,5},{5,6},{6,7},{7,0},{8,9},{9,10},{10,1... | collective-permute-start | bytes 1179656 | tf_op jit(solution)/shard_map/ppermute | solution.py:281
  12.6 13.0 %collective-permute-start.1 = (bf16[128,1536]{1,0:T(8,128)(2,1)}, bf16[128,1536]{1,0:T(8,128)(2,1)S(1)}, u32[]{:S(2)}, u32[]{:S(2)}) collective-permute-start(bf16[128,1536]{1,0:T(8,128)(2,1)} %front_pack.1.refs_9_), channel_id=1, source_target_pairs={{0,7},{1,0},{2,1},{3,2},{4,3},{5,4},{6,5},{7,6},{8,15},{9,8},{10,9... | collective-permute-start | bytes 1179656 | tf_op jit(solution)/shard_map/ppermute | solution.py:281
  16.5 20.4 %collective-permute-start.6 = (bf16[128,1536]{1,0:T(8,128)(2,1)}, bf16[128,1536]{1,0:T(8,128)(2,1)S(1)}, u32[]{:S(2)}, u32[]{:S(2)}) collective-permute-start(bf16[128,1536]{1,0:T(8,128)(2,1)} %front_pack.1.refs_9_), channel_id=1, source_target_pairs={{0,8},{8,32},{16,56},{24,16},{32,40},{40,0},{48,24},{56,48},{1,9},... | collective-permute-start | bytes 1179656 | tf_op jit(solution)/shard_map/ppermute | solution.py:282
  19.0 12.8 %copy-start.3 = (bf16[1,768,512]{2,1,0:T(8,128)(2,1)S(1)}, bf16[1,768,512]{2,1,0:T(8,128)(2,1)}, u32[]{:S(2)}) copy-start(bf16[1,768,512]{2,1,0:T(8,128)(2,1)} %param.8) | copy-start | bytes 2359300
  20.2 30.9 %copy-start.6 = (s32[1568]{0:T(1024)}, s32[1568]{0:T(1024)S(1)}, u32[]{:S(2)}) copy-start(s32[1568]{0:T(1024)S(1)} %convert_reduce_fusion.ids_s) | copy-start | bytes 18820
  25.6 25.5 %copy-start.4 = (bf16[128,1536]{1,0:T(8,128)(2,1)}, bf16[128,1536]{1,0:T(8,128)(2,1)S(1)}, u32[]{:S(2)}) copy-start(bf16[128,1536]{1,0:T(8,128)(2,1)S(1)} %collective-permute-done.refs_3_) | copy-start | bytes 1179652
  25.6 25.5 %copy-start.5 = (bf16[128,1536]{1,0:T(8,128)(2,1)}, bf16[128,1536]{1,0:T(8,128)(2,1)S(1)}, u32[]{:S(2)}) copy-start(bf16[128,1536]{1,0:T(8,128)(2,1)S(1)} %collective-permute-done.1.refs_4_) | copy-start | bytes 1179652
  26.6 12.2 %collective-permute-start.4 = (bf16[128,1536]{1,0:T(8,128)(2,1)S(1)}, bf16[128,1536]{1,0:T(8,128)(2,1)}, u32[]{:S(2)}, u32[]{:S(2)}) collective-permute-start(bf16[128,1536]{1,0:T(8,128)(2,1)S(1)} %collective-permute-done.refs_3_), channel_id=1, source_target_pairs={{0,1},{1,2},{2,3},{3,4},{4,5},{5,6},{6,7},{7,0},{8,9},{9,10},{10,1... | collective-permute-start | bytes 1179656 | tf_op jit(solution)/shard_map/ppermute | solution.py:281
  26.6 15.2 %collective-permute-start.5 = (bf16[128,1536]{1,0:T(8,128)(2,1)S(1)}, bf16[128,1536]{1,0:T(8,128)(2,1)}, u32[]{:S(2)}, u32[]{:S(2)}) collective-permute-start(bf16[128,1536]{1,0:T(8,128)(2,1)S(1)} %collective-permute-done.1.refs_4_), channel_id=1, source_target_pairs={{0,7},{1,0},{2,1},{3,2},{4,3},{5,4},{6,5},{7,6},{8,15},{9,8},{10,9... | collective-permute-start | bytes 1179656 | tf_op jit(solution)/shard_map/ppermute | solution.py:281
  29.3 23.2 %collective-permute-start.9 = (bf16[256,1536]{1,0:T(8,128)(2,1)S(1)}, bf16[256,1536]{1,0:T(8,128)(2,1)}, u32[]{:S(2)}, u32[]{:S(2)}) collective-permute-start(bf16[256,1536]{1,0:T(8,128)(2,1)S(1)} %pad_maximum_fusion.1), channel_id=1, source_target_pairs={{0,8},{8,32},{16,56},{24,16},{32,40},{40,0},{48,24},{56,48},{1,9},... | collective-permute-start | bytes 2359304 | tf_op jit(solution)/shard_map/ppermute | solution.py:282
  31.9 19.1 %collective-permute-start.2 = (bf16[16,512]{1,0:T(8,128)(2,1)S(1)}, bf16[16,512]{1,0:T(8,128)(2,1)S(1)}, u32[]{:S(2)}, u32[]{:S(2)}) collective-permute-start(bf16[16,512]{1,0:T(8,128)(2,1)S(1)} %dynamic-slice_bitcast_fusion), channel_id=1, source_target_pairs={{16,32},{48,64},{80,96},{112,128},{144,160},{176,192},{208,224},{3... | collective-permute-start | bytes 49160 | tf_op jit(solution)/shard_map/ppermute | solution.py:312
  36.9 1.9 %copy-start.14 = (bf16[128,1536]{1,0:T(8,128)(2,1)}, bf16[128,1536]{1,0:T(8,128)(2,1)S(1)}, u32[]{:S(2)}) copy-start(bf16[128,1536]{1,0:T(8,128)(2,1)S(1)} %collective-permute-done.6.refs_10_) | copy-start | bytes 1179652
  41.8 16.4 %collective-permute-start.7 = (bf16[128,1536]{1,0:T(8,128)(2,1)}, bf16[128,1536]{1,0:T(8,128)(2,1)S(1)}, u32[]{:S(2)}, u32[]{:S(2)}) collective-permute-start(bf16[128,1536]{1,0:T(8,128)(2,1)} %collective-permute-done.4.refs_5_), channel_id=1, source_target_pairs={{0,1},{1,2},{2,3},{3,4},{4,5},{5,6},{6,7},{7,0},{8,9},{9,10},{10,1... | collective-permute-start | bytes 1179656 | tf_op jit(solution)/shard_map/ppermute | solution.py:281
  44.4 15.9 %collective-permute-start.8 = (bf16[128,1536]{1,0:T(8,128)(2,1)}, bf16[128,1536]{1,0:T(8,128)(2,1)S(1)}, u32[]{:S(2)}, u32[]{:S(2)}) collective-permute-start(bf16[128,1536]{1,0:T(8,128)(2,1)} %collective-permute-done.5.refs_6_), channel_id=1, source_target_pairs={{0,7},{1,0},{2,1},{3,2},{4,3},{5,4},{6,5},{7,6},{8,15},{9,8},{10,9... | collective-permute-start | bytes 1179656 | tf_op jit(solution)/shard_map/ppermute | solution.py:281
  51.0 1.4 copy-start.8
  51.1 14.1 %collective-permute-start.3 = (bf16[784,512]{1,0:T(8,128)(2,1)S(1)}, bf16[784,512]{1,0:T(8,128)(2,1)S(1)}, u32[]{:S(2)}, u32[]{:S(2)}) collective-permute-start(bf16[784,512]{1,0:T(8,128)(2,1)S(1)} %pad_maximum_fusion), channel_id=1, source_target_pairs={{0,16},{16,0},{1,17},{17,1},{2,18},{18,2},{3,19},{19,3},{4,20},{20... | collective-permute-start | bytes 2408456 | tf_op jit(solution)/shard_map/ppermute | solution.py:283
  52.4 27.8 %collective-permute-start.10 = (bf16[256,1536]{1,0:T(8,128)(2,1)S(1)}, bf16[256,1536]{1,0:T(8,128)(2,1)}, u32[]{:S(2)}, u32[]{:S(2)}) collective-permute-start(bf16[256,1536]{1,0:T(8,128)(2,1)S(1)} %pad_maximum_fusion.2), channel_id=1, source_target_pairs={{0,8},{8,32},{16,56},{24,16},{32,40},{40,0},{48,24},{56,48},{1,9},... | collective-permute-start | bytes 2359304 | tf_op jit(solution)/shard_map/ppermute | solution.py:282
  58.2 6.4 %copy-start.1 = (bf16[128,1536]{1,0:T(8,128)(2,1)}, bf16[128,1536]{1,0:T(8,128)(2,1)S(1)}, u32[]{:S(2)}) copy-start(bf16[128,1536]{1,0:T(8,128)(2,1)S(1)} %collective-permute-done.7.refs_7_) | copy-start | bytes 1179652
  60.3 4.3 %copy-start.2 = (bf16[128,1536]{1,0:T(8,128)(2,1)}, bf16[128,1536]{1,0:T(8,128)(2,1)S(1)}, u32[]{:S(2)}) copy-start(bf16[128,1536]{1,0:T(8,128)(2,1)S(1)} %collective-permute-done.8.refs_8_) | copy-start | bytes 1179652
  60.4 27.1 %collective-permute-start.11 = (bf16[256,1536]{1,0:T(8,128)(2,1)S(1)}, bf16[256,1536]{1,0:T(8,128)(2,1)}, u32[]{:S(2)}, u32[]{:S(2)}) collective-permute-start(bf16[256,1536]{1,0:T(8,128)(2,1)S(1)} %pad_maximum_fusion.3), channel_id=1, source_target_pairs={{0,8},{8,32},{16,56},{24,16},{32,40},{40,0},{48,24},{56,48},{1,9},... | collective-permute-start | bytes 2359304 | tf_op jit(solution)/shard_map/ppermute | solution.py:282
  63.0 17.2 %collective-permute-start.12 = (bf16[128,1536]{1,0:T(8,128)(2,1)S(1)}, bf16[128,1536]{1,0:T(8,128)(2,1)}, u32[]{:S(2)}, u32[]{:S(2)}) collective-permute-start(bf16[128,1536]{1,0:T(8,128)(2,1)S(1)} %broadcast_select_fusion), channel_id=1, source_target_pairs={{0,9},{1,10},{2,11},{3,12},{4,13},{5,14},{6,15},{7,8},{8,33},{9,34... | collective-permute-start | bytes 1179656 | tf_op jit(solution)/shard_map/ppermute | solution.py:338
  64.6 6.2 %collective-permute-start.13 = (bf16[64,1536]{1,0:T(8,128)(2,1)S(1)}, bf16[64,1536]{1,0:T(8,128)(2,1)S(1)}, u32[]{:S(2)}, u32[]{:S(2)}) collective-permute-start(bf16[64,1536]{1,0:T(8,128)(2,1)S(1)} %slice.6), channel_id=1, source_target_pairs={{0,1},{1,2},{2,3},{3,4},{4,5},{5,6},{6,7},{7,0},{8,9},{9,10},{10,1... | collective-permute-start | bytes 589832 | tf_op jit(solution)/shard_map/ppermute | solution.py:281
  66.2 13.9 %collective-permute-start.14 = (bf16[64,1536]{1,0:T(8,128)(2,1)S(1)}, bf16[64,1536]{1,0:T(8,128)(2,1)S(1)}, u32[]{:S(2)}, u32[]{:S(2)}) collective-permute-start(bf16[64,1536]{1,0:T(8,128)(2,1)S(1)} %slice.7), channel_id=1, source_target_pairs={{0,7},{1,0},{2,1},{3,2},{4,3},{5,4},{6,5},{7,6},{8,15},{9,8},{10,9... | collective-permute-start | bytes 589832 | tf_op jit(solution)/shard_map/ppermute | solution.py:281
  70.8 16.6 %copy-start.15 = (bf16[64,1536]{1,0:T(8,128)(2,1)}, bf16[64,1536]{1,0:T(8,128)(2,1)S(1)}, u32[]{:S(2)}) copy-start(bf16[64,1536]{1,0:T(8,128)(2,1)S(1)} %collective-permute-done.13.refs_15_) | copy-start | bytes 589828
  80.1 7.4 %copy-start.16 = (bf16[64,1536]{1,0:T(8,128)(2,1)}, bf16[64,1536]{1,0:T(8,128)(2,1)S(1)}, u32[]{:S(2)}) copy-start(bf16[64,1536]{1,0:T(8,128)(2,1)S(1)} %collective-permute-done.14.refs_16_) | copy-start | bytes 589828
  118.3 3.1 %collective-permute-start.15 = (bf16[768,768]{1,0:T(8,128)(2,1)}, bf16[768,768]{1,0:T(8,128)(2,1)S(1)}, u32[]{:S(2)}, u32[]{:S(2)}) collective-permute-start(bf16[768,768]{1,0:T(8,128)(2,1)} %get-tuple-element.43), channel_id=1, source_target_pairs={{0,16},{16,0},{1,17},{17,1},{2,18},{18,2},{3,19},{19,3},{4,20},{20... | collective-permute-start | bytes 3538952 | tf_op jit(solution)/shard_map/ppermute | solution.py:283
  121.5 1.1 copy-start.12
  (2 other events, 1.9 us)
Sparse Core Ops, SparseCore 0:
  9.2 78.9 all-gather.1

commit v6 on v5

--- a/solution.py
+++ b/solution.py
@@ -18,6 +18,12 @@
     for c in range(2)
     for xl in range(2)
     for x2 in [(xh * 2 + xl + (1 if c == 0 else 3)) % 4]
+]
+LAST = [
+    ((c * 2 + xl) * 8 + z, (c * 2 + xl) * 8 + (z + (1 if c == 0 else -1)) % 8)
+    for c in range(2)
+    for xl in range(2)
+    for z in range(8)
 ]
 DIAG = [
     (((xh * 2 + c) * 2 + xl) * 8 + z, (((x2 // 2) * 2 + c) * 2 + x2 % 2) * 8 + (z + d) % 8)
@@ -335,9 +341,9 @@
     landed(block, [(False, 0, 0, hi)])
     for s, array in enumerate(crossed):
         landed(array, [(True, -s, 0, hi), (True, s, 0, hi)] if s else [(True, 0, 0, hi)])
-    landed(lax.ppermute(jnp.where(c == 0, p, m), ("xh", "c", "xl", "z"), DIAG), [(True, 4, 0, hi)])
-    landed(zshift(p[: hi // 2], 1), [(False, 4, 0, hi // 2)])
-    landed(zshift(m[hi // 2 :], -1), [(False, 4, hi // 2, hi)])
+    opposite = jnp.where(c == 0, p, m)
+    landed(lax.ppermute(opposite, ("c", "xl", "z"), LAST), [(False, 4, 0, hi)])
+    landed(lax.ppermute(opposite, ("xh", "c", "xl", "z"), DIAG), [(True, 4, 0, hi)])
 
     recv = swap(jnp.concatenate([own, halo]))
     w_back = lax.all_gather(w_half, FS + ("c",), axis=0, tiled=True)

time: 141 us -> 140 us (level); the launches traced: 139 us -> 140 us
  waiting for transfers between devices: 43.7 us -> 46.5 us
  starting transfers between devices: 29 us -> 26.6 us
    ppermute x1 -> x2, waiting for transfers between devices: 0.01 us -> 13.4 us  [the longest x1 7.79 us: on_device(): landed(lax.ppermute(opposite, ('c', 'xl', 'z'), LAST), [(False, 4, 0, hi)])]
    ppermute x8 -> x6, waiting for transfers between devices: 26.8 us -> 16.2 us  [on_device(): zshift = lambda a, s: lax.ppermute(a, 'z', cyc(8, s))]
    ppermute x8 -> x6, starting transfers between devices: 14.5 us -> 11.8 us  [on_device(): zshift = lambda a, s: lax.ppermute(a, 'z', cyc(8, s))]
    unnamed x34 -> x28, local copies, waits for them, and re-layouts: 3.03 us -> 2.04 us
  transfers between devices with their start and end apart: 17 -> 16, of which waited for: 10 -> 10; matrix products, arithmetic and copies ran while one was open for 5% -> 5% of each run, Pallas kernels for 24% -> 24%
where the time goes in v6:
time: 140 us
  waiting for transfers between devices  46.5 us (33%)
  Pallas kernels  42.8 us (31%)
  starting transfers between devices  26.6 us (19%)
  between operations  13.6 us (10%)
  local copies, waits for them, and re-layouts  6.31 us (5%)
  other arithmetic  3.69 us (3%)
    pallas_call x1, Pallas kernels, on_device(): pl.pallas_call(functools.partial(front_kernel, places), out_shape=[jax.Sh...  31.6 us
    ppermute x6, waiting for transfers between devices, on_device(): zshift = lambda a, s: lax.ppermute(a, 'z', cyc(8, s))  16.2 us
    ppermute x6, starting transfers between devices, on_device(): zshift = lambda a, s: lax.ppermute(a, 'z', cyc(8, s))  11.8 us
    pallas_call x1, Pallas kernels, on_device(): pl.pallas_call(back_kernel, out_shape=jax.ShapeDtypeStruct((span, width),...  9.27 us
    ppermute x4, starting transfers between devices, on_device(): cross = lambda a: lax.ppermute(a, ('xh', 'c', 'xl'), CROSS)  7.94 us
    ppermute x1, waiting for transfers between devices, on_device(): landed(lax.ppermute(opposite, ('c', 'xl', 'z'), LAST), [(False, 4, 0, hi)])  7.79 us
    ppermute x4, waiting for transfers between devices, on_device(): cross = lambda a: lax.ppermute(a, ('xh', 'c', 'xl'), CROSS)  7.38 us
    ppermute x1, waiting for transfers between devices, on_device(): halo = lax.ppermute(edge, TM, out_pairs + [(b, a) for a, b in out_pairs])  6.47 us
  transfers between devices with their start and end apart: 16, of which 10 were waited for; matrix products, arithmetic and copies ran while one was open for 5% of the time, Pallas kernels for 24%

profile of v6, /device:TPU:1, one launch (start us, length us, event | category | flops | bytes accessed | tf_op | source)
XLA Modules:
  0.0 139.5 jit_solution(8149643553337561197)
XLA Ops:
  6.6 0.9 copy-done
  7.5 0.7 constant_dynamic-slice_fusion
  8.2 1.9 %front_pack.1.refs_9_ = bf16[128,1536]{1,0:T(8,128)(2,1)} custom-call(bf16[32,1536]{1,0:T(8,128)(2,1)} %sub.15, bf16[96,3072]{1,0:T(8,128)(2,1)} %first.1), custom_call_target="tpu_custom_call" | custom-call | tf_op jit(solution)/shard_map/front_pack/pallas_call | solution.py:293
  10.1 2.5 %collective-permute-start = (bf16[128,1536]{1,0:T(8,128)(2,1)}, bf16[128,1536]{1,0:T(8,128)(2,1)S(1)}, u32[]{:S(2)}, u32[]{:S(2)}) collective-permute-start(bf16[128,1536]{1,0:T(8,128)(2,1)} %front_pack.1.refs_9_), channel_id=1, source_target_pairs={{0,1},{1,2},{2,3},{3,4},{4,5},{5,6},{6,7},{7,0},{8,9},{9,10},{10,1... | collective-permute-start | bytes 1179656 | tf_op jit(solution)/shard_map/ppermute | solution.py:287
  12.6 3.9 %collective-permute-start.1 = (bf16[128,1536]{1,0:T(8,128)(2,1)}, bf16[128,1536]{1,0:T(8,128)(2,1)S(1)}, u32[]{:S(2)}, u32[]{:S(2)}) collective-permute-start(bf16[128,1536]{1,0:T(8,128)(2,1)} %front_pack.1.refs_9_), channel_id=1, source_target_pairs={{0,7},{1,0},{2,1},{3,2},{4,3},{5,4},{6,5},{7,6},{8,15},{9,8},{10,9... | collective-permute-start | bytes 1179656 | tf_op jit(solution)/shard_map/ppermute | solution.py:287
  16.5 2.5 %collective-permute-start.6 = (bf16[128,1536]{1,0:T(8,128)(2,1)}, bf16[128,1536]{1,0:T(8,128)(2,1)S(1)}, u32[]{:S(2)}, u32[]{:S(2)}) collective-permute-start(bf16[128,1536]{1,0:T(8,128)(2,1)} %front_pack.1.refs_9_), channel_id=1, source_target_pairs={{0,8},{8,32},{16,56},{24,16},{32,40},{40,0},{48,24},{56,48},{1,9},... | collective-permute-start | bytes 1179656 | tf_op jit(solution)/shard_map/ppermute | solution.py:288
  19.2 0.6 dynamic_slice.15.refs_18_
  20.2 0.6 reshape.56.refs_16_
  20.8 0.7 add_subtract_fusion.starts
  22.0 3.5 %collective-permute-done.refs_3_ = bf16[128,1536]{1,0:T(8,128)(2,1)S(1)} collective-permute-done((bf16[128,1536]{1,0:T(8,128)(2,1)}, bf16[128,1536]{1,0:T(8,128)(2,1)S(1)}, u32[]{:S(2)}, u32[]{:S(2)}) %collective-permute-start) | collective-permute-done | bytes 393248 | tf_op jit(solution)/shard_map/ppermute | solution.py:287
  25.6 1.0 broadcast_in_dim.2.refs_17_
  26.6 2.7 %collective-permute-start.5 = (bf16[128,1536]{1,0:T(8,128)(2,1)S(1)}, bf16[128,1536]{1,0:T(8,128)(2,1)}, u32[]{:S(2)}, u32[]{:S(2)}) collective-permute-start(bf16[128,1536]{1,0:T(8,128)(2,1)S(1)} %collective-permute-done.1.refs_4_), channel_id=1, source_target_pairs={{0,7},{1,0},{2,1},{3,2},{4,3},{5,4},{6,5},{7,6},{8,15},{9,8},{10,9... | collective-permute-start | bytes 1179656 | tf_op jit(solution)/shard_map/ppermute | solution.py:287
  29.3 2.6 %collective-permute-start.9 = (bf16[256,1536]{1,0:T(8,128)(2,1)S(1)}, bf16[256,1536]{1,0:T(8,128)(2,1)}, u32[]{:S(2)}, u32[]{:S(2)}) collective-permute-start(bf16[256,1536]{1,0:T(8,128)(2,1)S(1)} %pad_maximum_fusion.1), channel_id=1, source_target_pairs={{0,8},{8,32},{16,56},{24,16},{32,40},{40,0},{48,24},{56,48},{1,9},... | collective-permute-start | bytes 2359304 | tf_op jit(solution)/shard_map/ppermute | solution.py:288
  31.9 5.0 %collective-permute-start.2 = (bf16[16,512]{1,0:T(8,128)(2,1)S(1)}, bf16[16,512]{1,0:T(8,128)(2,1)S(1)}, u32[]{:S(2)}, u32[]{:S(2)}) collective-permute-start(bf16[16,512]{1,0:T(8,128)(2,1)S(1)} %dynamic-slice_bitcast_fusion), channel_id=1, source_target_pairs={{16,32},{48,64},{80,96},{112,128},{144,160},{176,192},{208,224},{3... | collective-permute-start | bytes 49160 | tf_op jit(solution)/shard_map/ppermute | solution.py:318
  36.9 1.9 %collective-permute-done.4.refs_5_ = bf16[128,1536]{1,0:T(8,128)(2,1)} collective-permute-done((bf16[128,1536]{1,0:T(8,128)(2,1)S(1)}, bf16[128,1536]{1,0:T(8,128)(2,1)}, u32[]{:S(2)}, u32[]{:S(2)}) %collective-permute-start.4) | collective-permute-done | bytes 393248 | tf_op jit(solution)/shard_map/ppermute | solution.py:287
  38.9 3.0 %collective-permute-done.5.refs_6_ = bf16[128,1536]{1,0:T(8,128)(2,1)} collective-permute-done((bf16[128,1536]{1,0:T(8,128)(2,1)S(1)}, bf16[128,1536]{1,0:T(8,128)(2,1)}, u32[]{:S(2)}, u32[]{:S(2)}) %collective-permute-start.5) | collective-permute-done | bytes 393248 | tf_op jit(solution)/shard_map/ppermute | solution.py:287
  41.9 2.6 %collective-permute-start.7 = (bf16[128,1536]{1,0:T(8,128)(2,1)}, bf16[128,1536]{1,0:T(8,128)(2,1)S(1)}, u32[]{:S(2)}, u32[]{:S(2)}) collective-permute-start(bf16[128,1536]{1,0:T(8,128)(2,1)} %collective-permute-done.4.refs_5_), channel_id=1, source_target_pairs={{0,1},{1,2},{2,3},{3,4},{4,5},{5,6},{6,7},{7,0},{8,9},{9,10},{10,1... | collective-permute-start | bytes 1179656 | tf_op jit(solution)/shard_map/ppermute | solution.py:287
  44.5 6.5 %collective-permute-done.2.refs_1_ = bf16[16,512]{1,0:T(8,128)(2,1)S(1)} collective-permute-done((bf16[16,512]{1,0:T(8,128)(2,1)S(1)}, bf16[16,512]{1,0:T(8,128)(2,1)S(1)}, u32[]{:S(2)}, u32[]{:S(2)}) %collective-permute-start.2) | collective-permute-done | bytes 16416 | tf_op jit(solution)/shard_map/ppermute | solution.py:318
  51.2 1.2 pad_maximum_fusion.2
  52.5 5.4 %collective-permute-done.7.refs_7_ = bf16[128,1536]{1,0:T(8,128)(2,1)S(1)} collective-permute-done((bf16[128,1536]{1,0:T(8,128)(2,1)}, bf16[128,1536]{1,0:T(8,128)(2,1)S(1)}, u32[]{:S(2)}, u32[]{:S(2)}) %collective-permute-start.7) | collective-permute-done | bytes 393248 | tf_op jit(solution)/shard_map/ppermute | solution.py:287
  57.8 2.4 %collective-permute-done.8.refs_8_ = bf16[128,1536]{1,0:T(8,128)(2,1)S(1)} collective-permute-done((bf16[128,1536]{1,0:T(8,128)(2,1)}, bf16[128,1536]{1,0:T(8,128)(2,1)S(1)}, u32[]{:S(2)}, u32[]{:S(2)}) %collective-permute-start.8) | collective-permute-done | bytes 393248 | tf_op jit(solution)/shard_map/ppermute | solution.py:287
  60.3 2.8 %collective-permute-start.11 = (bf16[256,1536]{1,0:T(8,128)(2,1)S(1)}, bf16[256,1536]{1,0:T(8,128)(2,1)}, u32[]{:S(2)}, u32[]{:S(2)}) collective-permute-start(bf16[256,1536]{1,0:T(8,128)(2,1)S(1)} %pad_maximum_fusion.3), channel_id=1, source_target_pairs={{0,8},{8,32},{16,56},{24,16},{32,40},{40,0},{48,24},{56,48},{1,9},... | collective-permute-start | bytes 2359304 | tf_op jit(solution)/shard_map/ppermute | solution.py:288
  63.1 0.8 broadcast_select_fusion
  63.9 1.6 %collective-permute-start.12 = (bf16[128,1536]{1,0:T(8,128)(2,1)}, bf16[128,1536]{1,0:T(8,128)(2,1)}, u32[]{:S(2)}, u32[]{:S(2)}) collective-permute-start(bf16[128,1536]{1,0:T(8,128)(2,1)} %broadcast_select_fusion), channel_id=1, source_target_pairs={{0,1},{1,2},{2,3},{3,4},{4,5},{5,6},{6,7},{7,0},{8,9},{9,10},{10,1... | collective-permute-start | bytes 1179656 | tf_op jit(solution)/shard_map/ppermute | solution.py:345
  65.5 1.2 copy.16.refs_19_
  66.7 7.8 %collective-permute-done.12.refs_14_ = bf16[128,1536]{1,0:T(8,128)(2,1)} collective-permute-done((bf16[128,1536]{1,0:T(8,128)(2,1)}, bf16[128,1536]{1,0:T(8,128)(2,1)}, u32[]{:S(2)}, u32[]{:S(2)}) %collective-permute-start.12) | collective-permute-done | bytes 393248 | tf_op jit(solution)/shard_map/ppermute | solution.py:345
  74.5 5.6 %collective-permute-done.13.refs_15_ = bf16[128,1536]{1,0:T(8,128)(2,1)} collective-permute-done((bf16[128,1536]{1,0:T(8,128)(2,1)}, bf16[128,1536]{1,0:T(8,128)(2,1)}, u32[]{:S(2)}, u32[]{:S(2)}) %collective-permute-start.13) | collective-permute-done | bytes 393248 | tf_op jit(solution)/shard_map/ppermute | solution.py:346
  80.1 7.4 %collective-permute-done.11.refs_13_ = bf16[256,1536]{1,0:T(8,128)(2,1)} collective-permute-done((bf16[256,1536]{1,0:T(8,128)(2,1)S(1)}, bf16[256,1536]{1,0:T(8,128)(2,1)}, u32[]{:S(2)}, u32[]{:S(2)}) %collective-permute-start.11) | collective-permute-done | bytes 786464 | tf_op jit(solution)/shard_map/ppermute | solution.py:288
  87.5 31.6 %front.1 = (bf16[768,1536]{1,0:T(8,128)(2,1)}, bf16[768,768]{1,0:T(8,128)(2,1)}, bf16[768,768]{1,0:T(8,128)(2,1)}) custom-call(s32[3]{0:T(128)} %pad_add_fusion.meta, s32[1568]{0:T(1024)} %copy-done.6, s32[65]{0:T(128)} %add_subtract_fusion.starts, bf16[768,512]{1,0:T(8,128)(2,1)} %bitcast.10, bf16[16,512]{1,0:T(8,128)(2,1)} %copy-done.8, ...), custom_call_target="tpu_custom_call" | custom-call | flops 10000000000 | bytes 12582912 | tf_op jit(solution)/shard_map/front/pallas_call | solution.py:355
  119.2 3.0 %collective-permute-done.14.theirs = bf16[768,768]{1,0:T(8,128)(2,1)S(1)} collective-permute-done((bf16[768,768]{1,0:T(8,128)(2,1)}, bf16[768,768]{1,0:T(8,128)(2,1)S(1)}, u32[]{:S(2)}, u32[]{:S(2)}) %collective-permute-start.14) | collective-permute-done | bytes 1179680 | tf_op jit(solution)/shard_map/ppermute | solution.py:289
  122.3 1.1 copy-done.12
  123.4 9.3 %back.1 = bf16[768,1536]{1,0:T(8,128)(2,1)} custom-call(s32[3]{0:T(128)} %pad_add_fusion.meta, bf16[768,1536]{1,0:T(8,128)(2,1)} %get-tuple-element.40.sub, bf16[768,768]{1,0:T(8,128)(2,1)} %get-tuple-element.41.mine, bf16[768,768]{1,0:T(8,128)(2,1)} %copy-done.12, bf16[16,2,96,768]{3,2,1,0:T(8,128)(2,1)} %bitcast.14), custom_call_target="tpu_custom_call" | custom-call | flops 3600000000 | bytes 12582912 | tf_op jit(solution)/shard_map/back/pallas_call | solution.py:384
  (55 shorter events, 1.8 us)
Async XLA Ops:
  6.5 1.0 copy-start
  6.5 12.5 %copy-start.7 = (bf16[32,1536]{1,0:T(8,128)(2,1)S(1)}, bf16[32,1536]{1,0:T(8,128)(2,1)}, u32[]{:S(2)}) copy-start(bf16[32,1536]{1,0:T(8,128)(2,1)} %param.13) | copy-start | bytes 294916
  6.5 12.5 %copy-start.10 = (f32[1536]{0:T(1024)S(1)}, f32[1536]{0:T(1024)}, u32[]{:S(2)}) copy-start(f32[1536]{0:T(1024)} %param.14) | copy-start | bytes 18436
  6.5 13.2 %copy-start.11 = (s32[1,64]{1,0:T(1,128)S(1)}, s32[1,64]{1,0:T(1,128)}, u32[]{:S(2)}) copy-start(s32[1,64]{1,0:T(1,128)} %param.9) | copy-start | bytes 772
  6.5 13.7 %copy-start.9 = (f32[1536]{0:T(1024)S(1)}, f32[1536]{0:T(1024)}, u32[]{:S(2)}) copy-start(f32[1536]{0:T(1024)} %param.11) | copy-start | bytes 18436
  6.5 112.6 %all-gather.2.cloned.1.call-start = ((), (), s32[]{:S(2)}) async-start(), calls=%async_computation | async-start | bytes 4866048 | tf_op jit(solution)/shard_map/all_gather | solution.py:349
  10.1 15.5 %collective-permute-start = (bf16[128,1536]{1,0:T(8,128)(2,1)}, bf16[128,1536]{1,0:T(8,128)(2,1)S(1)}, u32[]{:S(2)}, u32[]{:S(2)}) collective-permute-start(bf16[128,1536]{1,0:T(8,128)(2,1)} %front_pack.1.refs_9_), channel_id=1, source_target_pairs={{0,1},{1,2},{2,3},{3,4},{4,5},{5,6},{6,7},{7,0},{8,9},{9,10},{10,1... | collective-permute-start | bytes 1179656 | tf_op jit(solution)/shard_map/ppermute | solution.py:287
  12.6 13.0 %collective-permute-start.1 = (bf16[128,1536]{1,0:T(8,128)(2,1)}, bf16[128,1536]{1,0:T(8,128)(2,1)S(1)}, u32[]{:S(2)}, u32[]{:S(2)}) collective-permute-start(bf16[128,1536]{1,0:T(8,128)(2,1)} %front_pack.1.refs_9_), channel_id=1, source_target_pairs={{0,7},{1,0},{2,1},{3,2},{4,3},{5,4},{6,5},{7,6},{8,15},{9,8},{10,9... | collective-permute-start | bytes 1179656 | tf_op jit(solution)/shard_map/ppermute | solution.py:287
  16.5 20.4 %collective-permute-start.6 = (bf16[128,1536]{1,0:T(8,128)(2,1)}, bf16[128,1536]{1,0:T(8,128)(2,1)S(1)}, u32[]{:S(2)}, u32[]{:S(2)}) collective-permute-start(bf16[128,1536]{1,0:T(8,128)(2,1)} %front_pack.1.refs_9_), channel_id=1, source_target_pairs={{0,8},{8,32},{16,56},{24,16},{32,40},{40,0},{48,24},{56,48},{1,9},... | collective-permute-start | bytes 1179656 | tf_op jit(solution)/shard_map/ppermute | solution.py:288
  19.0 12.9 %copy-start.3 = (bf16[1,768,512]{2,1,0:T(8,128)(2,1)S(1)}, bf16[1,768,512]{2,1,0:T(8,128)(2,1)}, u32[]{:S(2)}) copy-start(bf16[1,768,512]{2,1,0:T(8,128)(2,1)} %param.8) | copy-start | bytes 2359300
  20.2 30.9 %copy-start.6 = (s32[1568]{0:T(1024)}, s32[1568]{0:T(1024)S(1)}, u32[]{:S(2)}) copy-start(s32[1568]{0:T(1024)S(1)} %convert_reduce_fusion.ids_s) | copy-start | bytes 18820
  25.6 13.3 %copy-start.4 = (bf16[128,1536]{1,0:T(8,128)(2,1)}, bf16[128,1536]{1,0:T(8,128)(2,1)S(1)}, u32[]{:S(2)}) copy-start(bf16[128,1536]{1,0:T(8,128)(2,1)S(1)} %collective-permute-done.refs_3_) | copy-start | bytes 1179652
  25.6 16.3 %copy-start.5 = (bf16[128,1536]{1,0:T(8,128)(2,1)}, bf16[128,1536]{1,0:T(8,128)(2,1)S(1)}, u32[]{:S(2)}) copy-start(bf16[128,1536]{1,0:T(8,128)(2,1)S(1)} %collective-permute-done.1.refs_4_) | copy-start | bytes 1179652
  26.6 12.3 %collective-permute-start.4 = (bf16[128,1536]{1,0:T(8,128)(2,1)S(1)}, bf16[128,1536]{1,0:T(8,128)(2,1)}, u32[]{:S(2)}, u32[]{:S(2)}) collective-permute-start(bf16[128,1536]{1,0:T(8,128)(2,1)S(1)} %collective-permute-done.refs_3_), channel_id=1, source_target_pairs={{0,1},{1,2},{2,3},{3,4},{4,5},{5,6},{6,7},{7,0},{8,9},{9,10},{10,1... | collective-permute-start | bytes 1179656 | tf_op jit(solution)/shard_map/ppermute | solution.py:287
  26.6 15.3 %collective-permute-start.5 = (bf16[128,1536]{1,0:T(8,128)(2,1)S(1)}, bf16[128,1536]{1,0:T(8,128)(2,1)}, u32[]{:S(2)}, u32[]{:S(2)}) collective-permute-start(bf16[128,1536]{1,0:T(8,128)(2,1)S(1)} %collective-permute-done.1.refs_4_), channel_id=1, source_target_pairs={{0,7},{1,0},{2,1},{3,2},{4,3},{5,4},{6,5},{7,6},{8,15},{9,8},{10,9... | collective-permute-start | bytes 1179656 | tf_op jit(solution)/shard_map/ppermute | solution.py:287
  29.3 23.2 %collective-permute-start.9 = (bf16[256,1536]{1,0:T(8,128)(2,1)S(1)}, bf16[256,1536]{1,0:T(8,128)(2,1)}, u32[]{:S(2)}, u32[]{:S(2)}) collective-permute-start(bf16[256,1536]{1,0:T(8,128)(2,1)S(1)} %pad_maximum_fusion.1), channel_id=1, source_target_pairs={{0,8},{8,32},{16,56},{24,16},{32,40},{40,0},{48,24},{56,48},{1,9},... | collective-permute-start | bytes 2359304 | tf_op jit(solution)/shard_map/ppermute | solution.py:288
  31.9 19.1 %collective-permute-start.2 = (bf16[16,512]{1,0:T(8,128)(2,1)S(1)}, bf16[16,512]{1,0:T(8,128)(2,1)S(1)}, u32[]{:S(2)}, u32[]{:S(2)}) collective-permute-start(bf16[16,512]{1,0:T(8,128)(2,1)S(1)} %dynamic-slice_bitcast_fusion), channel_id=1, source_target_pairs={{16,32},{48,64},{80,96},{112,128},{144,160},{176,192},{208,224},{3... | collective-permute-start | bytes 49160 | tf_op jit(solution)/shard_map/ppermute | solution.py:318
  36.9 14.1 %copy-start.13 = (bf16[128,1536]{1,0:T(8,128)(2,1)}, bf16[128,1536]{1,0:T(8,128)(2,1)S(1)}, u32[]{:S(2)}) copy-start(bf16[128,1536]{1,0:T(8,128)(2,1)S(1)} %collective-permute-done.6.refs_10_) | copy-start | bytes 1179652
  41.9 16.0 %collective-permute-start.7 = (bf16[128,1536]{1,0:T(8,128)(2,1)}, bf16[128,1536]{1,0:T(8,128)(2,1)S(1)}, u32[]{:S(2)}, u32[]{:S(2)}) collective-permute-start(bf16[128,1536]{1,0:T(8,128)(2,1)} %collective-permute-done.4.refs_5_), channel_id=1, source_target_pairs={{0,1},{1,2},{2,3},{3,4},{4,5},{5,6},{6,7},{7,0},{8,9},{9,10},{10,1... | collective-permute-start | bytes 1179656 | tf_op jit(solution)/shard_map/ppermute | solution.py:287
  44.4 15.8 %collective-permute-start.8 = (bf16[128,1536]{1,0:T(8,128)(2,1)}, bf16[128,1536]{1,0:T(8,128)(2,1)S(1)}, u32[]{:S(2)}, u32[]{:S(2)}) collective-permute-start(bf16[128,1536]{1,0:T(8,128)(2,1)} %collective-permute-done.5.refs_6_), channel_id=1, source_target_pairs={{0,7},{1,0},{2,1},{3,2},{4,3},{5,4},{6,5},{7,6},{8,15},{9,8},{10,9... | collective-permute-start | bytes 1179656 | tf_op jit(solution)/shard_map/ppermute | solution.py:287
  51.0 1.4 copy-start.8
  51.1 15.6 %collective-permute-start.3 = (bf16[784,512]{1,0:T(8,128)(2,1)S(1)}, bf16[784,512]{1,0:T(8,128)(2,1)}, u32[]{:S(2)}, u32[]{:S(2)}) collective-permute-start(bf16[784,512]{1,0:T(8,128)(2,1)S(1)} %pad_maximum_fusion), channel_id=1, source_target_pairs={{0,16},{16,0},{1,17},{17,1},{2,18},{18,2},{3,19},{19,3},{4,20},{20... | collective-permute-start | bytes 2408456 | tf_op jit(solution)/shard_map/ppermute | solution.py:289
  52.4 27.7 %collective-permute-start.10 = (bf16[256,1536]{1,0:T(8,128)(2,1)S(1)}, bf16[256,1536]{1,0:T(8,128)(2,1)}, u32[]{:S(2)}, u32[]{:S(2)}) collective-permute-start(bf16[256,1536]{1,0:T(8,128)(2,1)S(1)} %pad_maximum_fusion.2), channel_id=1, source_target_pairs={{0,8},{8,32},{16,56},{24,16},{32,40},{40,0},{48,24},{56,48},{1,9},... | collective-permute-start | bytes 2359304 | tf_op jit(solution)/shard_map/ppermute | solution.py:288
  57.8 8.9 %copy-start.1 = (bf16[128,1536]{1,0:T(8,128)(2,1)}, bf16[128,1536]{1,0:T(8,128)(2,1)S(1)}, u32[]{:S(2)}) copy-start(bf16[128,1536]{1,0:T(8,128)(2,1)S(1)} %collective-permute-done.7.refs_7_) | copy-start | bytes 1179652
  60.2 6.5 %copy-start.2 = (bf16[128,1536]{1,0:T(8,128)(2,1)}, bf16[128,1536]{1,0:T(8,128)(2,1)S(1)}, u32[]{:S(2)}) copy-start(bf16[128,1536]{1,0:T(8,128)(2,1)S(1)} %collective-permute-done.8.refs_8_) | copy-start | bytes 1179652
  60.3 27.2 %collective-permute-start.11 = (bf16[256,1536]{1,0:T(8,128)(2,1)S(1)}, bf16[256,1536]{1,0:T(8,128)(2,1)}, u32[]{:S(2)}, u32[]{:S(2)}) collective-permute-start(bf16[256,1536]{1,0:T(8,128)(2,1)S(1)} %pad_maximum_fusion.3), channel_id=1, source_target_pairs={{0,8},{8,32},{16,56},{24,16},{32,40},{40,0},{48,24},{56,48},{1,9},... | collective-permute-start | bytes 2359304 | tf_op jit(solution)/shard_map/ppermute | solution.py:288
  63.9 10.6 %collective-permute-start.12 = (bf16[128,1536]{1,0:T(8,128)(2,1)}, bf16[128,1536]{1,0:T(8,128)(2,1)}, u32[]{:S(2)}, u32[]{:S(2)}) collective-permute-start(bf16[128,1536]{1,0:T(8,128)(2,1)} %broadcast_select_fusion), channel_id=1, source_target_pairs={{0,1},{1,2},{2,3},{3,4},{4,5},{5,6},{6,7},{7,0},{8,9},{9,10},{10,1... | collective-permute-start | bytes 1179656 | tf_op jit(solution)/shard_map/ppermute | solution.py:345
  65.5 14.6 %collective-permute-start.13 = (bf16[128,1536]{1,0:T(8,128)(2,1)}, bf16[128,1536]{1,0:T(8,128)(2,1)}, u32[]{:S(2)}, u32[]{:S(2)}) collective-permute-start(bf16[128,1536]{1,0:T(8,128)(2,1)} %broadcast_select_fusion), channel_id=1, source_target_pairs={{0,9},{1,10},{2,11},{3,12},{4,13},{5,14},{6,15},{7,8},{8,33},{9,34... | collective-permute-start | bytes 1179656 | tf_op jit(solution)/shard_map/ppermute | solution.py:346
  119.1 3.1 %collective-permute-start.14 = (bf16[768,768]{1,0:T(8,128)(2,1)}, bf16[768,768]{1,0:T(8,128)(2,1)S(1)}, u32[]{:S(2)}, u32[]{:S(2)}) collective-permute-start(bf16[768,768]{1,0:T(8,128)(2,1)} %get-tuple-element.43), channel_id=1, source_target_pairs={{0,16},{16,0},{1,17},{17,1},{2,18},{18,2},{3,19},{19,3},{4,20},{20... | collective-permute-start | bytes 3538952 | tf_op jit(solution)/shard_map/ppermute | solution.py:289
  122.3 1.1 copy-start.12
Sparse Core Ops, SparseCore 0:
  9.2 77.4 all-gather.1
